TPU v7x, 32 devices: a whole 2x2x4 slice. The times are simulated.
32 devices in a mesh: dp: 16 (over z, x, core), tensor: 2 (over y).
Axes of the slice: x: 2, y: 2, z: 4, core: 2. Of those that a mesh axis runs over, the one named last changes fastest.
Arguments:
- tokens: bfloat16 [16, 512, 1152], P('dp', 'tensor'), may hold values from -6 to 6
- text: bfloat16 [16, 120, 1152], P('dp', None, 'tensor'), may hold values from -6 to 6
- lengths: int32 [16], P('dp'), may hold values from 1 to 120, as said below
- modulation: float32 [16, 2, 6, 1152], P('dp'), may hold values from -1.5 to 1.5
- self_qkv: bfloat16 [2, 1152, 3, 1152], P(None, 'dp', None, 'tensor'), may hold values from -0.1875 to 0.1875
- self_out: bfloat16 [2, 1152, 1152], P(None, 'tensor', 'dp'), may hold values from -0.375 to 0.375
- cross_query: bfloat16 [2, 1152, 1152], P(None, 'dp', 'tensor'), may hold values from -0.1875 to 0.1875
- cross_keyvalue: bfloat16 [2, 1152, 2, 1152], P(None, 'dp', None, 'tensor'), may hold values from -0.1875 to 0.1875
- cross_out: bfloat16 [2, 1152, 1152], P(None, 'tensor', 'dp'), may hold values from -0.375 to 0.375
- mlp_in: bfloat16 [2, 1152, 4608], P(None, 'dp', 'tensor'), may hold values from -0.1875 to 0.1875
- mlp_out: bfloat16 [2, 4608, 1152], P(None, 'tensor', 'dp'), may hold values from -0.09375 to 0.09375
- cotangent: bfloat16 [16, 512, 1152], P('dp', 'tensor'), may hold values from -6 to 6
Outputs:
- output: bfloat16 [16, 512, 1152], P('dp', 'tensor')
- tokens_grad: float32 [16, 512, 1152], P('dp', 'tensor')
- text_grad: float32 [16, 120, 1152], P('dp', None, 'tensor')
- modulation_grad: float32 [16, 2, 6, 1152], P('dp')
- self_qkv_grad: float32 [2, 1152, 3, 1152], P(None, 'dp', None, 'tensor')
- self_out_grad: float32 [2, 1152, 1152], P(None, 'tensor', 'dp')
- cross_query_grad: float32 [2, 1152, 1152], P(None, 'dp', 'tensor')
- cross_keyvalue_grad: float32 [2, 1152, 2, 1152], P(None, 'dp', None, 'tensor')
- cross_out_grad: float32 [2, 1152, 1152], P(None, 'tensor', 'dp')
- mlp_in_grad: float32 [2, 1152, 4608], P(None, 'dp', 'tensor')
- mlp_out_grad: float32 [2, 4608, 1152], P(None, 'tensor', 'dp')
Inputs may be any that keep to these rules, and one draw needn't show every extreme that they name: `lengths`: some clip has all 120 text tokens valid.
All inputs are finite; a program needn't handle non-finite values.
Results may differ from a plain program's by a relative error of at most 0.028.
Values may be sent and summed in bfloat16 or wider, within the bound.
No kernel may reach another device: no remote copies, remote signals or barrier semaphores. Data moves between devices by JAX's collectives and lax.ppermute only.
A program may use at most 256 MiB of HBM per device.

v0:
```python
import jax
import jax.numpy as jnp
from jax import lax
from jax.sharding import PartitionSpec as P

HEADS = 16
HEAD_DIM = 72
TEXT = 120
PATCH = 256
LAYERS = 2


EPSILON = 1e-06
NEG_FILL = -1e30


def normalize(stream):
    center = stream - jnp.mean(stream, axis=-1, keepdims=True)
    root = lax.rsqrt(jnp.mean(center * center, axis=-1, keepdims=True) + EPSILON)
    return (center * root, root)


def norm_back(grad, unit, root):
    return root * (
        grad
        - jnp.mean(grad, axis=-1, keepdims=True)
        - unit * jnp.mean(grad * unit, axis=-1, keepdims=True)
    )


def gelu_tanh(field):
    return jax.nn.gelu(field, approximate=True)


def attend_forward(queries, key_rows, values, visible, scaling):
    scores = (
        jnp.einsum("glhe,gmhe->ghlm", queries, key_rows, preferred_element_type=jnp.float32)
        * scaling
    )
    if visible is not None:
        scores = jnp.where(visible, scores, NEG_FILL)
    log_total = jax.nn.logsumexp(scores, axis=-1)
    weights = jnp.exp(scores - log_total[..., None]).astype(jnp.bfloat16)
    result = jnp.einsum("ghlm,gmhe->glhe", weights, values, preferred_element_type=jnp.float32)
    return (result.astype(jnp.bfloat16), log_total)


def attend_back(queries, key_rows, values, visible, scaling, log_total, grad_out):
    scores = (
        jnp.einsum("glhe,gmhe->ghlm", queries, key_rows, preferred_element_type=jnp.float32)
        * scaling
    )
    if visible is not None:
        scores = jnp.where(visible, scores, NEG_FILL)
    probs = jnp.exp(scores - log_total[..., None])
    grad_probs = jnp.einsum("glhe,gmhe->ghlm", grad_out, values, preferred_element_type=jnp.float32)
    grad_values = jnp.einsum(
        "ghlm,glhe->gmhe", probs.astype(jnp.bfloat16), grad_out, preferred_element_type=jnp.float32
    )
    grad_scores = probs * (grad_probs - jnp.sum(probs * grad_probs, axis=-1, keepdims=True))
    grad_scores = grad_scores.astype(jnp.bfloat16)
    grad_queries = (
        jnp.einsum("ghlm,gmhe->glhe", grad_scores, key_rows, preferred_element_type=jnp.float32)
        * scaling
    )
    grad_keys = (
        jnp.einsum("ghlm,glhe->gmhe", grad_scores, queries, preferred_element_type=jnp.float32)
        * scaling
    )
    return (
        grad_queries.astype(jnp.bfloat16),
        grad_keys.astype(jnp.bfloat16),
        grad_values.astype(jnp.bfloat16),
    )


def per_device(
    tokens,
    text,
    lengths,
    modulation,
    self_qkv,
    self_out,
    cross_query,
    cross_keyvalue,
    cross_out,
    mlp_in,
    mlp_out,
    cotangent,
):
    tensor_size = lax.axis_size("tensor")
    rows_here = tokens.shape[1]
    total_rows = rows_here * tensor_size
    frames_all = total_rows // PATCH
    heads_here = HEADS // tensor_size
    columns = heads_here * HEAD_DIM
    scaling = HEAD_DIM ** (-0.5)
    text_full = lax.all_gather(text[0], "tensor", axis=1, tiled=True)
    visible = jnp.arange(TEXT) < lengths[0]

    def spread(field):
        return lax.all_gather(field, "tensor", axis=0, tiled=True)

    def collect(field, project):
        return lax.psum_scatter(project(field), "tensor", scatter_dimension=0, tiled=True)

    def fetch(layer):
        return (
            lax.all_gather(self_qkv[layer], "dp", axis=0, tiled=True),
            lax.all_gather(self_out[layer], "dp", axis=1, tiled=True),
            lax.all_gather(cross_query[layer], "dp", axis=0, tiled=True),
            lax.all_gather(cross_keyvalue[layer], "dp", axis=0, tiled=True),
            lax.all_gather(cross_out[layer], "dp", axis=1, tiled=True),
            lax.all_gather(mlp_in[layer], "dp", axis=0, tiled=True),
            lax.all_gather(mlp_out[layer], "dp", axis=1, tiled=True),
        )

    def to_groups(field, layer):
        grouped = field.reshape(frames_all, PATCH, heads_here, HEAD_DIM)
        if layer % 2 == 1:
            grouped = grouped.transpose(1, 0, 2, 3)
        return grouped

    def from_groups(field, layer):
        if layer % 2 == 1:
            field = field.transpose(1, 0, 2, 3)
        return field.reshape(total_rows, columns)

    stream = tokens[0].astype(jnp.float32)
    memory = []
    for layer in range(LAYERS):
        adaln = modulation[0, layer]
        weights = fetch(layer)
        weight_qkv, weight_proj, weight_query, weight_keyval, weight_cout, weight_in, weight_out = (
            weights
        )
        first_in = stream
        unit_one, root_one = normalize(first_in)
        normed_loc = (unit_one * (1.0 + adaln[1]) + adaln[0]).astype(jnp.bfloat16)
        normed_all = spread(normed_loc)
        qkv_rows = jnp.einsum(
            "sd,dtc->stc", normed_all, weight_qkv, preferred_element_type=jnp.float32
        ).astype(jnp.bfloat16)
        queries = to_groups(qkv_rows[:, 0], layer)
        key_rows = to_groups(qkv_rows[:, 1], layer)
        values = to_groups(qkv_rows[:, 2], layer)
        attended, log_self = attend_forward(queries, key_rows, values, None, scaling)
        attended = from_groups(attended, layer)

        def proj_self(piece):
            return jnp.dot(piece, weight_proj, preferred_element_type=jnp.float32)

        branch = collect(attended, proj_self)
        second_in = first_in + adaln[2] * branch
        cross_loc = second_in.astype(jnp.bfloat16)
        cross_all = spread(cross_loc)
        cross_q = jnp.dot(cross_all, weight_query, preferred_element_type=jnp.float32).astype(
            jnp.bfloat16
        )
        cross_q = cross_q.reshape(1, total_rows, heads_here, HEAD_DIM)
        text_kv = jnp.einsum(
            "nd,dtc->ntc", text_full, weight_keyval, preferred_element_type=jnp.float32
        ).astype(jnp.bfloat16)
        text_keys = text_kv[:, 0].reshape(1, TEXT, heads_here, HEAD_DIM)
        text_values = text_kv[:, 1].reshape(1, TEXT, heads_here, HEAD_DIM)
        cross_att, log_cross = attend_forward(cross_q, text_keys, text_values, visible, scaling)
        cross_att = cross_att.reshape(total_rows, columns)

        def proj_cross(piece):
            return jnp.dot(piece, weight_cout, preferred_element_type=jnp.float32)

        crossed = collect(cross_att, proj_cross)
        third_in = second_in + crossed
        unit_two, root_two = normalize(third_in)
        inner_loc = (unit_two * (1.0 + adaln[4]) + adaln[3]).astype(jnp.bfloat16)
        inner_all = spread(inner_loc)
        hidden = gelu_tanh(
            jnp.dot(inner_all, weight_in, preferred_element_type=jnp.float32)
        ).astype(jnp.bfloat16)

        def proj_mlp(piece):
            return jnp.dot(piece, weight_out, preferred_element_type=jnp.float32)

        mlp_branch = collect(hidden, proj_mlp)
        stream = third_in + adaln[5] * mlp_branch
        memory.append(
            (
                weights,
                adaln,
                unit_one,
                root_one,
                normed_loc,
                normed_all,
                queries,
                key_rows,
                values,
                attended,
                log_self,
                branch,
                cross_loc,
                cross_all,
                cross_q,
                text_keys,
                text_values,
                cross_att,
                log_cross,
                unit_two,
                root_two,
                inner_loc,
                inner_all,
                mlp_branch,
            )
        )
    output = stream.astype(jnp.bfloat16)
    grad_stream = cotangent[0].astype(jnp.float32)
    grad_text = jnp.zeros((TEXT, text_full.shape[1]), jnp.float32)
    layer_grads = [None] * LAYERS
    table_rows = [None] * LAYERS
    for layer in reversed(range(LAYERS)):
        (
            kept_weights,
            adaln,
            unit_one,
            root_one,
            normed_loc,
            normed_kept,
            queries,
            key_rows,
            values,
            attended,
            log_self,
            branch,
            cross_loc,
            cross_kept,
            cross_q,
            text_keys,
            text_values,
            cross_att,
            log_cross,
            unit_two,
            root_two,
            inner_loc,
            inner_kept,
            mlp_branch,
        ) = memory[layer]
        weights = fetch(layer)
        weight_qkv, weight_proj, weight_query, weight_keyval, weight_cout, weight_in, weight_out = (
            weights
        )
        normed_all = spread(normed_loc)
        cross_all = spread(cross_loc)
        grad_gate_two = jnp.sum(grad_stream * mlp_branch, axis=0)
        inner_all = spread(inner_loc)
        grad_mlp = spread((adaln[5] * grad_stream).astype(jnp.bfloat16))
        pre_mlp = jnp.dot(inner_all, weight_in, preferred_element_type=jnp.float32)
        hidden_f, gelu_backward = jax.vjp(gelu_tanh, pre_mlp)
        hidden = hidden_f.astype(jnp.bfloat16)
        grad_weight_out = jnp.einsum(
            "sh,sd->hd", hidden, grad_mlp, preferred_element_type=jnp.float32
        )
        grad_hidden = jnp.einsum(
            "sd,hd->sh", grad_mlp, weight_out, preferred_element_type=jnp.float32
        )
        grad_pre = gelu_backward(grad_hidden)[0].astype(jnp.bfloat16)
        grad_weight_in = jnp.einsum(
            "sd,sh->dh", inner_all, grad_pre, preferred_element_type=jnp.float32
        )

        def back_mlp(piece):
            return jnp.einsum("sh,dh->sd", piece, weight_in, preferred_element_type=jnp.float32)

        grad_inner = collect(grad_pre, back_mlp)
        grad_shift_two = jnp.sum(grad_inner, axis=0)
        grad_scale_two = jnp.sum(grad_inner * unit_two, axis=0)
        grad_stream = grad_stream + norm_back(grad_inner * (1.0 + adaln[4]), unit_two, root_two)
        grad_crossed = spread(grad_stream.astype(jnp.bfloat16))
        grad_weight_cout = jnp.einsum(
            "sc,sd->cd", cross_att, grad_crossed, preferred_element_type=jnp.float32
        )
        grad_catt = jnp.einsum(
            "sd,cd->sc", grad_crossed, weight_cout, preferred_element_type=jnp.float32
        ).astype(jnp.bfloat16)
        grad_cq, grad_tkeys, grad_tvalues = attend_back(
            cross_q,
            text_keys,
            text_values,
            visible,
            scaling,
            log_cross,
            grad_catt.reshape(1, total_rows, heads_here, HEAD_DIM),
        )
        grad_cq = grad_cq.reshape(total_rows, columns)
        grad_textkv = jnp.stack(
            [grad_tkeys.reshape(TEXT, columns), grad_tvalues.reshape(TEXT, columns)], axis=1
        )
        grad_weight_query = jnp.einsum(
            "sd,sc->dc", cross_all, grad_cq, preferred_element_type=jnp.float32
        )
        grad_weight_keyval = jnp.einsum(
            "nd,ntc->dtc", text_full, grad_textkv, preferred_element_type=jnp.float32
        )
        grad_text = grad_text + jnp.einsum(
            "ntc,dtc->nd", grad_textkv, weight_keyval, preferred_element_type=jnp.float32
        )

        def back_cross(piece):
            return jnp.einsum("sc,dc->sd", piece, weight_query, preferred_element_type=jnp.float32)

        grad_stream = grad_stream + collect(grad_cq, back_cross)
        grad_gate_one = jnp.sum(grad_stream * branch, axis=0)
        grad_branch = spread((adaln[2] * grad_stream).astype(jnp.bfloat16))
        grad_weight_proj = jnp.einsum(
            "sc,sd->cd", attended, grad_branch, preferred_element_type=jnp.float32
        )
        grad_att = jnp.einsum(
            "sd,cd->sc", grad_branch, weight_proj, preferred_element_type=jnp.float32
        ).astype(jnp.bfloat16)
        grad_att = to_groups(grad_att, layer)
        grad_q, grad_k, grad_v = attend_back(
            queries, key_rows, values, None, scaling, log_self, grad_att
        )
        grad_qkv = jnp.stack(
            [from_groups(grad_q, layer), from_groups(grad_k, layer), from_groups(grad_v, layer)],
            axis=1,
        )
        grad_weight_qkv = jnp.einsum(
            "sd,stc->dtc", normed_all, grad_qkv, preferred_element_type=jnp.float32
        )

        def back_self(piece):
            return jnp.einsum("stc,dtc->sd", piece, weight_qkv, preferred_element_type=jnp.float32)

        grad_normed = collect(grad_qkv, back_self)
        grad_shift_one = jnp.sum(grad_normed, axis=0)
        grad_scale_one = jnp.sum(grad_normed * unit_one, axis=0)
        grad_stream = grad_stream + norm_back(grad_normed * (1.0 + adaln[1]), unit_one, root_one)
        table_rows[layer] = jnp.stack(
            [
                grad_shift_one,
                grad_scale_one,
                grad_gate_one,
                grad_shift_two,
                grad_scale_two,
                grad_gate_two,
            ]
        )
        layer_grads[layer] = (
            lax.psum_scatter(grad_weight_qkv, "dp", scatter_dimension=0, tiled=True),
            lax.psum_scatter(grad_weight_proj, "dp", scatter_dimension=1, tiled=True),
            lax.psum_scatter(grad_weight_query, "dp", scatter_dimension=0, tiled=True),
            lax.psum_scatter(grad_weight_keyval, "dp", scatter_dimension=0, tiled=True),
            lax.psum_scatter(grad_weight_cout, "dp", scatter_dimension=1, tiled=True),
            lax.psum_scatter(grad_weight_in, "dp", scatter_dimension=0, tiled=True),
            lax.psum_scatter(grad_weight_out, "dp", scatter_dimension=1, tiled=True),
        )
    text_grad = lax.psum_scatter(grad_text, "tensor", scatter_dimension=1, tiled=True)
    table_grad = lax.psum(jnp.stack(table_rows), "tensor")
    stacked = [
        jnp.stack([layer_grads[layer][member] for layer in range(LAYERS)]) for member in range(7)
    ]
    return (
        output[None],
        grad_stream[None],
        text_grad[None],
        table_grad[None],
        stacked[0],
        stacked[1],
        stacked[2],
        stacked[3],
        stacked[4],
        stacked[5],
        stacked[6],
    )


def solution(mesh):
    return jax.shard_map(
        per_device,
        mesh=mesh,
        in_specs=(
            P("dp", "tensor", None),
            P("dp", None, "tensor"),
            P("dp"),
            P("dp", None, None, None),
            P(None, "dp", None, "tensor"),
            P(None, "tensor", "dp"),
            P(None, "dp", "tensor"),
            P(None, "dp", None, "tensor"),
            P(None, "tensor", "dp"),
            P(None, "dp", "tensor"),
            P(None, "tensor", "dp"),
            P("dp", "tensor", None),
        ),
        out_specs=(
            P("dp", "tensor", None),
            P("dp", "tensor", None),
            P("dp", None, "tensor"),
            P("dp", None, None, None),
            P(None, "dp", None, "tensor"),
            P(None, "tensor", "dp"),
            P(None, "dp", "tensor"),
            P(None, "dp", None, "tensor"),
            P(None, "tensor", "dp"),
            P(None, "dp", "tensor"),
            P(None, "tensor", "dp"),
        ),
        check_vma=False,
    )
```

profile of v0, /device:TPU:0, one launch (start us, length us, event | category | flops | bytes accessed | tf_op | source)
XLA Modules:
  0.0 2962.9 jit_solution(3827579811484252102)
XLA Ops:
  38.8 54.5 %all-gather.66.cloned.1.call-done = bf16[1,1152,3,576]{3,1,2,0:T(8,128)(2,1)} async-done(((bf16[1,72,3,576]{3,1,2,0:T(8,128)(2,1)}), bf16[1,1152,3,576]{3,1,2,0:T(8,128)(2,1)}) %all-gather.66.cloned.1.call-update) | async-done | bytes 3981328 | tf_op jit(solution)/shard_map/all_gather | solution.py:109
  181.9 37.4 %all-gather.70.cloned.1.call-done = bf16[1,1152,2,576]{3,2,0,1:T(2,128)(2,1)} async-done(((bf16[1,72,2,576]{3,2,0,1:T(2,128)(2,1)}), bf16[1,1152,2,576]{3,2,0,1:T(2,128)(2,1)}) %all-gather.70.cloned.1.call-update) | async-done | bytes 2654224 | tf_op jit(solution)/shard_map/all_gather | solution.py:112
  288.1 37.9 %all-gather.74.cloned.1.call-done = bf16[1,576,1152]{1,2,0:T(8,128)(2,1)} async-done(((bf16[1,576,72]{1,2,0:T(8,128)(2,1)}), bf16[1,576,1152]{1,2,0:T(8,128)(2,1)}) %all-gather.74.cloned.1.call-update) | async-done | bytes 1327120 | tf_op jit(solution)/shard_map/all_gather | solution.py:113
  368.8 53.9 %all-gather.76.cloned.1.call-done = bf16[1,1152,2304]{2,1,0:T(8,128)(2,1)} async-done(((bf16[1,72,2304]{2,1,0:T(8,128)(2,1)}), bf16[1,1152,2304]{2,1,0:T(8,128)(2,1)}) %all-gather.76.cloned.1.call-update) | async-done | bytes 5308432 | tf_op jit(solution)/shard_map/all_gather | solution.py:114
  454.6 50.7 %all-gather.78.cloned.1.call-done = bf16[1,2304,1152]{1,2,0:T(8,128)(2,1)} async-done(((bf16[1,2304,72]{1,2,0:T(8,128)(2,1)}), bf16[1,2304,1152]{1,2,0:T(8,128)(2,1)}) %all-gather.78.cloned.1.call-update) | async-done | bytes 5308432 | tf_op jit(solution)/shard_map/all_gather | solution.py:115
  552.5 50.3 %all-gather.80.cloned.1.call-done = bf16[1,1152,3,576]{3,1,2,0:T(8,128)(2,1)} async-done(((bf16[1,72,3,576]{3,1,2,0:T(8,128)(2,1)}), bf16[1,1152,3,576]{3,1,2,0:T(8,128)(2,1)}) %all-gather.80.cloned.1.call-update) | async-done | bytes 3981328 | tf_op jit(solution)/shard_map/all_gather | solution.py:109
  717.7 43.9 %all-gather.84.cloned.1.call-done = bf16[1,1152,2,576]{3,2,0,1:T(2,128)(2,1)} async-done(((bf16[1,72,2,576]{3,2,0,1:T(2,128)(2,1)}), bf16[1,1152,2,576]{3,2,0,1:T(2,128)(2,1)}) %all-gather.84.cloned.1.call-update) | async-done | bytes 2654224 | tf_op jit(solution)/shard_map/all_gather | solution.py:112
  831.1 35.5 %all-gather.88.cloned.1.call-done = bf16[1,576,1152]{1,2,0:T(8,128)(2,1)} async-done(((bf16[1,576,72]{1,2,0:T(8,128)(2,1)}), bf16[1,576,1152]{1,2,0:T(8,128)(2,1)}) %all-gather.88.cloned.1.call-update) | async-done | bytes 1327120 | tf_op jit(solution)/shard_map/all_gather | solution.py:113
  911.4 52.5 %all-gather.90.cloned.1.call-done = bf16[1,1152,2304]{2,1,0:T(8,128)(2,1)} async-done(((bf16[1,72,2304]{2,1,0:T(8,128)(2,1)}), bf16[1,1152,2304]{2,1,0:T(8,128)(2,1)}) %all-gather.90.cloned.1.call-update) | async-done | bytes 5308432 | tf_op jit(solution)/shard_map/all_gather | solution.py:114
  1011.8 59.2 %all-gather.92.cloned.1.call-done = bf16[1,2304,1152]{1,2,0:T(8,128)(2,1)} async-done(((bf16[1,2304,72]{1,2,0:T(8,128)(2,1)}), bf16[1,2304,1152]{1,2,0:T(8,128)(2,1)}) %all-gather.92.cloned.1.call-update) | async-done | bytes 5308432 | tf_op jit(solution)/shard_map/all_gather | solution.py:115
  1196.6 34.8 %reduce-scatter.52.cloned.1.call-done = f32[256,1152]{1,0:T(8,128)} async-done(((f32[512,1152]{1,0:T(8,128)}), f32[256,1152]{1,0:T(8,128)}) %reduce-scatter.52.cloned.1.call-update) | async-done | bytes 1179664 | tf_op jit(solution)/shard_map/reduce_scatter | solution.py:105
  1330.0 34.8 %reduce-scatter.54.cloned.1.call-done = f32[256,1152]{1,0:T(8,128)} async-done(((f32[512,1152]{1,0:T(8,128)}), f32[256,1152]{1,0:T(8,128)}) %reduce-scatter.54.cloned.1.call-update) | async-done | bytes 1179664 | tf_op jit(solution)/shard_map/reduce_scatter | solution.py:105
  1481.5 34.8 %reduce-scatter.58.cloned.1.call-done = f32[256,1152]{1,0:T(8,128)} async-done(((f32[512,1152]{1,0:T(8,128)}), f32[256,1152]{1,0:T(8,128)}) %reduce-scatter.58.cloned.1.call-update) | async-done | bytes 1179664 | tf_op jit(solution)/shard_map/reduce_scatter | solution.py:105
  1683.1 67.0 %reduce-scatter.86.cloned.1.call-done = f32[576,72]{0,1:T(8,128)} async-done(((f32[576,1152]{0,1:T(8,128)}), f32[576,72]{0,1:T(8,128)}) %reduce-scatter.86.cloned.1.call-update) | async-done | bytes 165904
  1750.1 68.7 %reduce-scatter.84.cloned.1.call-done = f32[576,72]{0,1:T(8,128)} async-done(((f32[576,1152]{0,1:T(8,128)}), f32[576,72]{0,1:T(8,128)}) %reduce-scatter.84.cloned.1.call-update) | async-done | bytes 165904
  1820.6 222.6 %all-reduce.11.cloned.1.call-done = (f32[1152,2,576]{2,1,0:T(2,128)}, f32[1152,2,576]{2,1,0:T(2,128)}) async-done(((f32[1152,2,576]{2,1,0:T(2,128)}, f32[1152,2,576]{2,1,0:T(2,128)}), (f32[1152,2,576]{2,1,0:T(2,128)}, f32[1152,2,576]{2,1,0:T(2,128)})) %all-reduce.11.cloned.1.call-update) | async-done | bytes 10616848
  2046.5 66.3 %reduce-scatter.78.cloned.1.call-done = f32[576,72]{0,1:T(8,128)} async-done(((f32[576,1152]{0,1:T(8,128)}), f32[576,72]{0,1:T(8,128)}) %reduce-scatter.78.cloned.1.call-update) | async-done | bytes 165904
  2112.8 68.7 %reduce-scatter.76.cloned.1.call-done = f32[576,72]{0,1:T(8,128)} async-done(((f32[576,1152]{0,1:T(8,128)}), f32[576,72]{0,1:T(8,128)}) %reduce-scatter.76.cloned.1.call-update) | async-done | bytes 165904
  2183.3 122.0 %reduce-scatter.70.cloned.1.call-done = f32[72,2304]{1,0:T(8,128)} async-done(((f32[1152,2304]{1,0:T(8,128)}), f32[72,2304]{1,0:T(8,128)}) %reduce-scatter.70.cloned.1.call-update) | async-done | bytes 663568 | tf_op jit(solution)/shard_map/reduce_scatter | solution.py:353
  2305.3 124.4 %reduce-scatter.68.cloned.1.call-done = f32[72,2304]{1,0:T(8,128)} async-done(((f32[1152,2304]{1,0:T(8,128)}), f32[72,2304]{1,0:T(8,128)}) %reduce-scatter.68.cloned.1.call-update) | async-done | bytes 663568 | tf_op jit(solution)/shard_map/reduce_scatter | solution.py:353
  2432.2 122.0 %reduce-scatter.74.cloned.1.call-done = f32[2304,72]{0,1:T(8,128)} async-done(((f32[2304,1152]{0,1:T(8,128)}), f32[2304,72]{0,1:T(8,128)}) %reduce-scatter.74.cloned.1.call-update) | async-done | bytes 663568 | tf_op jit(solution)/shard_map/reduce_scatter | solution.py:354
  2554.2 124.4 %reduce-scatter.72.cloned.1.call-done = f32[2304,72]{0,1:T(8,128)} async-done(((f32[2304,1152]{0,1:T(8,128)}), f32[2304,72]{0,1:T(8,128)}) %reduce-scatter.72.cloned.1.call-update) | async-done | bytes 663568 | tf_op jit(solution)/shard_map/reduce_scatter | solution.py:354
  2727.1 99.4 %reduce-scatter.66.cloned.1.call-done = f32[72,3,576]{2,0,1:T(8,128)} async-done(((f32[1152,3,576]{2,0,1:T(8,128)}), f32[72,3,576]{2,0,1:T(8,128)}) %reduce-scatter.66.cloned.1.call-update) | async-done | bytes 497680 | tf_op jit(solution)/shard_map/reduce_scatter | solution.py:348
  2826.5 111.4 %reduce-scatter.64.cloned.1.call-done = f32[72,3,576]{2,0,1:T(8,128)} async-done(((f32[1152,3,576]{2,0,1:T(8,128)}), f32[72,3,576]{2,0,1:T(8,128)}) %reduce-scatter.64.cloned.1.call-update) | async-done | bytes 497680 | tf_op jit(solution)/shard_map/reduce_scatter | solution.py:348
  (557 shorter events, 1167.6 us)
Async XLA Ops:
  14.9 156.8 %reduce-scatter.38.cloned.1.call-start = ((), (), s32[]{:S(2)}) async-start(), calls=%async_computation.26 | async-start | bytes 3538944 | tf_op jit(solution)/shard_map/reduce_scatter | solution.py:105
  173.9 152.1 %all-gather.74.cloned.1.call-start = ((), (), s32[]{:S(2)}) async-start(), calls=%async_computation.60 | async-start | bytes 1566720 | tf_op jit(solution)/shard_map/all_gather | solution.py:113
  174.7 189.1 %reduce-scatter.40.cloned.1.call-start = ((), (), s32[]{:S(2)}) async-start(), calls=%async_computation.28 | async-start | bytes 3538944 | tf_op jit(solution)/shard_map/reduce_scatter | solution.py:105
  368.7 179.5 %reduce-scatter.42.cloned.1.call-start = ((), (), s32[]{:S(2)}) async-start(), calls=%async_computation.30 | async-start | bytes 3538944 | tf_op jit(solution)/shard_map/reduce_scatter | solution.py:105
  552.1 162.6 %reduce-scatter.44.cloned.1.call-start = ((), (), s32[]{:S(2)}) async-start(), calls=%async_computation.32 | async-start | bytes 3538944 | tf_op jit(solution)/shard_map/reduce_scatter | solution.py:105
  716.9 149.7 %all-gather.88.cloned.1.call-start = ((), (), s32[]{:S(2)}) async-start(), calls=%async_computation.67 | async-start | bytes 1566720 | tf_op jit(solution)/shard_map/all_gather | solution.py:113
  717.7 186.9 %reduce-scatter.46.cloned.1.call-start = ((), (), s32[]{:S(2)}) async-start(), calls=%async_computation.34 | async-start | bytes 3538944 | tf_op jit(solution)/shard_map/reduce_scatter | solution.py:105
  910.6 160.4 %all-gather.92.cloned.1.call-start = ((), (), s32[]{:S(2)}) async-start(), calls=%async_computation.69 | async-start | bytes 5640192 | tf_op jit(solution)/shard_map/all_gather | solution.py:115
  911.2 211.4 %reduce-scatter.50.cloned.1.call-start = ((), (), s32[]{:S(2)}) async-start(), calls=%async_computation.38 | async-start | bytes 3538944 | tf_op jit(solution)/shard_map/reduce_scatter | solution.py:105
  1520.1 160.0 %reduce-scatter.82.cloned.1.call-start = ((), (), s32[]{:S(2)}) async-start(), calls=%async_computation.73 | async-start | bytes 3133440
  1524.3 157.0 %reduce-scatter.80.cloned.1.call-start = ((), (), s32[]{:S(2)}) async-start(), calls=%async_computation.72 | async-start | bytes 3133440
  1529.4 220.6 %reduce-scatter.86.cloned.1.call-start = ((), (), s32[]{:S(2)}) async-start(), calls=%async_computation.75 | async-start | bytes 3133440
  1534.5 284.3 %reduce-scatter.84.cloned.1.call-start = ((), (), s32[]{:S(2)}) async-start(), calls=%async_computation.74 | async-start | bytes 3133440
  1539.7 503.5 %all-reduce.11.cloned.1.call-start = ((), (), s32[]{:S(2)}) async-start(), calls=%async_computation.76 | async-start | bytes 23592960
  1577.6 535.2 %reduce-scatter.78.cloned.1.call-start = ((), (), s32[]{:S(2)}) async-start(), calls=%async_computation.71 | async-start | bytes 3133440
  1581.9 599.7 %reduce-scatter.76.cloned.1.call-start = ((), (), s32[]{:S(2)}) async-start(), calls=%async_computation.70 | async-start | bytes 3133440
  1586.9 718.4 %reduce-scatter.70.cloned.1.call-start = ((), (), s32[]{:S(2)}) async-start(), calls=%async_computation.53 | async-start | bytes 11280384 | tf_op jit(solution)/shard_map/reduce_scatter | solution.py:353
  1596.9 832.8 %reduce-scatter.68.cloned.1.call-start = ((), (), s32[]{:S(2)}) async-start(), calls=%async_computation.52 | async-start | bytes 11280384 | tf_op jit(solution)/shard_map/reduce_scatter | solution.py:353
  1606.8 947.4 %reduce-scatter.74.cloned.1.call-start = ((), (), s32[]{:S(2)}) async-start(), calls=%async_computation.55 | async-start | bytes 11280384 | tf_op jit(solution)/shard_map/reduce_scatter | solution.py:354
  1617.5 1061.2 %reduce-scatter.72.cloned.1.call-start = ((), (), s32[]{:S(2)}) async-start(), calls=%async_computation.54 | async-start | bytes 11280384 | tf_op jit(solution)/shard_map/reduce_scatter | solution.py:354
  1628.2 1087.1 %reduce-scatter.60.cloned.1.call-start = ((), (), s32[]{:S(2)}) async-start(), calls=%async_computation.48 | async-start | bytes 3538944 | tf_op jit(solution)/shard_map/reduce_scatter | solution.py:105
  1655.7 1170.7 %reduce-scatter.66.cloned.1.call-start = ((), (), s32[]{:S(2)}) async-start(), calls=%async_computation.51 | async-start | bytes 9400320 | tf_op jit(solution)/shard_map/reduce_scatter | solution.py:348
  1663.3 1274.6 %reduce-scatter.64.cloned.1.call-start = ((), (), s32[]{:S(2)}) async-start(), calls=%async_computation.50 | async-start | bytes 9400320 | tf_op jit(solution)/shard_map/reduce_scatter | solution.py:348
  1671.3 1284.6 %reduce-scatter.62.cloned.1.call-start = ((), (), s32[]{:S(2)}) async-start(), calls=%async_computation.49 | async-start | bytes 884736 | tf_op jit(solution)/shard_map/reduce_scatter | solution.py:356
  (138 other events, 4586.3 us)
Sparse Core Ops, SparseCore 0:
  41.6 51.7 all-gather.65
  174.5 44.7 all-gather.69
  286.6 39.3 all-gather.73
  366.3 56.3 all-gather.75
  448.8 56.3 all-gather.77
  551.1 51.7 all-gather.79
  628.5 39.3 all-gather.81
  716.7 44.8 all-gather.83
  827.2 39.3 all-gather.87
  907.5 56.3 all-gather.89
  1014.6 56.3 all-gather.91
  1547.4 65.2 reduce-scatter.81
  1617.0 64.2 reduce-scatter.79
  1685.7 64.2 reduce-scatter.85
  1754.5 64.2 reduce-scatter.83
  1823.0 220.1 all-reduce.10
  2047.5 65.3 reduce-scatter.77
  2117.2 64.2 reduce-scatter.75
  2186.0 119.2 reduce-scatter.69
  2309.8 119.9 reduce-scatter.67
  2434.2 119.9 reduce-scatter.73
  2558.7 119.9 reduce-scatter.71
  2719.5 106.9 reduce-scatter.65
  2831.0 106.7 reduce-scatter.63
  (28 shorter events, 805.9 us)
where the time goes:
time: 2970 us; the launch traced here: 2960 us
  waiting for transfers between devices  2420 us (81%)
  matrix products  273 us (9%)
  local copies, waits for them, and re-layouts  160 us (5%)
  other arithmetic  72.9 us (2%)
    unnamed x59, waiting for transfers between devices  500 us
    reduce_scatter x12, waiting for transfers between devices, collect(): lax.psum_scatter(project(field), 'tensor', scatter_dimension=0, tiled=True)  392 us
    all_gather x12, waiting for transfers between devices, spread(): return lax.all_gather(field, 'tensor', axis=0, tiled=True)  249 us
    reduce_scatter x2, waiting for transfers between devices, per_device(): lax.psum_scatter(grad_weight_out, 'dp', scatter_dimension=1, tiled=True)  246 us
    reduce_scatter x2, waiting for transfers between devices, per_device(): lax.psum_scatter(grad_weight_in, 'dp', scatter_dimension=0, tiled=True)  246 us
    reduce_scatter x2, waiting for transfers between devices, per_device(): lax.psum_scatter(grad_weight_qkv, 'dp', scatter_dimension=0, tiled=True)  211 us
    all_gather x2, waiting for transfers between devices, fetch(): lax.all_gather(mlp_out[layer], 'dp', axis=1, tiled=True)  110 us
    all_gather x2, waiting for transfers between devices, fetch(): lax.all_gather(mlp_in[layer], 'dp', axis=0, tiled=True)  106 us
  transfers between devices with their start and end apart: 52, of which 49 were waited for; matrix products, arithmetic and copies ran while one was open for 10% of the time, Pallas kernels for 0%

commit v1 on v0

v1 whole, which is shorter than its diff:
```python
import jax
import jax.numpy as jnp
from jax import lax
from jax.sharding import PartitionSpec as P

HEADS = 16
HEAD_DIM = 72
TEXT = 120
PATCH = 256
LAYERS = 2
LANES = 128

EPSILON = 1e-06
NEG_FILL = -1e30
F32 = jnp.float32
BF16 = jnp.bfloat16


def normalize(stream):
    center = stream - jnp.mean(stream, axis=-1, keepdims=True)
    root = lax.rsqrt(jnp.mean(center * center, axis=-1, keepdims=True) + EPSILON)
    return (center * root, root)


def norm_back(grad, unit, root):
    return root * (
        grad
        - jnp.mean(grad, axis=-1, keepdims=True)
        - unit * jnp.mean(grad * unit, axis=-1, keepdims=True)
    )


def gelu_tanh(field):
    return jax.nn.gelu(field, approximate=True)


def dot(left, right, contract=((1,), (0,))):
    return lax.dot_general(left, right, (contract, ((), ())), preferred_element_type=F32)


def attend_forward(queries, key_rows, values, visible, scaling):
    scores = (
        jnp.einsum("glhe,gmhe->ghlm", queries, key_rows, preferred_element_type=F32) * scaling
    )
    if visible is not None:
        scores = jnp.where(visible, scores, NEG_FILL)
    log_total = jax.nn.logsumexp(scores, axis=-1)
    weights = jnp.exp(scores - log_total[..., None]).astype(BF16)
    result = jnp.einsum("ghlm,gmhe->glhe", weights, values, preferred_element_type=F32)
    return (result.astype(BF16), log_total)


def attend_back(queries, key_rows, values, visible, scaling, log_total, grad_out):
    scores = (
        jnp.einsum("glhe,gmhe->ghlm", queries, key_rows, preferred_element_type=F32) * scaling
    )
    if visible is not None:
        scores = jnp.where(visible, scores, NEG_FILL)
    probs = jnp.exp(scores - log_total[..., None])
    grad_probs = jnp.einsum("glhe,gmhe->ghlm", grad_out, values, preferred_element_type=F32)
    grad_values = jnp.einsum(
        "ghlm,glhe->gmhe", probs.astype(BF16), grad_out, preferred_element_type=F32
    )
    grad_scores = probs * (grad_probs - jnp.sum(probs * grad_probs, axis=-1, keepdims=True))
    grad_scores = grad_scores.astype(BF16)
    grad_queries = (
        jnp.einsum("ghlm,gmhe->glhe", grad_scores, key_rows, preferred_element_type=F32)
        * scaling
    )
    grad_keys = (
        jnp.einsum("ghlm,glhe->gmhe", grad_scores, queries, preferred_element_type=F32)
        * scaling
    )
    return (grad_queries.astype(BF16), grad_keys.astype(BF16), grad_values.astype(BF16))


def line_order(count):
    return list(range(0, count, 2)) + list(reversed(range(1, count, 2)))


class Layout:
    def __init__(self):
        self.tensor = lax.axis_size("tensor")
        self.dp = lax.axis_size("dp")
        self.core = 2
        self.far = 4
        self.near = self.dp // (self.core * self.far)
        self.far_order = line_order(self.far)
        self.near_order = line_order(self.near)
        self.tensor_order = line_order(self.tensor)

    def place(self, far, near, core):
        return (far * self.near + near) * self.core + core

    def hops(self, which):
        pairs = []
        for far in range(self.far):
            for near in range(self.near):
                for core in range(self.core):
                    here = self.place(far, near, core)
                    if which == "far":
                        spot = self.far_order.index(far)
                        there = (self.far_order[(spot + 1) % self.far], near, core)
                    elif which == "near":
                        spot = self.near_order.index(near)
                        there = (far, self.near_order[(spot + 1) % self.near], core)
                    else:
                        there = (far, near, 1 - core)
                    pairs.append((here, self.place(*there)))
        return pairs

    def send(self, field, which):
        if which == "tensor":
            count = self.tensor
            order = self.tensor_order
            pairs = [(order[i], order[(i + 1) % count]) for i in range(count)]
            return lax.ppermute(field, "tensor", pairs)
        return lax.ppermute(field, "dp", self.hops(which))

    def ring_gather(self, field, which, count):
        blocks = [field]
        for _ in range(count - 1):
            blocks.append(self.send(blocks[-1], which))
        return blocks

    def ring_sum(self, blocks, which):
        count = len(blocks)
        if count == 1:
            return blocks[0].astype(F32)
        moving = blocks[1].astype(BF16)
        for step in range(2, count):
            moving = (self.send(moving, which).astype(F32) + blocks[step].astype(F32)).astype(BF16)
        return self.send(moving, which).astype(F32) + blocks[0].astype(F32)

    def gather_rows(self, piece):
        near_in = jnp.concatenate(self.ring_gather(piece, "far", self.far), axis=0)
        mine = self.ring_gather(near_in, "near", self.near)
        others = [self.send(part, "core") for part in mine]
        return jnp.concatenate(mine + others, axis=0)

    def sum_rows(self, rows):
        half = rows.shape[0] // 2
        arrived = self.send(rows[half:], "core")
        rows = (rows[:half].astype(F32) + arrived.astype(F32)).astype(BF16)
        size = half // self.near
        blocks = [rows[i * size : (i + 1) * size] for i in range(self.near)]
        rows = self.ring_sum(blocks, "near").astype(BF16)
        size = size // self.far
        blocks = [rows[i * size : (i + 1) * size] for i in range(self.far)]
        return self.ring_sum(blocks, "far")

    def own_features(self, block, spot):
        me = lax.axis_index("dp")
        core = me % self.core
        near = (me // self.core) % self.near
        far = me // (self.core * self.near)

        def look(table, index):
            found = jnp.zeros_like(index)
            for place, value in enumerate(table):
                found = jnp.where(index == place, value, found)
            return found

        def spots(order):
            return [order.index(place) for place in range(len(order))]

        inner = spot % block
        which = spot // block
        far_step = which % self.far
        near_step = (which // self.far) % self.near
        core_step = which // (self.far * self.near)
        far_at = look(self.far_order, (look(spots(self.far_order), far) - far_step) % self.far)
        near_at = look(
            self.near_order, (look(spots(self.near_order), near) - near_step) % self.near
        )
        core_at = (core + core_step) % self.core
        return ((far_at * self.near + near_at) * self.core + core_at) * block + inner


def padded(width):
    return -(-width // LANES) * LANES


def widen(field):
    extra = padded(field.shape[-1]) - field.shape[-1]
    if extra == 0:
        return field
    return jnp.pad(field, [(0, 0)] * (field.ndim - 1) + [(0, extra)])


def per_device(
    tokens,
    text,
    lengths,
    modulation,
    self_qkv,
    self_out,
    cross_query,
    cross_keyvalue,
    cross_out,
    mlp_in,
    mlp_out,
    cotangent,
):
    lay = Layout()
    tensor_size = lay.tensor
    rows_here = tokens.shape[1]
    total_rows = rows_here * tensor_size
    frames_all = total_rows // PATCH
    heads_here = HEADS // tensor_size
    columns = heads_here * HEAD_DIM
    wide = padded(columns)
    width = tokens.shape[2]
    block = self_qkv.shape[1]
    scaling = HEAD_DIM ** (-0.5)
    me_tensor = lax.axis_index("tensor")
    visible = jnp.arange(TEXT) < lengths[0]

    spot = lax.broadcasted_iota(jnp.int32, (1, width), 1)
    wanted = lay.own_features(block, spot)
    feature = lax.broadcasted_iota(jnp.int32, (width, width), 0)
    order = (feature == wanted).astype(BF16)

    def exact(left, right, contract):
        return lax.dot_general(
            left,
            right.astype(left.dtype),
            (contract, ((), ())),
            precision=lax.Precision.HIGHEST,
            preferred_element_type=F32,
        )

    def into(field):
        if field.dtype == BF16:
            return dot(field, order)
        return exact(field, order, ((1,), (0,)))

    def back(field):
        if field.dtype == BF16:
            return dot(field, order, ((1,), (1,))).astype(BF16)
        return exact(field, order, ((1,), (1,)))

    def spread(field):
        return jnp.concatenate(lay.ring_gather(field, "tensor", tensor_size), axis=0)

    def collect(whole):
        return lay.ring_sum(
            [whole[i * rows_here : (i + 1) * rows_here] for i in range(tensor_size)], "tensor"
        )

    def fetch(layer):
        qkv = self_qkv[layer]
        keyval = cross_keyvalue[layer]
        first = jnp.concatenate(
            [widen(qkv[:, 0]), widen(qkv[:, 1]), widen(qkv[:, 2]), widen(self_out[layer].T)], axis=1
        )
        second = jnp.concatenate(
            [
                widen(cross_query[layer]),
                widen(keyval[:, 0]),
                widen(keyval[:, 1]),
                widen(cross_out[layer].T),
            ],
            axis=1,
        )
        return [lay.gather_rows(part) for part in (first, second, mlp_in[layer], mlp_out[layer].T)]

    def to_groups(field, layer):
        grouped = field.reshape(frames_all, PATCH, heads_here, HEAD_DIM)
        if layer % 2 == 1:
            grouped = grouped.transpose(1, 0, 2, 3)
        return grouped

    def from_groups(field, layer):
        if layer % 2 == 1:
            field = field.transpose(1, 0, 2, 3)
        return field.reshape(total_rows, columns)

    def piece(weight, index):
        return weight[:, index * wide : index * wide + columns]

    text_full = jnp.concatenate(
        [
            part
            for part in [lax.all_gather(text[0], "tensor", axis=1, tiled=True)]
        ],
        axis=1,
    )
    text_full = into(text_full).astype(BF16)
    table = into(modulation[0].reshape(LAYERS * 6, width)).reshape(LAYERS, 6, width)

    gathered = [fetch(layer) for layer in range(LAYERS)]

    stream = into(tokens[0])
    memory = []
    for layer in range(LAYERS):
        adaln = table[layer]
        first, second, weight_in, weight_out = gathered[layer]
        first_in = stream
        unit_one, root_one = normalize(first_in)
        normed_all = spread((unit_one * (1.0 + adaln[1]) + adaln[0]).astype(BF16))
        qkv_rows = [dot(normed_all, piece(first, i)).astype(BF16) for i in range(3)]
        queries, key_rows, values = [to_groups(part, layer) for part in qkv_rows]
        attended, log_self = attend_forward(queries, key_rows, values, None, scaling)
        attended = from_groups(attended, layer)
        branch = collect(dot(attended, piece(first, 3), ((1,), (1,))))
        second_in = first_in + adaln[2] * branch
        cross_all = spread(second_in.astype(BF16))
        cross_q = dot(cross_all, piece(second, 0)).astype(BF16)
        cross_q = cross_q.reshape(1, total_rows, heads_here, HEAD_DIM)
        text_keys = dot(text_full, piece(second, 1)).astype(BF16)
        text_values = dot(text_full, piece(second, 2)).astype(BF16)
        text_keys = text_keys.reshape(1, TEXT, heads_here, HEAD_DIM)
        text_values = text_values.reshape(1, TEXT, heads_here, HEAD_DIM)
        cross_att, log_cross = attend_forward(cross_q, text_keys, text_values, visible, scaling)
        cross_att = cross_att.reshape(total_rows, columns)
        crossed = collect(dot(cross_att, piece(second, 3), ((1,), (1,))))
        third_in = second_in + crossed
        unit_two, root_two = normalize(third_in)
        inner_all = spread((unit_two * (1.0 + adaln[4]) + adaln[3]).astype(BF16))
        hidden = gelu_tanh(dot(inner_all, weight_in)).astype(BF16)
        mlp_branch = collect(dot(hidden, weight_out, ((1,), (1,))))
        stream = third_in + adaln[5] * mlp_branch
        memory.append(
            (
                adaln,
                unit_one,
                root_one,
                normed_all,
                queries,
                key_rows,
                values,
                attended,
                log_self,
                branch,
                cross_all,
                cross_q,
                text_keys,
                text_values,
                cross_att,
                log_cross,
                unit_two,
                root_two,
                inner_all,
                mlp_branch,
            )
        )
    output = back(stream.astype(BF16))
    grad_stream = into(cotangent[0])
    grad_text = jnp.zeros((TEXT, width), F32)
    layer_grads = [None] * LAYERS
    table_rows = [None] * LAYERS
    for layer in reversed(range(LAYERS)):
        (
            adaln,
            unit_one,
            root_one,
            normed_all,
            queries,
            key_rows,
            values,
            attended,
            log_self,
            branch,
            cross_all,
            cross_q,
            text_keys,
            text_values,
            cross_att,
            log_cross,
            unit_two,
            root_two,
            inner_all,
            mlp_branch,
        ) = memory[layer]
        first, second, weight_in, weight_out = gathered[layer]
        rows_of = ((0,), (0,))
        over_columns = ((1,), (1,))

        grad_gate_two = jnp.sum(grad_stream * mlp_branch, axis=0)
        grad_mlp = spread((adaln[5] * grad_stream).astype(BF16))
        pre_mlp = dot(inner_all, weight_in)
        hidden_f, gelu_backward = jax.vjp(gelu_tanh, pre_mlp)
        hidden = hidden_f.astype(BF16)
        grad_hidden = dot(grad_mlp, weight_out)
        grad_pre = gelu_backward(grad_hidden)[0].astype(BF16)
        grad_inner = collect(dot(grad_pre, weight_in, over_columns))
        wide_out = lay.sum_rows(dot(grad_mlp, hidden, rows_of).astype(BF16))
        wide_in = lay.sum_rows(dot(inner_all, grad_pre, rows_of).astype(BF16))
        grad_shift_two = jnp.sum(grad_inner, axis=0)
        grad_scale_two = jnp.sum(grad_inner * unit_two, axis=0)
        grad_stream = grad_stream + norm_back(grad_inner * (1.0 + adaln[4]), unit_two, root_two)

        grad_crossed = spread(grad_stream.astype(BF16))
        grad_catt = dot(grad_crossed, piece(second, 3)).astype(BF16)
        grad_cq, grad_tkeys, grad_tvalues = attend_back(
            cross_q,
            text_keys,
            text_values,
            visible,
            scaling,
            log_cross,
            grad_catt.reshape(1, total_rows, heads_here, HEAD_DIM),
        )
        grad_cq = grad_cq.reshape(total_rows, columns)
        grad_tkeys = grad_tkeys.reshape(TEXT, columns)
        grad_tvalues = grad_tvalues.reshape(TEXT, columns)
        grad_stream = grad_stream + collect(dot(grad_cq, piece(second, 0), over_columns))
        grad_text = (
            grad_text
            + dot(grad_tkeys, piece(second, 1), over_columns)
            + dot(grad_tvalues, piece(second, 2), over_columns)
        )
        wide_second = lay.sum_rows(
            jnp.concatenate(
                [
                    widen(dot(cross_all, grad_cq, rows_of).astype(BF16)),
                    widen(dot(text_full, grad_tkeys, rows_of).astype(BF16)),
                    widen(dot(text_full, grad_tvalues, rows_of).astype(BF16)),
                    widen(dot(grad_crossed, cross_att, rows_of).astype(BF16)),
                ],
                axis=1,
            )
        )

        grad_gate_one = jnp.sum(grad_stream * branch, axis=0)
        grad_branch = spread((adaln[2] * grad_stream).astype(BF16))
        grad_att = to_groups(dot(grad_branch, piece(first, 3)).astype(BF16), layer)
        grads = attend_back(queries, key_rows, values, None, scaling, log_self, grad_att)
        grad_q, grad_k, grad_v = [from_groups(part, layer) for part in grads]
        partial = (
            dot(grad_q, piece(first, 0), over_columns)
            + dot(grad_k, piece(first, 1), over_columns)
            + dot(grad_v, piece(first, 2), over_columns)
        )
        grad_normed = collect(partial)
        wide_first = lay.sum_rows(
            jnp.concatenate(
                [
                    widen(dot(normed_all, grad_q, rows_of).astype(BF16)),
                    widen(dot(normed_all, grad_k, rows_of).astype(BF16)),
                    widen(dot(normed_all, grad_v, rows_of).astype(BF16)),
                    widen(dot(grad_branch, attended, rows_of).astype(BF16)),
                ],
                axis=1,
            )
        )
        grad_shift_one = jnp.sum(grad_normed, axis=0)
        grad_scale_one = jnp.sum(grad_normed * unit_one, axis=0)
        grad_stream = grad_stream + norm_back(grad_normed * (1.0 + adaln[1]), unit_one, root_one)
        table_rows[layer] = jnp.stack(
            [
                grad_shift_one,
                grad_scale_one,
                grad_gate_one,
                grad_shift_two,
                grad_scale_two,
                grad_gate_two,
            ]
        )
        layer_grads[layer] = (
            jnp.stack([piece(wide_first, i) for i in range(3)], axis=1),
            piece(wide_first, 3).T,
            piece(wide_second, 0),
            jnp.stack([piece(wide_second, i) for i in (1, 2)], axis=1),
            piece(wide_second, 3).T,
            wide_in,
            wide_out.T,
        )
    share = width // tensor_size
    grad_text = back(grad_text)
    text_grad = lax.psum_scatter(grad_text, "tensor", scatter_dimension=1, tiled=True)
    table_grad = back(
        lax.psum(jnp.stack(table_rows), "tensor").reshape(LAYERS * 6, width)
    ).reshape(LAYERS, 6, width)
    stacked = [
        jnp.stack([layer_grads[layer][member] for layer in range(LAYERS)]) for member in range(7)
    ]
    return (
        output[None],
        back(grad_stream)[None],
        text_grad[None],
        table_grad[None],
        *stacked,
    )


def solution(mesh):
    return jax.shard_map(
        per_device,
        mesh=mesh,
        in_specs=(
            P("dp", "tensor", None),
            P("dp", None, "tensor"),
            P("dp"),
            P("dp", None, None, None),
            P(None, "dp", None, "tensor"),
            P(None, "tensor", "dp"),
            P(None, "dp", "tensor"),
            P(None, "dp", None, "tensor"),
            P(None, "tensor", "dp"),
            P(None, "dp", "tensor"),
            P(None, "tensor", "dp"),
            P("dp", "tensor", None),
        ),
        out_specs=(
            P("dp", "tensor", None),
            P("dp", "tensor", None),
            P("dp", None, "tensor"),
            P("dp", None, None, None),
            P(None, "dp", None, "tensor"),
            P(None, "tensor", "dp"),
            P(None, "dp", "tensor"),
            P(None, "dp", None, "tensor"),
            P(None, "tensor", "dp"),
            P(None, "dp", "tensor"),
            P(None, "tensor", "dp"),
        ),
        check_vma=False,
    )
```

time: 2970 us -> 1150 us (0.39)
  waiting for transfers between devices: 2420 us -> 496 us
  starting transfers between devices: 4.49 us -> 155 us
  matrix products: 273 us -> 230 us
    reduce_scatter x18 -> x0, waiting for transfers between devices: 1100 us -> none  [the longest x12 392 us: collect(): lax.psum_scatter(project(field), 'tensor', scatter_dimension=0, tiled=True)]
    all_gather x26 -> x0, waiting for transfers between devices: 809 us -> none  [the longest x12 249 us: spread(): return lax.all_gather(field, 'tensor', axis=0, tiled=True)]
    unnamed x59 -> x1, waiting for transfers between devices: 500 us -> 0.02 us
    ppermute x0 -> x112, waiting for transfers between devices: none -> 496 us  [the longest x88 347 us: send(): return lax.ppermute(field, 'dp', self.hops(which))]
    ppermute x0 -> x112, starting transfers between devices: none -> 155 us  [the longest x88 121 us: send(): return lax.ppermute(field, 'dp', self.hops(which))]
    dot_general x58 -> x84, matrix products: 260 us -> 219 us  [the longest x64 168 us: dot(): lax.dot_general(left, right, (contract, ((), ())), preferred_element_type...]
    another operation x19 -> x1, local copies, waits for them, and re-layouts: 33.8 us -> 0.01 us  [per_device(): modulation[0].reshape(LAYERS * 6, width)]
  transfers between devices with their start and end apart: 52 -> 113, of which waited for: 49 -> 59; matrix products, arithmetic and copies ran while one was open for 10% -> 36% of each run, Pallas kernels for 0% -> 0%
where the time goes in v1:
time: 1150 us; the launch traced here: 1140 us
  waiting for transfers between devices  496 us (43%)
  matrix products  230 us (20%)
  starting transfers between devices  155 us (13%)
  local copies, waits for them, and re-layouts  135 us (12%)
  other arithmetic  86.5 us (8%)
  blocking collectives  22.1 us (2%)
  between operations  19.3 us (2%)
    ppermute x88, waiting for transfers between devices, send(): return lax.ppermute(field, 'dp', self.hops(which))  347 us
    dot_general x64, matrix products, dot(): lax.dot_general(left, right, (contract, ((), ())), preferred_element_type...  168 us
    ppermute x24, waiting for transfers between devices, send(): return lax.ppermute(field, 'tensor', pairs)  149 us
    ppermute x88, starting transfers between devices, send(): return lax.ppermute(field, 'dp', self.hops(which))  121 us
    unnamed x489, local copies, waits for them, and re-layouts  57.2 us
    ppermute x24, starting transfers between devices, send(): return lax.ppermute(field, 'tensor', pairs)  34 us
  transfers between devices with their start and end apart: 113, of which 59 were waited for; matrix products, arithmetic and copies ran while one was open for 36% of the time, Pallas kernels for 0%

profile of v1, /device:TPU:0, one launch (start us, length us, event | category | flops | bytes accessed | tf_op | source)
XLA Modules:
  0.0 1143.5 jit_solution(4133961978206638291)
XLA Ops:
  27.1 13.6 %all-gather = bf16[1,120,1152]{1,2,0:T(8,128)(2,1)S(1)} all-gather(bf16[1,120,576]{1,2,0:T(8,128)(2,1)S(1)} %copy-done.132), channel_id=2, replica_groups=mesh['dp'=16,'tensor'=2] {'tensor'}, dimensions={2}, use_global_device_ids=true | all-gather | bytes 414720 | tf_op jit(solution)/shard_map/all_gather | solution.py:285
  148.5 21.3 %collective-permute-done.25 = bf16[72,2304]{1,0:T(8,128)(2,1)S(1)} collective-permute-done((bf16[72,2304]{1,0:T(8,128)(2,1)S(1)}, bf16[72,2304]{1,0:T(8,128)(2,1)S(1)}, u32[]{:S(2)}, u32[]{:S(2)}) %collective-permute-start.25) | collective-permute-done | bytes 331808 | tf_op jit(solution)/shard_map/ppermute | solution.py:118
  204.2 11.9 %collective-permute-done.50 = bf16[288,2304]{1,0:T(8,128)(2,1)S(1)} collective-permute-done((bf16[288,2304]{1,0:T(8,128)(2,1)}, bf16[288,2304]{1,0:T(8,128)(2,1)S(1)}, u32[]{:S(2)}, u32[]{:S(2)}) %collective-permute-start.50) | collective-permute-done | bytes 1327136 | tf_op jit(solution)/shard_map/ppermute | solution.py:118
  216.2 28.3 %collective-permute-done.20 = bf16[288,2304]{1,0:T(8,128)(2,1)S(1)} collective-permute-done((bf16[288,2304]{1,0:T(8,128)(2,1)S(1)}, bf16[288,2304]{1,0:T(8,128)(2,1)S(1)}, u32[]{:S(2)}, u32[]{:S(2)}) %collective-permute-start.20) | collective-permute-done | bytes 1327136 | tf_op jit(solution)/shard_map/ppermute | solution.py:118
  246.0 30.1 %collective-permute-done.4 = bf16[288,2560]{1,0:T(8,128)(2,1)S(1)} collective-permute-done((bf16[288,2560]{1,0:T(8,128)(2,1)S(1)}, bf16[288,2560]{1,0:T(8,128)(2,1)S(1)}, u32[]{:S(2)}, u32[]{:S(2)}) %collective-permute-start.4) | collective-permute-done | bytes 1474592 | tf_op jit(solution)/shard_map/ppermute | solution.py:118
  280.3 22.6 %collective-permute-done.11 = bf16[288,2560]{1,0:T(8,128)(2,1)} collective-permute-done((bf16[288,2560]{1,0:T(8,128)(2,1)}, bf16[288,2560]{1,0:T(8,128)(2,1)}, u32[]{:S(2)}, u32[]{:S(2)}) %collective-permute-start.11) | collective-permute-done | bytes 1474592 | tf_op jit(solution)/shard_map/ppermute | solution.py:118
  327.9 10.7 collective-permute-done.7
  344.8 9.7 collective-permute-done.14
  359.2 11.4 collective-permute-done.26
  372.5 9.8 collective-permute-done.15
  385.5 13.7 %collective-permute-done.16 = bf16[256,1152]{1,0:T(8,128)(2,1)S(1)} collective-permute-done((bf16[256,1152]{1,0:T(8,128)(2,1)S(1)}, bf16[256,1152]{1,0:T(8,128)(2,1)S(1)}, u32[]{:S(2)}, u32[]{:S(2)}) %collective-permute-start.16) | collective-permute-done | bytes 589856 | tf_op jit(solution)/shard_map/ppermute | solution.py:117
  400.7 17.4 %fusion.169 = f32[512,2304]{1,0:T(8,128)} fusion(bf16[1152,2304]{1,0:T(8,128)(2,1)S(1)} %constant_dynamic-update-slice_fusion.14, bf16[256,1152]{1,0:T(8,128)(2,1)S(1)} %collective-permute-done.16, bf16[256,1152]{1,0:T(8,128)(2,1)S(1)} %add_convert_fusion.19), kind=kOutput, calls=%fused_computation.345 | convolution fusion | flops 2720268288 | bytes 11206656 | tf_op jit(solution)/shard_map/dot_general | solution.py:38
  441.9 24.6 %collective-permute-done.41 = bf16[288,2560]{1,0:T(8,128)(2,1)} collective-permute-done((bf16[288,2560]{1,0:T(8,128)(2,1)}, bf16[288,2560]{1,0:T(8,128)(2,1)}, u32[]{:S(2)}, u32[]{:S(2)}) %collective-permute-start.41) | collective-permute-done | bytes 1474592 | tf_op jit(solution)/shard_map/ppermute | solution.py:118
  521.0 8.4 collective-permute-done.37
  555.1 11.4 collective-permute-done.45
  570.5 11.8 %collective-permute-done.46 = bf16[256,1152]{1,0:T(8,128)(2,1)S(1)} collective-permute-done((bf16[256,1152]{1,0:T(8,128)(2,1)S(1)}, bf16[256,1152]{1,0:T(8,128)(2,1)S(1)}, u32[]{:S(2)}, u32[]{:S(2)}) %collective-permute-start.46) | collective-permute-done | bytes 589856 | tf_op jit(solution)/shard_map/ppermute | solution.py:117
  611.8 18.6 %collective-permute-done.61 = bf16[256,1152]{1,0:T(8,128)(2,1)S(1)} collective-permute-done((bf16[256,1152]{1,0:T(8,128)(2,1)S(1)}, bf16[256,1152]{1,0:T(8,128)(2,1)S(1)}, u32[]{:S(2)}, u32[]{:S(2)}) %collective-permute-start.61) | collective-permute-done | bytes 589856 | tf_op jit(solution)/shard_map/ppermute | solution.py:117
  657.3 11.8 %collective-permute-done.63 = bf16[256,1152]{1,0:T(8,128)(2,1)S(1)} collective-permute-done((bf16[256,1152]{1,0:T(8,128)(2,1)S(1)}, bf16[256,1152]{1,0:T(8,128)(2,1)S(1)}, u32[]{:S(2)}, u32[]{:S(2)}) %collective-permute-start.63) | collective-permute-done | bytes 589856 | tf_op jit(solution)/shard_map/ppermute | solution.py:117
  696.8 10.5 multiply_reduce_fusion.2
  774.8 8.5 fusion.38
  1003.1 20.4 %collective-permute-done.93 = bf16[288,2304]{1,0:T(8,128)(2,1)S(1)} collective-permute-done((bf16[288,2304]{1,0:T(8,128)(2,1)S(1)}, bf16[288,2304]{1,0:T(8,128)(2,1)S(1)}, u32[]{:S(2)}, u32[]{:S(2)}) %collective-permute-start.93) | collective-permute-done | bytes 1327136 | tf_op jit(solution)/shard_map/ppermute | solution.py:118
  1090.2 16.0 %collective-permute-done.73 = bf16[288,2560]{1,0:T(8,128)(2,1)S(1)} collective-permute-done((bf16[288,2560]{1,0:T(8,128)(2,1)S(1)}, bf16[288,2560]{1,0:T(8,128)(2,1)S(1)}, u32[]{:S(2)}, u32[]{:S(2)}) %collective-permute-start.73) | collective-permute-done | bytes 1474592 | tf_op jit(solution)/shard_map/ppermute | solution.py:118
  1107.0 8.9 collective-permute-done.74
  1116.2 10.4 collective-permute-done.75
  (1040 shorter events, 762.4 us)
Async XLA Ops:
  7.2 1129.1 %reduce-scatter.2.cloned.1.call-start = ((), (), s32[]{:S(2)}) async-start(), calls=%async_computation.1 | async-start | bytes 884736 | tf_op jit(solution)/shard_map/reduce_scatter | solution.py:472
  23.2 280.4 %collective-permute-start = (bf16[256,1152]{1,0:T(8,128)(2,1)S(1)}, bf16[256,1152]{1,0:T(8,128)(2,1)S(1)}, u32[]{:S(2)}, u32[]{:S(2)}) collective-permute-start(bf16[256,1152]{1,0:T(8,128)(2,1)S(1)} %add_convert_fusion.20), channel_id=1, source_target_pairs={{0,1},{1,0},{2,3},{3,2},{4,5},{5,4},{6,7},{7,6},{8,9},{9,8},{10,11... | collective-permute-start | bytes 1769480 | tf_op jit(solution)/shard_map/ppermute | solution.py:117
  120.7 61.5 %collective-permute-start.49 = (bf16[72,2304]{1,0:T(8,128)(2,1)S(1)}, bf16[72,2304]{1,0:T(8,128)(2,1)S(1)}, u32[]{:S(2)}, u32[]{:S(2)}) collective-permute-start(bf16[72,2304]{1,0:T(8,128)(2,1)S(1)} %collective-permute-done.48), channel_id=1, source_target_pairs={{0,16},{2,18},{4,20},{6,22},{8,0},{10,2},{12,4},{14,6},{16,24},{18... | collective-permute-start | bytes 995336 | tf_op jit(solution)/shard_map/ppermute | solution.py:118
  190.0 54.5 %collective-permute-start.20 = (bf16[288,2304]{1,0:T(8,128)(2,1)S(1)}, bf16[288,2304]{1,0:T(8,128)(2,1)S(1)}, u32[]{:S(2)}, u32[]{:S(2)}) collective-permute-start(bf16[288,2304]{1,0:T(8,128)(2,1)S(1)} %pad_maximum_fusion.4), channel_id=1, source_target_pairs={{0,4},{2,6},{4,0},{6,2},{8,12},{10,14},{12,8},{14,10},{16,20},{18,... | collective-permute-start | bytes 3981320 | tf_op jit(solution)/shard_map/ppermute | solution.py:118
  197.8 78.3 %collective-permute-start.4 = (bf16[288,2560]{1,0:T(8,128)(2,1)S(1)}, bf16[288,2560]{1,0:T(8,128)(2,1)S(1)}, u32[]{:S(2)}, u32[]{:S(2)}) collective-permute-start(bf16[288,2560]{1,0:T(8,128)(2,1)S(1)} %pad_maximum_fusion), channel_id=1, source_target_pairs={{0,4},{2,6},{4,0},{6,2},{8,12},{10,14},{12,8},{14,10},{16,20},{18,... | collective-permute-start | bytes 4423688 | tf_op jit(solution)/shard_map/ppermute | solution.py:118
  202.1 74.1 %collective-permute-start.21 = (bf16[288,2304]{1,0:T(8,128)(2,1)S(1)}, bf16[288,2304]{1,0:T(8,128)(2,1)S(1)}, u32[]{:S(2)}, u32[]{:S(2)}) collective-permute-start(bf16[288,2304]{1,0:T(8,128)(2,1)S(1)} %pad_maximum_fusion.4), channel_id=1, source_target_pairs={{0,2},{2,0},{4,6},{6,4},{8,10},{10,8},{12,14},{14,12},{16,18},{18,... | collective-permute-start | bytes 3981320 | tf_op jit(solution)/shard_map/ppermute | solution.py:118
  216.1 61.9 %collective-permute-start.5 = (bf16[288,2560]{1,0:T(8,128)(2,1)S(1)}, bf16[288,2560]{1,0:T(8,128)(2,1)S(1)}, u32[]{:S(2)}, u32[]{:S(2)}) collective-permute-start(bf16[288,2560]{1,0:T(8,128)(2,1)S(1)} %pad_maximum_fusion), channel_id=1, source_target_pairs={{0,2},{2,0},{4,6},{6,4},{8,10},{10,8},{12,14},{14,12},{16,18},{18,... | collective-permute-start | bytes 4423688 | tf_op jit(solution)/shard_map/ppermute | solution.py:118
  244.5 58.4 %collective-permute-start.11 = (bf16[288,2560]{1,0:T(8,128)(2,1)}, bf16[288,2560]{1,0:T(8,128)(2,1)}, u32[]{:S(2)}, u32[]{:S(2)}) collective-permute-start(bf16[288,2560]{1,0:T(8,128)(2,1)} %pad_maximum_fusion.1), channel_id=1, source_target_pairs={{0,4},{2,6},{4,0},{6,2},{8,12},{10,14},{12,8},{14,10},{16,20},{18,... | collective-permute-start | bytes 4423688 | tf_op jit(solution)/shard_map/ppermute | solution.py:118
  276.2 314.5 %collective-permute-start.60 = (bf16[256,1152]{1,0:T(8,128)(2,1)}, bf16[256,1152]{1,0:T(8,128)(2,1)}, u32[]{:S(2)}, u32[]{:S(2)}) collective-permute-start(bf16[256,1152]{1,0:T(8,128)(2,1)} %get-tuple-element.162), channel_id=1, source_target_pairs={{0,1},{1,0},{2,3},{3,2},{4,5},{5,4},{6,7},{7,6},{8,9},{9,8},{10,11... | collective-permute-start | bytes 1769480 | tf_op jit(solution)/shard_map/ppermute | solution.py:117
  278.0 272.9 %collective-permute-start.51 = (bf16[288,2304]{1,0:T(8,128)(2,1)}, bf16[288,2304]{1,0:T(8,128)(2,1)}, u32[]{:S(2)}, u32[]{:S(2)}) collective-permute-start(bf16[288,2304]{1,0:T(8,128)(2,1)} %pad_maximum_fusion.6), channel_id=1, source_target_pairs={{0,2},{2,0},{4,6},{6,4},{8,10},{10,8},{12,14},{14,12},{16,18},{18,... | collective-permute-start | bytes 3981320 | tf_op jit(solution)/shard_map/ppermute | solution.py:118
  354.5 69.8 %collective-permute-start.56 = (bf16[288,2304]{1,0:T(8,128)(2,1)S(1)}, bf16[288,2304]{1,0:T(8,128)(2,1)S(1)}, u32[]{:S(2)}, u32[]{:S(2)}) collective-permute-start(bf16[288,2304]{1,0:T(8,128)(2,1)S(1)} %copy-done.67), channel_id=1, source_target_pairs={{0,4},{2,6},{4,0},{6,2},{8,12},{10,14},{12,8},{14,10},{16,20},{18,... | collective-permute-start | bytes 3981320 | tf_op jit(solution)/shard_map/ppermute | solution.py:118
  385.3 54.8 %collective-permute-start.35 = (bf16[288,2560]{1,0:T(8,128)(2,1)S(1)}, bf16[288,2560]{1,0:T(8,128)(2,1)S(1)}, u32[]{:S(2)}, u32[]{:S(2)}) collective-permute-start(bf16[288,2560]{1,0:T(8,128)(2,1)S(1)} %copy-done.66), channel_id=1, source_target_pairs={{0,2},{2,0},{4,6},{6,4},{8,10},{10,8},{12,14},{14,12},{16,18},{18,... | collective-permute-start | bytes 4423688 | tf_op jit(solution)/shard_map/ppermute | solution.py:118
  466.5 52.0 %collective-permute-start.42 = (bf16[288,2560]{1,0:T(8,128)(2,1)}, bf16[288,2560]{1,0:T(8,128)(2,1)}, u32[]{:S(2)}, u32[]{:S(2)}) collective-permute-start(bf16[288,2560]{1,0:T(8,128)(2,1)} %pad_maximum_fusion.3), channel_id=1, source_target_pairs={{0,2},{2,0},{4,6},{6,4},{8,10},{10,8},{12,14},{14,12},{16,18},{18,... | collective-permute-start | bytes 4423688 | tf_op jit(solution)/shard_map/ppermute | solution.py:118
  466.5 63.3 %collective-permute-start.43 = (bf16[288,2560]{1,0:T(8,128)(2,1)}, bf16[288,2560]{1,0:T(8,128)(2,1)}, u32[]{:S(2)}, u32[]{:S(2)}) collective-permute-start(bf16[288,2560]{1,0:T(8,128)(2,1)} %collective-permute-done.41), channel_id=1, source_target_pairs={{0,2},{2,0},{4,6},{6,4},{8,10},{10,8},{12,14},{14,12},{16,18},{18,... | collective-permute-start | bytes 4423688 | tf_op jit(solution)/shard_map/ppermute | solution.py:118
  642.9 108.5 %collective-permute-start.107 = (bf16[576,2304]{1,0:T(8,128)(2,1)}, bf16[576,2304]{1,0:T(8,128)(2,1)}, u32[]{:S(2)}, u32[]{:S(2)}) collective-permute-start(bf16[576,2304]{1,0:T(8,128)(2,1)} %slice.813), channel_id=1, source_target_pairs={{0,2},{2,0},{4,6},{6,4},{8,10},{10,8},{12,14},{14,12},{16,18},{18,... | collective-permute-start | bytes 7962632 | tf_op jit(solution)/shard_map/ppermute | solution.py:118
  642.9 117.7 %collective-permute-start.97 = (bf16[576,2304]{1,0:T(8,128)(2,1)}, bf16[576,2304]{1,0:T(8,128)(2,1)}, u32[]{:S(2)}, u32[]{:S(2)}) collective-permute-start(bf16[576,2304]{1,0:T(8,128)(2,1)} %slice.797), channel_id=1, source_target_pairs={{0,2},{2,0},{4,6},{6,4},{8,10},{10,8},{12,14},{14,12},{16,18},{18,... | collective-permute-start | bytes 7962632 | tf_op jit(solution)/shard_map/ppermute | solution.py:118
  674.2 146.2 %collective-permute-start.87 = (bf16[576,2560]{1,0:T(8,128)(2,1)}, bf16[576,2560]{1,0:T(8,128)(2,1)}, u32[]{:S(2)}, u32[]{:S(2)}) collective-permute-start(bf16[576,2560]{1,0:T(8,128)(2,1)} %slice.774), channel_id=1, source_target_pairs={{0,2},{2,0},{4,6},{6,4},{8,10},{10,8},{12,14},{14,12},{16,18},{18,... | collective-permute-start | bytes 8847368 | tf_op jit(solution)/shard_map/ppermute | solution.py:118
  751.4 155.9 %collective-permute-start.77 = (bf16[576,2560]{1,0:T(8,128)(2,1)}, bf16[576,2560]{1,0:T(8,128)(2,1)}, u32[]{:S(2)}, u32[]{:S(2)}) collective-permute-start(bf16[576,2560]{1,0:T(8,128)(2,1)} %slice.752), channel_id=1, source_target_pairs={{0,2},{2,0},{4,6},{6,4},{8,10},{10,8},{12,14},{14,12},{16,18},{18,... | collective-permute-start | bytes 8847368 | tf_op jit(solution)/shard_map/ppermute | solution.py:118
  805.8 144.8 %collective-permute-start.102 = (bf16[576,2304]{1,0:T(8,128)(2,1)}, bf16[576,2304]{1,0:T(8,128)(2,1)}, u32[]{:S(2)}, u32[]{:S(2)}) collective-permute-start(bf16[576,2304]{1,0:T(8,128)(2,1)} %slice.805), channel_id=1, source_target_pairs={{0,2},{2,0},{4,6},{6,4},{8,10},{10,8},{12,14},{14,12},{16,18},{18,... | collective-permute-start | bytes 7962632 | tf_op jit(solution)/shard_map/ppermute | solution.py:118
  815.4 138.0 %collective-permute-start.92 = (bf16[576,2304]{1,0:T(8,128)(2,1)}, bf16[576,2304]{1,0:T(8,128)(2,1)}, u32[]{:S(2)}, u32[]{:S(2)}) collective-permute-start(bf16[576,2304]{1,0:T(8,128)(2,1)} %slice.789), channel_id=1, source_target_pairs={{0,2},{2,0},{4,6},{6,4},{8,10},{10,8},{12,14},{14,12},{16,18},{18,... | collective-permute-start | bytes 7962632 | tf_op jit(solution)/shard_map/ppermute | solution.py:118
  854.4 58.6 %collective-permute-start.88 = (bf16[288,2560]{1,0:T(8,128)(2,1)}, bf16[288,2560]{1,0:T(8,128)(2,1)}, u32[]{:S(2)}, u32[]{:S(2)}) collective-permute-start(bf16[288,2560]{1,0:T(8,128)(2,1)} %slice.775), channel_id=1, source_target_pairs={{0,4},{2,6},{4,0},{6,2},{8,12},{10,14},{12,8},{14,10},{16,20},{18,... | collective-permute-start | bytes 4423688 | tf_op jit(solution)/shard_map/ppermute | solution.py:118
  906.2 119.8 %collective-permute-start.82 = (bf16[576,2560]{1,0:T(8,128)(2,1)}, bf16[576,2560]{1,0:T(8,128)(2,1)}, u32[]{:S(2)}, u32[]{:S(2)}) collective-permute-start(bf16[576,2560]{1,0:T(8,128)(2,1)} %slice.765), channel_id=1, source_target_pairs={{0,2},{2,0},{4,6},{6,4},{8,10},{10,8},{12,14},{14,12},{16,18},{18,... | collective-permute-start | bytes 8847368 | tf_op jit(solution)/shard_map/ppermute | solution.py:118
  913.0 75.5 %collective-permute-start.78 = (bf16[288,2560]{1,0:T(8,128)(2,1)}, bf16[288,2560]{1,0:T(8,128)(2,1)}, u32[]{:S(2)}, u32[]{:S(2)}) collective-permute-start(bf16[288,2560]{1,0:T(8,128)(2,1)} %slice.753), channel_id=1, source_target_pairs={{0,4},{2,6},{4,0},{6,2},{8,12},{10,14},{12,8},{14,10},{16,20},{18,... | collective-permute-start | bytes 4423688 | tf_op jit(solution)/shard_map/ppermute | solution.py:118
  950.7 121.1 %collective-permute-start.72 = (bf16[576,2560]{1,0:T(8,128)(2,1)}, bf16[576,2560]{1,0:T(8,128)(2,1)}, u32[]{:S(2)}, u32[]{:S(2)}) collective-permute-start(bf16[576,2560]{1,0:T(8,128)(2,1)} %slice.741), channel_id=1, source_target_pairs={{0,2},{2,0},{4,6},{6,4},{8,10},{10,8},{12,14},{14,12},{16,18},{18,... | collective-permute-start | bytes 8847368 | tf_op jit(solution)/shard_map/ppermute | solution.py:118
  (307 other events, 6043.3 us)
Sparse Core Ops, SparseCore 0:
  876.9 13.3 reduce-scatter.1

commit v2 on v0

v2 whole, which is shorter than its diff:
```python
import jax
import jax.numpy as jnp
from jax import lax
from jax.experimental import pallas as pl
from jax.experimental.pallas import tpu as pltpu
from jax.sharding import PartitionSpec as P

HEADS = 16
HEAD_DIM = 72
TEXT = 120
PATCH = 256
LAYERS = 2
LANES = 128

EPSILON = 1e-06
NEG_FILL = -1e30
F32 = jnp.float32
BF16 = jnp.bfloat16


def normalize(stream):
    center = stream - jnp.mean(stream, axis=-1, keepdims=True)
    root = lax.rsqrt(jnp.mean(center * center, axis=-1, keepdims=True) + EPSILON)
    return (center * root, root)


def norm_back(grad, unit, root):
    return root * (
        grad
        - jnp.mean(grad, axis=-1, keepdims=True)
        - unit * jnp.mean(grad * unit, axis=-1, keepdims=True)
    )


def gelu_tanh(field):
    return jax.nn.gelu(field, approximate=True)


def dot(left, right, contract=((1,), (0,))):
    return lax.dot_general(left, right, (contract, ((), ())), preferred_element_type=F32)


def padded(width):
    return -(-width // LANES) * LANES


def widen(field):
    extra = padded(field.shape[-1]) - field.shape[-1]
    if extra == 0:
        return field
    return jnp.pad(field, [(0, 0)] * (field.ndim - 1) + [(0, extra)])


def head_window(head):
    first = head * HEAD_DIM
    low = first // LANES * LANES
    high = padded(first + HEAD_DIM)
    lane = lax.broadcasted_iota(jnp.int32, (1, high - low), 1) + low
    return low, high, (lane >= first) & (lane < first + HEAD_DIM)


def hide(scores, limit_ref, period):
    if limit_ref is not None:
        key = lax.broadcasted_iota(jnp.int32, scores.shape, 1)
        return jnp.where(key < limit_ref[0], scores, NEG_FILL)
    if period is not None:
        row = lax.broadcasted_iota(jnp.int32, scores.shape, 0)
        key = lax.broadcasted_iota(jnp.int32, scores.shape, 1)
        return jnp.where(lax.rem(row, period) == lax.rem(key, period), scores, NEG_FILL)
    return scores


def attend_kernel(heads, period, limited, *refs):
    limit_ref = refs[0] if limited else None
    q_ref, k_ref, v_ref, out_ref, log_ref, held = refs[1 if limited else 0 :]
    scaling = HEAD_DIM ** (-0.5)
    held[...] = jnp.zeros_like(held)
    rows = held.shape[0]
    lane = lax.broadcasted_iota(jnp.int32, (rows, LANES), 1)
    logs = jnp.zeros((rows, LANES), F32)

    def take(ref, low, high):
        field = ref[:, :, low:high]
        return field.reshape(field.shape[0] * field.shape[1], high - low)

    for head in range(heads):
        low, high, inside = head_window(head)
        keep = inside.astype(F32).astype(BF16)
        scores = dot(take(q_ref, low, high) * keep, take(k_ref, low, high), ((1,), (1,)))
        scores = hide(scores * scaling, limit_ref, period)
        top = jnp.max(scores, axis=1, keepdims=True)
        weights = jnp.exp(scores - top)
        total = jnp.sum(weights, axis=1, keepdims=True)
        weights = (weights * (1.0 / total)).astype(BF16)
        result = dot(weights, take(v_ref, low, high))
        held[:, low:high] = jnp.where(inside, result, held[:, low:high])
        logs = jnp.where(lane == head, top + jnp.log(total), logs)
    out_ref[...] = held[...].astype(BF16).reshape(out_ref.shape)
    log_ref[...] = logs.reshape(log_ref.shape)


def attend_back_kernel(heads, period, limited, packed, *refs):
    limit_ref = refs[0] if limited else None
    refs = refs[1 if limited else 0 :]
    q_ref, k_ref, v_ref, grad_ref, log_ref, *outs, q_held, k_held, v_held = refs
    scaling = HEAD_DIM ** (-0.5)
    for held in (q_held, k_held, v_held):
        held[...] = jnp.zeros_like(held)
    rows = q_held.shape[0]
    lane = lax.broadcasted_iota(jnp.int32, (rows, LANES), 1)

    def take(ref, low, high):
        field = ref[:, :, low:high]
        return field.reshape(field.shape[0] * field.shape[1], high - low)

    for head in range(heads):
        low, high, inside = head_window(head)
        keep = inside.astype(F32).astype(BF16)
        queries = take(q_ref, low, high)
        keys = take(k_ref, low, high)
        grads = take(grad_ref, low, high)
        scores = dot(queries * keep, keys, ((1,), (1,))) * scaling
        scores = hide(scores, limit_ref, period)
        logs = jnp.where(lane == head, take(log_ref, 0, LANES), 0.0)
        probs = jnp.exp(scores - jnp.sum(logs, axis=1, keepdims=True))
        grad_probs = dot(grads * keep, take(v_ref, low, high), ((1,), (1,)))
        mean = jnp.sum(probs * grad_probs, axis=1, keepdims=True)
        grad_scores = (probs * (grad_probs - mean)).astype(BF16)
        first = ((0,), (0,))
        for held, value in (
            (q_held, dot(grad_scores, keys) * scaling),
            (k_held, dot(grad_scores, queries, first) * scaling),
            (v_held, dot(probs.astype(BF16), grads, first)),
        ):
            held[:, low:high] = jnp.where(inside, value, held[:, low:high])
    width = q_held.shape[1]
    query_out = outs[0]
    others = outs[0] if packed else outs[1]
    start = width if packed else 0
    spot = query_out.shape[:2] + (width,)
    query_out[:, :, :width] = q_held[...].astype(BF16).reshape(spot)
    spot = others.shape[:2] + (width,)
    others[:, :, start : start + width] = k_held[...].astype(others.dtype).reshape(spot)
    others[:, :, start + width :] = v_held[...].astype(others.dtype).reshape(spot)


def kernel_cost(units, heads, rows, keys, products):
    area = units * heads * rows * keys
    return pl.CostEstimate(
        flops=products * 2 * area * 256,
        transcendentals=area,
        bytes_accessed=units * (4 * rows + 2 * keys) * padded(heads * HEAD_DIM) * 2,
    )


def attend_parts(query, keyval, unit, heads):
    wide = padded(heads * HEAD_DIM)
    frames, rows = query.shape[:2]
    units = (frames // unit[0]) * (rows // unit[1])
    across = frames // unit[0]

    def at(u, column):
        return (u % across, u // across, column)

    own = pl.BlockSpec((*unit, wide), lambda u, *_: at(u, 0))
    if keyval is None:
        arrays = [query] * 3
        rest = [
            pl.BlockSpec((*unit, wide), lambda u, *_: at(u, 1)),
            pl.BlockSpec((*unit, wide), lambda u, *_: at(u, 2)),
        ]
        keys = unit[0] * unit[1]
    else:
        arrays = [query, keyval, keyval]
        keys = keyval.shape[1]
        rest = [
            pl.BlockSpec((1, keys, wide), lambda u, *_: (0, 0, 0)),
            pl.BlockSpec((1, keys, wide), lambda u, *_: (0, 0, 1)),
        ]
    logs = pl.BlockSpec((*unit, LANES), lambda u, *_: at(u, 0))
    packed = pl.BlockSpec((*unit, 3 * wide), lambda u, *_: at(u, 0))
    return arrays, [own, *rest], own, logs, packed, units, keys, wide


def attend(query, keyval, unit, heads, period=None, limit=None):
    arrays, specs, own, logs, _, units, keys, wide = attend_parts(query, keyval, unit, heads)
    limited = limit is not None
    rows = unit[0] * unit[1]
    return pl.pallas_call(
        lambda *refs: attend_kernel(heads, period, limited, *refs),
        out_shape=(
            jax.ShapeDtypeStruct((*query.shape[:2], wide), BF16),
            jax.ShapeDtypeStruct((*query.shape[:2], LANES), F32),
        ),
        grid_spec=pltpu.PrefetchScalarGridSpec(
            num_scalar_prefetch=1 if limited else 0,
            grid=(units,),
            in_specs=specs,
            out_specs=(own, logs),
            scratch_shapes=[pltpu.VMEM((rows, wide), F32)],
        ),
        cost_estimate=kernel_cost(units, heads, rows, keys, 2),
        name="attend",
    )(*([limit] if limited else []), *arrays)


def attend_back(query, keyval, grad, log, unit, heads, period=None, limit=None):
    arrays, specs, own, logs, packed, units, keys, wide = attend_parts(query, keyval, unit, heads)
    rows = unit[0] * unit[1]
    if keyval is None:
        out_shape = (jax.ShapeDtypeStruct(query.shape, BF16),)
        out_specs = (packed,)
    else:
        assert units == 1
        out_shape = (
            jax.ShapeDtypeStruct(query.shape, BF16),
            jax.ShapeDtypeStruct(keyval.shape, F32),
        )
        out_specs = (own, pl.BlockSpec((1, keys, 2 * wide), lambda u, *_: (0, 0, 0)))
    limited = limit is not None
    return pl.pallas_call(
        lambda *refs: attend_back_kernel(heads, period, limited, keyval is None, *refs),
        out_shape=out_shape,
        grid_spec=pltpu.PrefetchScalarGridSpec(
            num_scalar_prefetch=1 if limited else 0,
            grid=(units,),
            in_specs=[*specs, own, logs],
            out_specs=out_specs,
            scratch_shapes=[
                pltpu.VMEM((rows, wide), F32),
                pltpu.VMEM((keys, wide), F32),
                pltpu.VMEM((keys, wide), F32),
            ],
        ),
        cost_estimate=kernel_cost(units, heads, rows, keys, 5),
        name="attend_back",
    )(*([limit] if limited else []), *arrays, grad, log)


class Layout:
    def __init__(self):
        self.dp = lax.axis_size("dp")
        self.bits = self.dp.bit_length() - 1
        self.tensor = lax.axis_size("tensor")

    def send(self, field, bit):
        return lax.ppermute(field, "dp", [(place, place ^ (1 << bit)) for place in range(self.dp)])

    def shift(self, field, step):
        size = self.tensor
        return lax.ppermute(field, "tensor", [(i, (i + step) % size) for i in range(size)])

    def gathering(self, rows):
        for bit in range(self.bits - 1, -1, -1):
            rows = jnp.concatenate([rows] + (yield [(rows, bit)]), axis=0)
        return rows

    def summing(self, make):
        came = yield [(make(1).astype(BF16), 0)]
        rows = make(0) + came[0].astype(F32)
        for bit in range(1, self.bits):
            rows = rows.astype(BF16)
            half = rows.shape[0] // 2
            came = yield [(rows[half:], bit)]
            rows = rows[:half].astype(F32) + came[0].astype(F32)
        return rows

    def own_features(self, block, spot):
        which = spot // block
        place = jnp.zeros_like(which) + lax.axis_index("dp")
        for bit in range(self.bits):
            place = place ^ ((which >> bit & 1) << (self.bits - 1 - bit))
        return place * block + spot % block


def after(field, *others):
    return lax.optimization_barrier((field, *others))[0]


class Line:
    def __init__(self, send, patience):
        self.send = send
        self.patience = patience
        self.count = 0
        self.waiting = []
        self.moving = {}
        self.results = {}

    def add(self, name, begin, *fields):
        self.waiting.append((name, begin, fields))

    def resume(self, name, steps, came):
        try:
            return [(name, steps, steps.send(came))]
        except StopIteration as stop:
            self.results[name] = stop.value
            return []

    def depart(self, leaving):
        for name, steps, hops in leaving:
            due = self.count + 1 + self.patience.get(hops[0][1], 0)
            self.moving[name] = (steps, [self.send(*hop) for hop in hops], due)

    def step(self, field=None, exchange=None, starts=1):
        self.count += 1
        due = [name for name, entry in self.moving.items() if entry[2] <= self.count]
        begun = [self.waiting.pop(0) for _ in range(min(starts, len(self.waiting)))]
        flat = [block for name in due for block in self.moving[name][1]]
        flat += [block for *_, fields in begun for block in fields]
        if field is None:
            flat = list(lax.optimization_barrier(flat)) if flat else flat
        else:
            field, *flat = lax.optimization_barrier((field, *flat))
            came = exchange(field)
        leaving = []
        for name in due:
            steps, blocks, _ = self.moving.pop(name)
            leaving += self.resume(name, steps, [flat.pop(0) for _ in blocks])
        for name, begin, fields in begun:
            leaving += self.resume(name, begin(*[flat.pop(0) for _ in fields]), None)
        if field is not None:
            came = after(came, *[hop[0] for *_, hops in leaving for hop in hops])
        self.depart(leaving)
        return came if field is not None else None

    def need(self, name):
        while name not in self.results:
            steps, blocks, _ = self.moving.pop(name)
            self.depart(self.resume(name, steps, blocks))
        return self.results[name]

    def finish(self):
        while self.moving or self.waiting:
            leaving = []
            for name in list(self.moving):
                steps, blocks, _ = self.moving.pop(name)
                leaving += self.resume(name, steps, blocks)
            while self.waiting:
                name, begin, fields = self.waiting.pop(0)
                leaving += self.resume(name, begin(*fields), None)
            self.depart(leaving)


def per_device(
    tokens,
    text,
    lengths,
    modulation,
    self_qkv,
    self_out,
    cross_query,
    cross_keyvalue,
    cross_out,
    mlp_in,
    mlp_out,
    cotangent,
):
    lay = Layout()
    places = lay.tensor
    rows_here = tokens.shape[1]
    total_rows = rows_here * places
    heads_here = HEADS // places
    columns = heads_here * HEAD_DIM
    wide = padded(columns)
    width = tokens.shape[2]
    block = self_qkv.shape[1]
    me_tensor = lax.axis_index("tensor")
    share = width // places
    half = width // 2
    rows_of = ((0,), (0,))
    over_columns = ((1,), (1,))

    wanted = lay.own_features(block, lax.broadcasted_iota(jnp.int32, (1, width), 1))
    order = (lax.broadcasted_iota(jnp.int32, (width, width), 0) == wanted).astype(BF16)

    def share_order(step):
        first = (me_tensor - step) % places * share
        rows = lax.broadcasted_iota(jnp.int32, (share, width), 0) + first
        return (rows == wanted).astype(BF16)

    shares = [share_order(step) for step in range(places)]

    def exact(left, right, contract):
        return lax.dot_general(
            left,
            right.astype(F32),
            (contract, ((), ())),
            precision=lax.Precision.HIGHEST,
            preferred_element_type=F32,
        )

    def exchange(field, shift):
        starts = starts_at.get(line.count + 1, 0) if forward else 1
        return line.step(field, lambda f: lay.shift(f, shift), starts)

    def spread(field, timed=True):
        came = []
        for k in range(1, places):
            if timed and k == 1:
                came.append(exchange(field, 1))
            else:
                came.append(lay.shift(field, k))
        return [field, jnp.concatenate(came, axis=0) if len(came) > 1 else came[0]]

    def collect(parts):
        own, others = parts
        total = own
        for k in range(1, places):
            leaving = others[(k - 1) * rows_here : k * rows_here].astype(BF16)
            came = exchange(leaving, -1) if k == 1 else lay.shift(leaving, -k)
            total = total + came.astype(F32)
        return total

    def each(parts, weight, contract=((1,), (0,))):
        return [dot(part, weight, contract) for part in parts]

    def low(parts):
        return [part.astype(BF16) for part in parts]

    def join(parts):
        return jnp.concatenate(parts, axis=0)

    def split(field):
        return [field[:rows_here], field[rows_here:]]

    def pack(layer):
        qkv = self_qkv[layer]
        keyval = cross_keyvalue[layer]
        return {
            "qkv": jnp.concatenate([widen(qkv[:, i]) for i in range(3)], axis=1),
            "proj": widen(self_out[layer].T),
            "query": widen(cross_query[layer]),
            "keyval": jnp.concatenate([widen(keyval[:, i]) for i in range(2)], axis=1),
            "cproj": widen(cross_out[layer].T),
            "in": mlp_in[layer],
            "out": mlp_out[layer].T,
        }

    packs = [pack(layer) for layer in range(LAYERS)]
    groups = [
        (layer, names)
        for layer in range(LAYERS)
        for names in (("qkv", "proj"), ("query", "keyval", "cproj"), ("in",), ("out",))
    ]
    line = Line(lay.send, {1: 1})
    place_of = {}
    for index, (layer, names) in enumerate(groups):
        parts = [packs[layer][name] for name in names]
        piece = jnp.concatenate(parts, axis=1) if len(parts) > 1 else parts[0]
        line.add(index, lay.gathering, piece)
        start = 0
        for name, part in zip(names, parts):
            place_of[layer, name] = (index, start, start + part.shape[1])
            start += part.shape[1]
    starts_at = {6: 1, 8: 1, 9: 1, 10: 1, 12: 1}

    def weight(layer, name):
        index, start, stop = place_of[layer, name]
        return line.need(index)[:, start:stop]

    for starts in (1, 0, 1, 0, 1):
        line.step(starts=starts)

    text_rows = jnp.pad(text[0], ((0, LANES - TEXT), (0, 0)))
    text_full = sum(dot(part, at) for part, at in zip([text_rows] + [lay.shift(text_rows, k) for k in range(1, places)], shares))
    text_full = text_full.astype(BF16)
    table = exact(modulation[0].reshape(LAYERS * 6, width), order, ((1,), (0,)))
    table = table.reshape(LAYERS, 6, width)

    def frames(field):
        return field.reshape(-1, rows_here, field.shape[-1])

    def flat(field):
        return field.reshape(-1, field.shape[-1])

    def attend_self(layer, qkv):
        if layer % 2 == 0:
            found = [attend(frames(part), None, (1, rows_here), heads_here) for part in qkv]
            return [flat(one) for one, _ in found], [log for _, log in found]
        period = rows_here // places
        result, log = attend(frames(join(qkv)), None, (places, period), heads_here, period)
        return split(flat(result)), log

    def attend_self_back(layer, qkv, grad, log):
        if layer % 2 == 0:
            return [
                flat(attend_back(frames(a), None, frames(b), c, (1, rows_here), heads_here)[0])
                for a, b, c in zip(qkv, grad, log)
            ]
        period = rows_here // places
        (result,) = attend_back(
            frames(join(qkv)), None, frames(join(grad)), log, (places, period), heads_here, period
        )
        return split(flat(result))

    def attend_cross(queries, keyval):
        found = [
            attend(part[None], keyval[None], (1, part.shape[0]), heads_here, limit=lengths)
            for part in queries
        ]
        return [one[0] for one, _ in found], [log for _, log in found]

    def attend_cross_back(queries, keyval, grad, log):
        found = [
            attend_back(
                a[None], keyval[None], b[None], c, (1, a.shape[0]), heads_here, limit=lengths
            )
            for a, b, c in zip(queries, grad, log)
        ]
        return [one[0] for one, _ in found], sum(two[0] for _, two in found).astype(BF16)

    stream = dot(tokens[0], order)
    memory = []
    forward = True
    for layer in range(LAYERS):
        adaln = table[layer]
        save = {}
        save["unit_one"], save["root_one"] = normalize(stream)
        normed = spread(
            (save["unit_one"] * (1.0 + adaln[1]) + adaln[0]).astype(BF16), layer > 0
        )
        save["normed"] = join(normed)
        save["qkv"] = qkv = low(each(normed, weight(layer, "qkv")))
        attended, save["log_self"] = attend_self(layer, qkv)
        save["attended"] = join(attended)
        save["branch"] = branch = collect(each(attended, weight(layer, "proj"), over_columns))
        stream = stream + adaln[2] * branch
        crossing = spread(stream.astype(BF16))
        save["crossing"] = join(crossing)
        save["queries"] = queries = low(each(crossing, weight(layer, "query")))
        save["keyval"] = keyval = dot(text_full, weight(layer, "keyval")).astype(BF16)
        crossed, save["log_cross"] = attend_cross(queries, keyval)
        save["crossed"] = join(crossed)
        stream = stream + collect(each(crossed, weight(layer, "cproj"), over_columns))
        save["unit_two"], save["root_two"] = normalize(stream)
        inner = spread((save["unit_two"] * (1.0 + adaln[4]) + adaln[3]).astype(BF16))
        save["inner"] = join(inner)
        save["pre"] = pre = each(inner, weight(layer, "in"))
        hidden = low([gelu_tanh(part) for part in pre])
        save["hidden"] = join(hidden)
        save["mlp_branch"] = mlp_branch = collect(each(hidden, weight(layer, "out"), over_columns))
        stream = stream + adaln[5] * mlp_branch
        memory.append(save)
    output = dot(stream.astype(BF16), order, over_columns).astype(BF16)

    def product(*pairs):
        def make(which):
            made = [
                dot(left[:, which * half : (which + 1) * half], right, rows_of)
                for left, right in pairs
            ]
            return made[0] if len(made) == 1 else jnp.concatenate(made, axis=1)
        return lambda: lay.summing(make)

    weights = [
        {name: weight(layer, name) for spot, name in place_of if spot == layer}
        for layer in range(LAYERS)
    ]
    line = Line(lay.send, {1: 1})
    forward = False
    grad_stream = dot(cotangent[0], order)
    grad_text = jnp.zeros((LANES, width), F32)
    table_rows = [None] * LAYERS
    for layer in reversed(range(LAYERS)):
        adaln = table[layer]
        kind = weights[layer]
        save = memory[layer]

        grad_gate_two = jnp.sum(grad_stream * save["mlp_branch"], axis=0)
        grad_mlp = spread((adaln[5] * grad_stream).astype(BF16))
        line.add((layer, "out"), product((join(grad_mlp), save["hidden"])))
        grad_pre = [
            jax.vjp(gelu_tanh, pre)[1](dot(part, kind["out"]))[0].astype(BF16)
            for pre, part in zip(save["pre"], grad_mlp)
        ]
        line.add((layer, "in"), product((save["inner"], join(grad_pre))))
        grad_inner = collect(each(grad_pre, kind["in"], over_columns))
        grad_shift_two = jnp.sum(grad_inner, axis=0)
        grad_scale_two = jnp.sum(grad_inner * save["unit_two"], axis=0)
        grad_stream = grad_stream + norm_back(
            grad_inner * (1.0 + adaln[4]), save["unit_two"], save["root_two"]
        )

        grad_crossed = spread(grad_stream.astype(BF16))
        grad_catt = low(each(grad_crossed, kind["cproj"]))
        grad_cq, grad_keyval = attend_cross_back(
            save["queries"], save["keyval"], grad_catt, save["log_cross"]
        )
        line.add(
            (layer, "cross"),
            product(
                (save["crossing"], join(grad_cq)),
                (text_full, grad_keyval),
                (join(grad_crossed), save["crossed"]),
            ),
        )
        grad_stream = grad_stream + collect(each(grad_cq, kind["query"], over_columns))
        grad_text = grad_text + dot(grad_keyval, kind["keyval"], over_columns)

        grad_gate_one = jnp.sum(grad_stream * save["branch"], axis=0)
        grad_branch = spread((adaln[2] * grad_stream).astype(BF16))
        line.add((layer, "proj"), product((join(grad_branch), save["attended"])))
        grad_att = low(each(grad_branch, kind["proj"]))
        grad_qkv = attend_self_back(layer, save["qkv"], grad_att, save["log_self"])
        line.add(
            (layer, "self"),
            product((save["normed"], join(grad_qkv))),
        )
        grad_normed = collect(each(grad_qkv, kind["qkv"], over_columns))
        grad_shift_one = jnp.sum(grad_normed, axis=0)
        grad_scale_one = jnp.sum(grad_normed * save["unit_one"], axis=0)
        grad_stream = grad_stream + norm_back(
            grad_normed * (1.0 + adaln[1]), save["unit_one"], save["root_one"]
        )
        table_rows[layer] = jnp.stack(
            [
                grad_shift_one,
                grad_scale_one,
                grad_gate_one,
                grad_shift_two,
                grad_scale_two,
                grad_gate_two,
            ]
        )
    line.finish()

    def apart(field, first, count):
        return jnp.stack(
            [field[:, i * wide : i * wide + columns] for i in range(first, first + count)], axis=1
        )

    text_parts = [exact(grad_text[:TEXT], at, over_columns) for at in shares]
    text_grad = text_parts[0]
    for k in range(1, places):
        text_grad = text_grad + lay.shift(text_parts[k], -k)
    table_grad = exact(jnp.stack(table_rows).reshape(LAYERS * 6, width), order, over_columns)
    if places == 2:
        table_grad = table_grad + lay.shift(table_grad, 1)
    else:
        table_grad = lax.psum(table_grad, "tensor")
    selfs = [line.results[layer, "self"] for layer in range(LAYERS)]
    crosses = [line.results[layer, "cross"] for layer in range(LAYERS)]
    return (
        output[None],
        exact(grad_stream, order, over_columns)[None],
        text_grad[None],
        table_grad.reshape(LAYERS, 6, width)[None],
        jnp.stack([apart(one, 0, 3) for one in selfs]),
        jnp.stack([line.results[layer, "proj"][:, :columns].T for layer in range(LAYERS)]),
        jnp.stack([one[:, :columns] for one in crosses]),
        jnp.stack([apart(one, 1, 2) for one in crosses]),
        jnp.stack([one[:, 3 * wide : 3 * wide + columns].T for one in crosses]),
        jnp.stack([line.results[layer, "in"] for layer in range(LAYERS)]),
        jnp.stack([line.results[layer, "out"].T for layer in range(LAYERS)]),
    )


def solution(mesh):
    return jax.shard_map(
        per_device,
        mesh=mesh,
        in_specs=(
            P("dp", "tensor", None),
            P("dp", None, "tensor"),
            P("dp"),
            P("dp", None, None, None),
            P(None, "dp", None, "tensor"),
            P(None, "tensor", "dp"),
            P(None, "dp", "tensor"),
            P(None, "dp", None, "tensor"),
            P(None, "tensor", "dp"),
            P(None, "dp", "tensor"),
            P(None, "tensor", "dp"),
            P("dp", "tensor", None),
        ),
        out_specs=(
            P("dp", "tensor", None),
            P("dp", "tensor", None),
            P("dp", None, "tensor"),
            P("dp", None, None, None),
            P(None, "dp", None, "tensor"),
            P(None, "tensor", "dp"),
            P(None, "dp", "tensor"),
            P(None, "dp", None, "tensor"),
            P(None, "tensor", "dp"),
            P(None, "dp", "tensor"),
            P(None, "tensor", "dp"),
        ),
        check_vma=False,
    )
```

time: 2970 us -> 921 us (0.31)
  waiting for transfers between devices: 2420 us -> 337 us
  starting transfers between devices: 4.49 us -> 105 us
  Pallas kernels: 0 us -> 66.2 us
  local copies, waits for them, and re-layouts: 160 us -> 106 us
  matrix products: 273 us -> 237 us
    reduce_scatter x19 -> x0, waiting for transfers between devices: 1110 us -> none  [the longest x12 392 us: collect(): lax.psum_scatter(project(field), 'tensor', scatter_dimension=0, tiled=True)]
    all_gather x26 -> x0, waiting for transfers between devices: 809 us -> none  [the longest x12 249 us: spread(): return lax.all_gather(field, 'tensor', axis=0, tiled=True)]
    unnamed x59 -> x0, waiting for transfers between devices: 500 us -> none
    ppermute x0 -> x99, waiting for transfers between devices: none -> 337 us  [the longest x72 234 us: send(): lax.ppermute(field, 'dp', [(place, place ^ 1 << bit) for place in range(s...]
    ppermute x0 -> x99, starting transfers between devices: none -> 105 us  [the longest x72 77.7 us: send(): lax.ppermute(field, 'dp', [(place, place ^ 1 << bit) for place in range(s...]
    pallas_call x0 -> x14, Pallas kernels: none -> 66.2 us  [the longest x7 41.4 us: attend_back(): pl.pallas_call(lambda *refs: attend_back_kernel(heads, period, limited, k...]
    dot_general x66 -> x90, matrix products: 273 us -> 237 us  [the longest x85 223 us: dot(): lax.dot_general(left, right, (contract, ((), ())), preferred_element_type...]
    another operation x21 -> x6, local copies, waits for them, and re-layouts: 35.9 us -> 0.93 us  [the longest x2 0.83 us: per_device(): jnp.stack([one[:, 3 * wide:3 * wide + columns].T for one in crosses])]
  transfers between devices with their start and end apart: 52 -> 99, of which waited for: 49 -> 43; matrix products, arithmetic and copies ran while one was open for 10% -> 39% of each run, Pallas kernels for 0% -> 7%
where the time goes in v2:
time: 921 us; the launch traced here: 914 us
  waiting for transfers between devices  337 us (37%)
  matrix products  237 us (26%)
  local copies, waits for them, and re-layouts  106 us (12%)
  starting transfers between devices  105 us (11%)
  Pallas kernels  66.2 us (7%)
  other arithmetic  59.6 us (6%)
    ppermute x72, waiting for transfers between devices, send(): lax.ppermute(field, 'dp', [(place, place ^ 1 << bit) for place in range(s...  234 us
    dot_general x85, matrix products, dot(): lax.dot_general(left, right, (contract, ((), ())), preferred_element_type...  223 us
    ppermute x27, waiting for transfers between devices, shift(): lax.ppermute(field, 'tensor', [(i, (i + step) % size) for i in range(size)])  102 us
    ppermute x72, starting transfers between devices, send(): lax.ppermute(field, 'dp', [(place, place ^ 1 << bit) for place in range(s...  77.7 us
    unnamed x502, local copies, waits for them, and re-layouts  60.1 us
    pallas_call x7, Pallas kernels, attend_back(): pl.pallas_call(lambda *refs: attend_back_kernel(heads, period, limited, k...  41.4 us
    ppermute x27, starting transfers between devices, shift(): lax.ppermute(field, 'tensor', [(i, (i + step) % size) for i in range(size)])  27.2 us
    pallas_call x7, Pallas kernels, attend(): pl.pallas_call(lambda *refs: attend_kernel(heads, period, limited, *refs)...  24.8 us
  transfers between devices with their start and end apart: 99, of which 43 were waited for; matrix products, arithmetic and copies ran while one was open for 39% of the time, Pallas kernels for 7%

profile of v2, /device:TPU:0, one launch (start us, length us, event | category | flops | bytes accessed | tf_op | source)
XLA Modules:
  0.0 914.4 jit_solution(14011608384001829390)
XLA Ops:
  16.6 6.9 collective-permute-done
  25.2 16.1 %collective-permute-done.1 = bf16[144,2560]{1,0:T(8,128)(2,1)S(1)} collective-permute-done((bf16[144,2560]{1,0:T(8,128)(2,1)S(1)}, bf16[144,2560]{1,0:T(8,128)(2,1)S(1)}, u32[]{:S(2)}, u32[]{:S(2)}) %collective-permute-start.1) | collective-permute-done | bytes 737312 | tf_op jit(solution)/shard_map/ppermute | solution.py:247
  47.9 12.6 %collective-permute-done.3 = bf16[72,2560]{1,0:T(8,128)(2,1)S(1)} collective-permute-done((bf16[72,2560]{1,0:T(8,128)(2,1)S(1)}, bf16[72,2560]{1,0:T(8,128)(2,1)S(1)}, u32[]{:S(2)}, u32[]{:S(2)}) %collective-permute-start.3) | collective-permute-done | bytes 368672 | tf_op jit(solution)/shard_map/ppermute | solution.py:247
  64.8 14.4 %collective-permute-done.4 = bf16[144,2560]{1,0:T(8,128)(2,1)S(1)} collective-permute-done((bf16[144,2560]{1,0:T(8,128)(2,1)}, bf16[144,2560]{1,0:T(8,128)(2,1)S(1)}, u32[]{:S(2)}, u32[]{:S(2)}) %collective-permute-start.4) | collective-permute-done | bytes 737312 | tf_op jit(solution)/shard_map/ppermute | solution.py:247
  150.8 7.7 collective-permute-done.14
  193.1 14.8 %collective-permute-done.20 = bf16[288,2304]{1,0:T(8,128)(2,1)} collective-permute-done((bf16[288,2304]{1,0:T(8,128)(2,1)}, bf16[288,2304]{1,0:T(8,128)(2,1)}, u32[]{:S(2)}, u32[]{:S(2)}) %collective-permute-start.20) | collective-permute-done | bytes 1327136 | tf_op jit(solution)/shard_map/ppermute | solution.py:247
  217.2 8.6 collective-permute-done.22
  248.5 24.5 %collective-permute-done.26 = bf16[288,2560]{1,0:T(8,128)(2,1)S(1)} collective-permute-done((bf16[288,2560]{1,0:T(8,128)(2,1)S(1)}, bf16[288,2560]{1,0:T(8,128)(2,1)S(1)}, u32[]{:S(2)}, u32[]{:S(2)}) %collective-permute-start.26) | collective-permute-done | bytes 1474592 | tf_op jit(solution)/shard_map/ppermute | solution.py:247
  283.9 11.2 %collective-permute-done.28 = bf16[144,2560]{1,0:T(8,128)(2,1)S(1)} collective-permute-done((bf16[144,2560]{1,0:T(8,128)(2,1)S(1)}, bf16[144,2560]{1,0:T(8,128)(2,1)S(1)}, u32[]{:S(2)}, u32[]{:S(2)}) %collective-permute-start.28) | collective-permute-done | bytes 737312 | tf_op jit(solution)/shard_map/ppermute | solution.py:247
  300.1 10.1 %collective-permute-done.30 = bf16[256,1152]{1,0:T(8,128)(2,1)S(1)} collective-permute-done((bf16[256,1152]{1,0:T(8,128)(2,1)S(1)}, bf16[256,1152]{1,0:T(8,128)(2,1)S(1)}, u32[]{:S(2)}, u32[]{:S(2)}) %collective-permute-start.30) | collective-permute-done | bytes 589856 | tf_op jit(solution)/shard_map/ppermute | solution.py:251
  327.4 10.8 %collective-permute-done.32 = bf16[256,1152]{1,0:T(8,128)(2,1)S(1)} collective-permute-done((bf16[256,1152]{1,0:T(8,128)(2,1)S(1)}, bf16[256,1152]{1,0:T(8,128)(2,1)S(1)}, u32[]{:S(2)}, u32[]{:S(2)}) %collective-permute-start.32) | collective-permute-done | bytes 589856 | tf_op jit(solution)/shard_map/ppermute | solution.py:251
  348.7 10.6 %collective-permute-done.36 = bf16[256,1152]{1,0:T(8,128)(2,1)S(1)} collective-permute-done((bf16[256,1152]{1,0:T(8,128)(2,1)S(1)}, bf16[256,1152]{1,0:T(8,128)(2,1)S(1)}, u32[]{:S(2)}, u32[]{:S(2)}) %collective-permute-start.36) | collective-permute-done | bytes 589856 | tf_op jit(solution)/shard_map/ppermute | solution.py:251
  383.9 23.0 %collective-permute-done.41 = bf16[288,2304]{1,0:T(8,128)(2,1)S(1)} collective-permute-done((bf16[288,2304]{1,0:T(8,128)(2,1)S(1)}, bf16[288,2304]{1,0:T(8,128)(2,1)S(1)}, u32[]{:S(2)}, u32[]{:S(2)}) %collective-permute-start.41) | collective-permute-done | bytes 1327136 | tf_op jit(solution)/shard_map/ppermute | solution.py:247
  424.5 10.3 %collective-permute-done.43 = bf16[256,1152]{1,0:T(8,128)(2,1)S(1)} collective-permute-done((bf16[256,1152]{1,0:T(8,128)(2,1)S(1)}, bf16[256,1152]{1,0:T(8,128)(2,1)S(1)}, u32[]{:S(2)}, u32[]{:S(2)}) %collective-permute-start.43) | collective-permute-done | bytes 589856 | tf_op jit(solution)/shard_map/ppermute | solution.py:251
  468.3 11.3 %collective-permute-done.44 = bf16[256,1152]{1,0:T(8,128)(2,1)S(1)} collective-permute-done((bf16[256,1152]{1,0:T(8,128)(2,1)S(1)}, bf16[256,1152]{1,0:T(8,128)(2,1)S(1)}, u32[]{:S(2)}, u32[]{:S(2)}) %collective-permute-start.44) | collective-permute-done | bytes 589856 | tf_op jit(solution)/shard_map/ppermute | solution.py:251
  540.2 13.8 %collective-permute-done.51 = bf16[288,2304]{1,0:T(8,128)(2,1)S(1)} collective-permute-done((bf16[288,2304]{1,0:T(8,128)(2,1)S(1)}, bf16[288,2304]{1,0:T(8,128)(2,1)S(1)}, u32[]{:S(2)}, u32[]{:S(2)}) %collective-permute-start.51) | collective-permute-done | bytes 1327136 | tf_op jit(solution)/shard_map/ppermute | solution.py:247
  569.6 9.3 %attend_back.9 = bf16[2,256,1920]{2,1,0:T(8,128)(2,1)} custom-call(bf16[2,256,1920]{2,1,0:T(8,128)(2,1)} %bitcast.323, bf16[2,256,1920]{2,1,0:T(8,128)(2,1)} %bitcast.324, bf16[2,256,1920]{2,1,0:T(8,128)(2,1)} %bitcast.325, bf16[2,256,640]{2,1,0:T(8,128)(2,1)} %bitcast.332, f32[2,256,128]{2,1,0:T(8,128)} %get-tuple-element.196.refs_4_), custom_call_target="tpu_custom_call" | custom-call | flops 2684354560 | bytes 3932160 | tf_op jit(solution)/shard_map/attend_back/pallas_call | solution.py:221
  595.2 7.9 collective-permute-done.56
  796.0 15.1 %collective-permute-done.98 = bf16[72,2304]{1,0:T(8,128)(2,1)S(1)} collective-permute-done((bf16[72,2304]{1,0:T(8,128)(2,1)S(1)}, bf16[72,2304]{1,0:T(8,128)(2,1)S(1)}, u32[]{:S(2)}, u32[]{:S(2)}) %collective-permute-start.98) | collective-permute-done | bytes 331808 | tf_op jit(solution)/shard_map/ppermute | solution.py:247
  839.1 7.9 collective-permute-done.97
  847.1 13.6 %collective-permute-done.91 = bf16[144,640]{1,0:T(8,128)(2,1)S(1)} collective-permute-done((bf16[144,640]{1,0:T(8,128)(2,1)S(1)}, bf16[144,640]{1,0:T(8,128)(2,1)S(1)}, u32[]{:S(2)}, u32[]{:S(2)}) %collective-permute-start.91) | collective-permute-done | bytes 184352 | tf_op jit(solution)/shard_map/ppermute | solution.py:247
  870.5 17.9 %collective-permute-done.86 = bf16[288,1920]{1,0:T(8,128)(2,1)S(1)} collective-permute-done((bf16[288,1920]{1,0:T(8,128)(2,1)S(1)}, bf16[288,1920]{1,0:T(8,128)(2,1)S(1)}, u32[]{:S(2)}, u32[]{:S(2)}) %collective-permute-start.86) | collective-permute-done | bytes 1105952 | tf_op jit(solution)/shard_map/ppermute | solution.py:247
  891.4 10.9 %collective-permute-done.87 = bf16[144,1920]{1,0:T(8,128)(2,1)S(1)} collective-permute-done((bf16[144,1920]{1,0:T(8,128)(2,1)S(1)}, bf16[144,1920]{1,0:T(8,128)(2,1)S(1)}, u32[]{:S(2)}, u32[]{:S(2)}) %collective-permute-start.87) | collective-permute-done | bytes 552992 | tf_op jit(solution)/shard_map/ppermute | solution.py:247
  905.4 7.5 collective-permute-done.88
  (957 shorter events, 612.7 us)
Async XLA Ops:
  13.4 80.2 %collective-permute-start.6 = (bf16[256,1152]{1,0:T(8,128)(2,1)}, bf16[256,1152]{1,0:T(8,128)(2,1)}, u32[]{:S(2)}, u32[]{:S(2)}) collective-permute-start(bf16[256,1152]{1,0:T(8,128)(2,1)} %add_convert_fusion.26), channel_id=1, source_target_pairs={{0,1},{1,0},{2,3},{3,2},{4,5},{5,4},{6,7},{7,6},{8,9},{9,8},{10,11... | collective-permute-start | bytes 1769480 | tf_op jit(solution)/shard_map/ppermute | solution.py:251
  15.7 123.0 %collective-permute-start.13 = (bf16[128,576]{0,1:T(8,128)(2,1)}, bf16[128,576]{0,1:T(8,128)(2,1)}, u32[]{:S(2)}, u32[]{:S(2)}) collective-permute-start(bf16[128,576]{0,1:T(8,128)(2,1)} %pad.61), channel_id=1, source_target_pairs={{0,1},{1,0},{2,3},{3,2},{4,5},{5,4},{6,7},{7,6},{8,9},{9,8},{10,11... | collective-permute-start | bytes 442376 | tf_op jit(solution)/shard_map/ppermute | solution.py:251
  148.2 41.2 %collective-permute-start.17 = (bf16[288,2304]{1,0:T(8,128)(2,1)}, bf16[288,2304]{1,0:T(8,128)(2,1)}, u32[]{:S(2)}, u32[]{:S(2)}) collective-permute-start(bf16[288,2304]{1,0:T(8,128)(2,1)} %get-tuple-element.341), channel_id=1, source_target_pairs={{0,4},{2,6},{4,0},{6,2},{8,12},{10,14},{12,8},{14,10},{16,20},{18,... | collective-permute-start | bytes 3981320 | tf_op jit(solution)/shard_map/ppermute | solution.py:247
  193.1 35.4 %collective-permute-start.19 = (bf16[576,2304]{1,0:T(8,128)(2,1)}, bf16[576,2304]{1,0:T(8,128)(2,1)S(1)}, u32[]{:S(2)}, u32[]{:S(2)}) collective-permute-start(bf16[576,2304]{1,0:T(8,128)(2,1)} %get-tuple-element.310), channel_id=1, source_target_pairs={{0,2},{2,0},{4,6},{6,4},{8,10},{10,8},{12,14},{14,12},{16,18},{18,... | collective-permute-start | bytes 7962632 | tf_op jit(solution)/shard_map/ppermute | solution.py:247
  245.5 38.3 %collective-permute-start.29 = (bf16[72,2304]{1,0:T(8,128)(2,1)S(1)}, bf16[72,2304]{1,0:T(8,128)(2,1)S(1)}, u32[]{:S(2)}, u32[]{:S(2)}) collective-permute-start(bf16[72,2304]{1,0:T(8,128)(2,1)S(1)} %copy-done.66), channel_id=1, source_target_pairs={{0,16},{2,18},{4,20},{6,22},{8,24},{10,26},{12,28},{14,30},{16,0},... | collective-permute-start | bytes 995336 | tf_op jit(solution)/shard_map/ppermute | solution.py:247
  274.2 36.1 %collective-permute-start.27 = (bf16[576,2560]{1,0:T(8,128)(2,1)S(1)}, bf16[576,2560]{1,0:T(8,128)(2,1)S(1)}, u32[]{:S(2)}, u32[]{:S(2)}) collective-permute-start(bf16[576,2560]{1,0:T(8,128)(2,1)S(1)} %pad_maximum_fusion.2), channel_id=1, source_target_pairs={{0,2},{2,0},{4,6},{6,4},{8,10},{10,8},{12,14},{14,12},{16,18},{18,... | collective-permute-start | bytes 8847368 | tf_op jit(solution)/shard_map/ppermute | solution.py:247
  299.6 41.8 %collective-permute-start.33 = (bf16[288,2560]{1,0:T(8,128)(2,1)}, bf16[288,2560]{1,0:T(8,128)(2,1)}, u32[]{:S(2)}, u32[]{:S(2)}) collective-permute-start(bf16[288,2560]{1,0:T(8,128)(2,1)} %get-tuple-element.325), channel_id=1, source_target_pairs={{0,4},{2,6},{4,0},{6,2},{8,12},{10,14},{12,8},{14,10},{16,20},{18,... | collective-permute-start | bytes 4423688 | tf_op jit(solution)/shard_map/ppermute | solution.py:247
  379.6 39.4 %collective-permute-start.40 = (bf16[576,2304]{1,0:T(8,128)(2,1)}, bf16[576,2304]{1,0:T(8,128)(2,1)}, u32[]{:S(2)}, u32[]{:S(2)}) collective-permute-start(bf16[576,2304]{1,0:T(8,128)(2,1)} %get-tuple-element.308), channel_id=1, source_target_pairs={{0,2},{2,0},{4,6},{6,4},{8,10},{10,8},{12,14},{14,12},{16,18},{18,... | collective-permute-start | bytes 7962632 | tf_op jit(solution)/shard_map/ppermute | solution.py:247
  466.7 56.3 %collective-permute-start.49 = (bf16[576,2304]{1,0:T(8,128)(2,1)}, bf16[576,2304]{1,0:T(8,128)(2,1)}, u32[]{:S(2)}, u32[]{:S(2)}) collective-permute-start(bf16[576,2304]{1,0:T(8,128)(2,1)} %convolution_convert_fusion.2), channel_id=1, source_target_pairs={{0,2},{2,0},{4,6},{6,4},{8,10},{10,8},{12,14},{14,12},{16,18},{18,... | collective-permute-start | bytes 7962632 | tf_op jit(solution)/shard_map/ppermute | solution.py:247
  516.6 37.4 %collective-permute-start.52 = (bf16[576,2560]{1,0:T(8,128)(2,1)S(1)}, bf16[576,2560]{1,0:T(8,128)(2,1)S(1)}, u32[]{:S(2)}, u32[]{:S(2)}) collective-permute-start(bf16[576,2560]{1,0:T(8,128)(2,1)S(1)} %pad_maximum_fusion.3), channel_id=1, source_target_pairs={{0,2},{2,0},{4,6},{6,4},{8,10},{10,8},{12,14},{14,12},{16,18},{18,... | collective-permute-start | bytes 8847368 | tf_op jit(solution)/shard_map/ppermute | solution.py:247
  532.5 55.3 %collective-permute-start.54 = (bf16[288,2304]{1,0:T(8,128)(2,1)}, bf16[288,2304]{1,0:T(8,128)(2,1)}, u32[]{:S(2)}, u32[]{:S(2)}) collective-permute-start(bf16[288,2304]{1,0:T(8,128)(2,1)} %slice.706), channel_id=1, source_target_pairs={{0,4},{2,6},{4,0},{6,2},{8,12},{10,14},{12,8},{14,10},{16,20},{18,... | collective-permute-start | bytes 3981320 | tf_op jit(solution)/shard_map/ppermute | solution.py:247
  559.9 60.6 %collective-permute-start.57 = (bf16[288,2560]{1,0:T(8,128)(2,1)}, bf16[288,2560]{1,0:T(8,128)(2,1)}, u32[]{:S(2)}, u32[]{:S(2)}) collective-permute-start(bf16[288,2560]{1,0:T(8,128)(2,1)} %slice.715), channel_id=1, source_target_pairs={{0,4},{2,6},{4,0},{6,2},{8,12},{10,14},{12,8},{14,10},{16,20},{18,... | collective-permute-start | bytes 4423688 | tf_op jit(solution)/shard_map/ppermute | solution.py:247
  568.7 51.7 %collective-permute-start.60 = (bf16[576,640]{1,0:T(8,128)(2,1)}, bf16[576,640]{1,0:T(8,128)(2,1)}, u32[]{:S(2)}, u32[]{:S(2)}) collective-permute-start(bf16[576,640]{1,0:T(8,128)(2,1)} %convolution_convert_fusion.21), channel_id=1, source_target_pairs={{0,2},{2,0},{4,6},{6,4},{8,10},{10,8},{12,14},{14,12},{16,18},{18,... | collective-permute-start | bytes 2211848 | tf_op jit(solution)/shard_map/ppermute | solution.py:247
  585.6 66.0 %collective-permute-start.64 = (bf16[576,1920]{1,0:T(8,128)(2,1)}, bf16[576,1920]{1,0:T(8,128)(2,1)}, u32[]{:S(2)}, u32[]{:S(2)}) collective-permute-start(bf16[576,1920]{1,0:T(8,128)(2,1)} %convolution_convert_fusion.5), channel_id=1, source_target_pairs={{0,2},{2,0},{4,6},{6,4},{8,10},{10,8},{12,14},{14,12},{16,18},{18,... | collective-permute-start | bytes 6635528 | tf_op jit(solution)/shard_map/ppermute | solution.py:247
  631.0 47.1 %collective-permute-start.66 = (bf16[288,640]{1,0:T(8,128)(2,1)}, bf16[288,640]{1,0:T(8,128)(2,1)}, u32[]{:S(2)}, u32[]{:S(2)}) collective-permute-start(bf16[288,640]{1,0:T(8,128)(2,1)} %slice.728), channel_id=1, source_target_pairs={{0,4},{2,6},{4,0},{6,2},{8,12},{10,14},{12,8},{14,10},{16,20},{18,... | collective-permute-start | bytes 1105928 | tf_op jit(solution)/shard_map/ppermute | solution.py:247
  649.3 54.8 %collective-permute-start.72 = (bf16[576,2304]{1,0:T(8,128)(2,1)}, bf16[576,2304]{1,0:T(8,128)(2,1)}, u32[]{:S(2)}, u32[]{:S(2)}) collective-permute-start(bf16[576,2304]{1,0:T(8,128)(2,1)} %convolution_convert_fusion), channel_id=1, source_target_pairs={{0,2},{2,0},{4,6},{6,4},{8,10},{10,8},{12,14},{14,12},{16,18},{18,... | collective-permute-start | bytes 7962632 | tf_op jit(solution)/shard_map/ppermute | solution.py:247
  665.7 38.5 %collective-permute-start.70 = (bf16[288,1920]{1,0:T(8,128)(2,1)}, bf16[288,1920]{1,0:T(8,128)(2,1)}, u32[]{:S(2)}, u32[]{:S(2)}) collective-permute-start(bf16[288,1920]{1,0:T(8,128)(2,1)} %slice.733), channel_id=1, source_target_pairs={{0,4},{2,6},{4,0},{6,2},{8,12},{10,14},{12,8},{14,10},{16,20},{18,... | collective-permute-start | bytes 3317768 | tf_op jit(solution)/shard_map/ppermute | solution.py:247
  690.0 63.3 %collective-permute-start.74 = (bf16[288,2304]{1,0:T(8,128)(2,1)}, bf16[288,2304]{1,0:T(8,128)(2,1)}, u32[]{:S(2)}, u32[]{:S(2)}) collective-permute-start(bf16[288,2304]{1,0:T(8,128)(2,1)} %slice.738), channel_id=1, source_target_pairs={{0,4},{2,6},{4,0},{6,2},{8,12},{10,14},{12,8},{14,10},{16,20},{18,... | collective-permute-start | bytes 3981320 | tf_op jit(solution)/shard_map/ppermute | solution.py:247
  704.2 36.7 %collective-permute-start.73 = (bf16[256,1152]{1,0:T(8,128)(2,1)S(1)}, bf16[256,1152]{1,0:T(8,128)(2,1)S(1)}, u32[]{:S(2)}, u32[]{:S(2)}) collective-permute-start(bf16[256,1152]{1,0:T(8,128)(2,1)S(1)} %convolution_convert_fusion.8), channel_id=1, source_target_pairs={{0,1},{1,0},{2,3},{3,2},{4,5},{5,4},{6,7},{7,6},{8,9},{9,8},{10,11... | collective-permute-start | bytes 1769480 | tf_op jit(solution)/shard_map/ppermute | solution.py:251
  714.3 39.1 %collective-permute-start.77 = (bf16[576,2560]{1,0:T(8,128)(2,1)}, bf16[576,2560]{1,0:T(8,128)(2,1)}, u32[]{:S(2)}, u32[]{:S(2)}) collective-permute-start(bf16[576,2560]{1,0:T(8,128)(2,1)} %pad_maximum_fusion.4), channel_id=1, source_target_pairs={{0,2},{2,0},{4,6},{6,4},{8,10},{10,8},{12,14},{14,12},{16,18},{18,... | collective-permute-start | bytes 8847368 | tf_op jit(solution)/shard_map/ppermute | solution.py:247
  740.9 47.7 %collective-permute-start.79 = (bf16[288,2304]{1,0:T(8,128)(2,1)}, bf16[288,2304]{1,0:T(8,128)(2,1)}, u32[]{:S(2)}, u32[]{:S(2)}) collective-permute-start(bf16[288,2304]{1,0:T(8,128)(2,1)} %slice.745), channel_id=1, source_target_pairs={{0,4},{2,6},{4,0},{6,2},{8,12},{10,14},{12,8},{14,10},{16,20},{18,... | collective-permute-start | bytes 3981320 | tf_op jit(solution)/shard_map/ppermute | solution.py:247
  767.3 65.5 %collective-permute-start.93 = (bf16[288,2560]{1,0:T(8,128)(2,1)}, bf16[288,2560]{1,0:T(8,128)(2,1)}, u32[]{:S(2)}, u32[]{:S(2)}) collective-permute-start(bf16[288,2560]{1,0:T(8,128)(2,1)} %slice.754), channel_id=1, source_target_pairs={{0,4},{2,6},{4,0},{6,2},{8,12},{10,14},{12,8},{14,10},{16,20},{18,... | collective-permute-start | bytes 4423688 | tf_op jit(solution)/shard_map/ppermute | solution.py:247
  785.7 75.9 %collective-permute-start.85 = (bf16[576,1920]{1,0:T(8,128)(2,1)}, bf16[576,1920]{1,0:T(8,128)(2,1)}, u32[]{:S(2)}, u32[]{:S(2)}) collective-permute-start(bf16[576,1920]{1,0:T(8,128)(2,1)} %convolution_convert_fusion.4), channel_id=1, source_target_pairs={{0,2},{2,0},{4,6},{6,4},{8,10},{10,8},{12,14},{14,12},{16,18},{18,... | collective-permute-start | bytes 6635528 | tf_op jit(solution)/shard_map/ppermute | solution.py:247
  788.6 37.2 %collective-permute-start.89 = (bf16[576,640]{1,0:T(8,128)(2,1)}, bf16[576,640]{1,0:T(8,128)(2,1)}, u32[]{:S(2)}, u32[]{:S(2)}) collective-permute-start(bf16[576,640]{1,0:T(8,128)(2,1)} %convolution_convert_fusion.18), channel_id=1, source_target_pairs={{0,2},{2,0},{4,6},{6,4},{8,10},{10,8},{12,14},{14,12},{16,18},{18,... | collective-permute-start | bytes 2211848 | tf_op jit(solution)/shard_map/ppermute | solution.py:247
  (309 other events, 4277.2 us)

commit v3 on v2

--- a/solution.py
+++ b/solution.py
@@ -281,7 +281,10 @@
     def __init__(self, send, patience):
         self.send = send
         self.patience = patience
+        self.prompt = False
         self.count = 0
+        self.ending = False
+        self.last = None
         self.waiting = []
         self.moving = {}
         self.results = {}
@@ -321,24 +324,37 @@
         if field is not None:
             came = after(came, *[hop[0] for *_, hops in leaving for hop in hops])
         self.depart(leaving)
-        return came if field is not None else None
+        if field is None:
+            return None
+        self.begun = [name for name, *_ in begun]
+        for name, *_ in begun:
+            if self.prompt:
+                steps, blocks, due = self.moving[name]
+                came, *blocks = lax.optimization_barrier((came, *blocks))
+                self.moving[name] = (steps, blocks, due)
+        self.last = came
+        return came
+
+    def hop(self, name, token):
+        steps, blocks, _ = self.moving.pop(name)
+        if token is not None:
+            blocks = [after(block, token) for block in blocks]
+        leaving = self.resume(name, steps, blocks)
+        self.depart(leaving)
+        return leaving[0][2][0][0] if leaving else self.results[name]
 
     def need(self, name):
         while name not in self.results:
-            steps, blocks, _ = self.moving.pop(name)
-            self.depart(self.resume(name, steps, blocks))
+            self.hop(name, self.last)
         return self.results[name]
 
     def finish(self):
-        while self.moving or self.waiting:
-            leaving = []
+        token = self.last
+        for name in list(self.begun):
+            token = self.hop(name, token)
+        while self.moving:
             for name in list(self.moving):
-                steps, blocks, _ = self.moving.pop(name)
-                leaving += self.resume(name, steps, blocks)
-            while self.waiting:
-                name, begin, fields = self.waiting.pop(0)
-                leaving += self.resume(name, begin(*fields), None)
-            self.depart(leaving)
+                self.hop(name, token)
 
 
 def per_device(
@@ -390,7 +406,7 @@
         )
 
     def exchange(field, shift):
-        starts = starts_at.get(line.count + 1, 0) if forward else 1
+        starts = starts_at.get(line.count + 1, 0) if forward else 2 if line.ending else 1
         return line.step(field, lambda f: lay.shift(f, shift), starts)
 
     def spread(field, timed=True):
@@ -556,7 +572,8 @@
         {name: weight(layer, name) for spot, name in place_of if spot == layer}
         for layer in range(LAYERS)
     ]
-    line = Line(lay.send, {1: 1})
+    line = Line(lay.send, {})
+    line.prompt = True
     forward = False
     grad_stream = dot(cotangent[0], order)
     grad_text = jnp.zeros((LANES, width), F32)
@@ -606,6 +623,7 @@
             (layer, "self"),
             product((save["normed"], join(grad_qkv))),
         )
+        line.ending = layer == 0
         grad_normed = collect(each(grad_qkv, kind["qkv"], over_columns))
         grad_shift_one = jnp.sum(grad_normed, axis=0)
         grad_scale_one = jnp.sum(grad_normed * save["unit_one"], axis=0)

time: 921 us -> 890 us (0.966)
  matrix products: 237 us -> 221 us
  local copies, waits for them, and re-layouts: 106 us -> 93.8 us
    ppermute x72, waiting for transfers between devices: 234 us -> 157 us  [send(): lax.ppermute(field, 'dp', [(place, place ^ 1 << bit) for place in range(s...]
    ppermute x27, waiting for transfers between devices: 102 us -> 179 us  [shift(): lax.ppermute(field, 'tensor', [(i, (i + step) % size) for i in range(size)])]
    dot_general x85, matrix products: 223 us -> 209 us  [dot(): lax.dot_general(left, right, (contract, ((), ())), preferred_element_type...]
    ppermute x72, starting transfers between devices: 77.7 us -> 67.4 us  [send(): lax.ppermute(field, 'dp', [(place, place ^ 1 << bit) for place in range(s...]
    unnamed x502 -> x432, local copies, waits for them, and re-layouts: 60.1 us -> 56.4 us
  transfers between devices with their start and end apart: 99 -> 99, of which waited for: 43 -> 56; matrix products, arithmetic and copies ran while one was open for 39% -> 37% of each run, Pallas kernels for 7% -> 8%
where the time goes in v3:
time: 890 us; the launch traced here: 883 us
  waiting for transfers between devices  336 us (38%)
  matrix products  221 us (25%)
  starting transfers between devices  99.3 us (11%)
  local copies, waits for them, and re-layouts  93.8 us (11%)
  Pallas kernels  67.1 us (8%)
  other arithmetic  61.1 us (7%)
    dot_general x85, matrix products, dot(): lax.dot_general(left, right, (contract, ((), ())), preferred_element_type...  209 us
    ppermute x27, waiting for transfers between devices, shift(): lax.ppermute(field, 'tensor', [(i, (i + step) % size) for i in range(size)])  179 us
    ppermute x72, waiting for transfers between devices, send(): lax.ppermute(field, 'dp', [(place, place ^ 1 << bit) for place in range(s...  157 us
    ppermute x72, starting transfers between devices, send(): lax.ppermute(field, 'dp', [(place, place ^ 1 << bit) for place in range(s...  67.4 us
    unnamed x432, local copies, waits for them, and re-layouts  56.4 us
    pallas_call x7, Pallas kernels, attend_back(): pl.pallas_call(lambda *refs: attend_back_kernel(heads, period, limited, k...  42.3 us
    ppermute x27, starting transfers between devices, shift(): lax.ppermute(field, 'tensor', [(i, (i + step) % size) for i in range(size)])  31.9 us
    pallas_call x7, Pallas kernels, attend(): pl.pallas_call(lambda *refs: attend_kernel(heads, period, limited, *refs)...  24.8 us
  transfers between devices with their start and end apart: 99, of which 56 were waited for; matrix products, arithmetic and copies ran while one was open for 37% of the time, Pallas kernels for 8%

profile of v3, /device:TPU:0, one launch (start us, length us, event | category | flops | bytes accessed | tf_op | source)
XLA Modules:
  0.0 882.9 jit_solution(14025461503119407748)
XLA Ops:
  26.4 15.5 %collective-permute-done.1 = bf16[144,2560]{1,0:T(8,128)(2,1)S(1)} collective-permute-done((bf16[144,2560]{1,0:T(8,128)(2,1)S(1)}, bf16[144,2560]{1,0:T(8,128)(2,1)S(1)}, u32[]{:S(2)}, u32[]{:S(2)}) %collective-permute-start.1) | collective-permute-done | bytes 737312 | tf_op jit(solution)/shard_map/ppermute | solution.py:247
  48.5 12.6 %collective-permute-done.3 = bf16[72,2560]{1,0:T(8,128)(2,1)S(1)} collective-permute-done((bf16[72,2560]{1,0:T(8,128)(2,1)S(1)}, bf16[72,2560]{1,0:T(8,128)(2,1)S(1)}, u32[]{:S(2)}, u32[]{:S(2)}) %collective-permute-start.3) | collective-permute-done | bytes 368672 | tf_op jit(solution)/shard_map/ppermute | solution.py:247
  64.8 15.0 %collective-permute-done.4 = bf16[144,2560]{1,0:T(8,128)(2,1)S(1)} collective-permute-done((bf16[144,2560]{1,0:T(8,128)(2,1)}, bf16[144,2560]{1,0:T(8,128)(2,1)S(1)}, u32[]{:S(2)}, u32[]{:S(2)}) %collective-permute-start.4) | collective-permute-done | bytes 737312 | tf_op jit(solution)/shard_map/ppermute | solution.py:247
  150.8 7.7 collective-permute-done.13
  195.9 12.8 %collective-permute-done.20 = bf16[256,1152]{1,0:T(8,128)(2,1)S(1)} collective-permute-done((bf16[256,1152]{1,0:T(8,128)(2,1)S(1)}, bf16[256,1152]{1,0:T(8,128)(2,1)S(1)}, u32[]{:S(2)}, u32[]{:S(2)}) %collective-permute-start.20) | collective-permute-done | bytes 589856 | tf_op jit(solution)/shard_map/ppermute | solution.py:251
  245.6 7.3 collective-permute-done.25
  268.7 10.4 %collective-permute-done.29 = bf16[256,1152]{1,0:T(8,128)(2,1)S(1)} collective-permute-done((bf16[256,1152]{1,0:T(8,128)(2,1)S(1)}, bf16[256,1152]{1,0:T(8,128)(2,1)S(1)}, u32[]{:S(2)}, u32[]{:S(2)}) %collective-permute-start.29) | collective-permute-done | bytes 589856 | tf_op jit(solution)/shard_map/ppermute | solution.py:251
  305.5 9.2 %collective-permute-done.32 = bf16[256,1152]{1,0:T(8,128)(2,1)S(1)} collective-permute-done((bf16[256,1152]{1,0:T(8,128)(2,1)S(1)}, bf16[256,1152]{1,0:T(8,128)(2,1)S(1)}, u32[]{:S(2)}, u32[]{:S(2)}) %collective-permute-start.32) | collective-permute-done | bytes 589856 | tf_op jit(solution)/shard_map/ppermute | solution.py:251
  324.6 11.7 %collective-permute-done.36 = bf16[256,1152]{1,0:T(8,128)(2,1)S(1)} collective-permute-done((bf16[256,1152]{1,0:T(8,128)(2,1)S(1)}, bf16[256,1152]{1,0:T(8,128)(2,1)S(1)}, u32[]{:S(2)}, u32[]{:S(2)}) %collective-permute-start.36) | collective-permute-done | bytes 589856 | tf_op jit(solution)/shard_map/ppermute | solution.py:251
  363.4 7.4 collective-permute-done.39
  375.6 13.8 %collective-permute-done.42 = bf16[256,1152]{1,0:T(8,128)(2,1)S(1)} collective-permute-done((bf16[256,1152]{1,0:T(8,128)(2,1)S(1)}, bf16[256,1152]{1,0:T(8,128)(2,1)S(1)}, u32[]{:S(2)}, u32[]{:S(2)}) %collective-permute-start.42) | collective-permute-done | bytes 589856 | tf_op jit(solution)/shard_map/ppermute | solution.py:251
  393.9 14.5 %collective-permute-done.45 = bf16[256,1152]{1,0:T(8,128)(2,1)S(1)} collective-permute-done((bf16[256,1152]{1,0:T(8,128)(2,1)S(1)}, bf16[256,1152]{1,0:T(8,128)(2,1)S(1)}, u32[]{:S(2)}, u32[]{:S(2)}) %collective-permute-start.45) | collective-permute-done | bytes 589856 | tf_op jit(solution)/shard_map/ppermute | solution.py:251
  449.3 12.2 %collective-permute-done.44 = bf16[256,1152]{1,0:T(8,128)(2,1)S(1)} collective-permute-done((bf16[256,1152]{1,0:T(8,128)(2,1)S(1)}, bf16[256,1152]{1,0:T(8,128)(2,1)S(1)}, u32[]{:S(2)}, u32[]{:S(2)}) %collective-permute-start.44) | collective-permute-done | bytes 589856 | tf_op jit(solution)/shard_map/ppermute | solution.py:251
  515.8 9.4 %collective-permute-done.51 = bf16[256,1152]{1,0:T(8,128)(2,1)S(1)} collective-permute-done((bf16[256,1152]{1,0:T(8,128)(2,1)S(1)}, bf16[256,1152]{1,0:T(8,128)(2,1)S(1)}, u32[]{:S(2)}, u32[]{:S(2)}) %collective-permute-start.51) | collective-permute-done | bytes 589856 | tf_op jit(solution)/shard_map/ppermute | solution.py:251
  530.1 11.8 %collective-permute-done.54 = bf16[288,2304]{1,0:T(8,128)(2,1)S(1)} collective-permute-done((bf16[288,2304]{1,0:T(8,128)(2,1)S(1)}, bf16[288,2304]{1,0:T(8,128)(2,1)S(1)}, u32[]{:S(2)}, u32[]{:S(2)}) %collective-permute-start.54) | collective-permute-done | bytes 1327136 | tf_op jit(solution)/shard_map/ppermute | solution.py:247
  559.3 9.6 %attend_back.9 = bf16[2,256,1920]{2,1,0:T(8,128)(2,1)} custom-call(bf16[2,256,1920]{2,1,0:T(8,128)(2,1)} %bitcast.323, bf16[2,256,1920]{2,1,0:T(8,128)(2,1)} %bitcast.324, bf16[2,256,1920]{2,1,0:T(8,128)(2,1)} %bitcast.325, bf16[2,256,640]{2,1,0:T(8,128)(2,1)} %bitcast.332, f32[2,256,128]{2,1,0:T(8,128)} %get-tuple-element.256.refs_4_), custom_call_target="tpu_custom_call" | custom-call | flops 2684354560 | bytes 3932160 | tf_op jit(solution)/shard_map/attend_back/pallas_call | solution.py:221
  591.9 6.6 collective-permute-done.59
  618.7 7.7 collective-permute-done.63
  647.1 8.0 collective-permute-done.67
  658.6 12.7 %collective-permute-done.70 = bf16[288,1920]{1,0:T(8,128)(2,1)S(1)} collective-permute-done((bf16[288,1920]{1,0:T(8,128)(2,1)S(1)}, bf16[288,1920]{1,0:T(8,128)(2,1)S(1)}, u32[]{:S(2)}, u32[]{:S(2)}) %collective-permute-start.70) | collective-permute-done | bytes 1105952 | tf_op jit(solution)/shard_map/ppermute | solution.py:247
  733.2 8.5 collective-permute-done.76
  803.1 8.3 collective-permute-done.85
  855.0 10.7 %collective-permute-done.95 = bf16[72,640]{1,0:T(8,128)(2,1)S(1)} collective-permute-done((bf16[72,640]{1,0:T(8,128)(2,1)S(1)}, bf16[72,640]{1,0:T(8,128)(2,1)S(1)}, u32[]{:S(2)}, u32[]{:S(2)}) %collective-permute-start.95) | collective-permute-done | bytes 92192 | tf_op jit(solution)/shard_map/ppermute | solution.py:247
  870.1 11.3 %collective-permute-done.92 = bf16[72,1920]{1,0:T(8,128)(2,1)S(1)} collective-permute-done((bf16[72,1920]{1,0:T(8,128)(2,1)S(1)}, bf16[72,1920]{1,0:T(8,128)(2,1)S(1)}, u32[]{:S(2)}, u32[]{:S(2)}) %collective-permute-start.92) | collective-permute-done | bytes 276512 | tf_op jit(solution)/shard_map/ppermute | solution.py:247
  (888 shorter events, 623.4 us)
Async XLA Ops:
  14.0 80.4 %collective-permute-start.6 = (bf16[256,1152]{1,0:T(8,128)(2,1)}, bf16[256,1152]{1,0:T(8,128)(2,1)}, u32[]{:S(2)}, u32[]{:S(2)}) collective-permute-start(bf16[256,1152]{1,0:T(8,128)(2,1)} %add_convert_fusion.26), channel_id=1, source_target_pairs={{0,1},{1,0},{2,3},{3,2},{4,5},{5,4},{6,7},{7,6},{8,9},{9,8},{10,11... | collective-permute-start | bytes 1769480 | tf_op jit(solution)/shard_map/ppermute | solution.py:251
  16.2 122.4 %collective-permute-start.14 = (bf16[128,576]{0,1:T(8,128)(2,1)}, bf16[128,576]{0,1:T(8,128)(2,1)}, u32[]{:S(2)}, u32[]{:S(2)}) collective-permute-start(bf16[128,576]{0,1:T(8,128)(2,1)} %pad.61), channel_id=1, source_target_pairs={{0,1},{1,0},{2,3},{3,2},{4,5},{5,4},{6,7},{7,6},{8,9},{9,8},{10,11... | collective-permute-start | bytes 442376 | tf_op jit(solution)/shard_map/ppermute | solution.py:251
  46.2 33.7 %collective-permute-start.2 = (bf16[288,2560]{1,0:T(8,128)(2,1)}, bf16[288,2560]{1,0:T(8,128)(2,1)}, u32[]{:S(2)}, u32[]{:S(2)}) collective-permute-start(bf16[288,2560]{1,0:T(8,128)(2,1)} %pad_maximum_fusion.22), channel_id=1, source_target_pairs={{0,4},{2,6},{4,0},{6,2},{8,12},{10,14},{12,8},{14,10},{16,20},{18,... | collective-permute-start | bytes 4423688 | tf_op jit(solution)/shard_map/ppermute | solution.py:247
  92.7 34.1 %collective-permute-start.9 = (bf16[288,2560]{1,0:T(8,128)(2,1)}, bf16[288,2560]{1,0:T(8,128)(2,1)}, u32[]{:S(2)}, u32[]{:S(2)}) collective-permute-start(bf16[288,2560]{1,0:T(8,128)(2,1)} %pad_maximum_fusion.23), channel_id=1, source_target_pairs={{0,4},{2,6},{4,0},{6,2},{8,12},{10,14},{12,8},{14,10},{16,20},{18,... | collective-permute-start | bytes 4423688 | tf_op jit(solution)/shard_map/ppermute | solution.py:247
  148.0 41.2 %collective-permute-start.17 = (bf16[288,2304]{1,0:T(8,128)(2,1)}, bf16[288,2304]{1,0:T(8,128)(2,1)}, u32[]{:S(2)}, u32[]{:S(2)}) collective-permute-start(bf16[288,2304]{1,0:T(8,128)(2,1)} %get-tuple-element.427), channel_id=1, source_target_pairs={{0,4},{2,6},{4,0},{6,2},{8,12},{10,14},{12,8},{14,10},{16,20},{18,... | collective-permute-start | bytes 3981320 | tf_op jit(solution)/shard_map/ppermute | solution.py:247
  176.2 32.5 %collective-permute-start.21 = (bf16[288,2304]{1,0:T(8,128)(2,1)}, bf16[288,2304]{1,0:T(8,128)(2,1)}, u32[]{:S(2)}, u32[]{:S(2)}) collective-permute-start(bf16[288,2304]{1,0:T(8,128)(2,1)} %get-tuple-element.424), channel_id=1, source_target_pairs={{0,4},{2,6},{4,0},{6,2},{8,12},{10,14},{12,8},{14,10},{16,20},{18,... | collective-permute-start | bytes 3981320 | tf_op jit(solution)/shard_map/ppermute | solution.py:247
  243.8 35.3 %collective-permute-start.26 = (bf16[288,2560]{1,0:T(8,128)(2,1)S(1)}, bf16[288,2560]{1,0:T(8,128)(2,1)S(1)}, u32[]{:S(2)}, u32[]{:S(2)}) collective-permute-start(bf16[288,2560]{1,0:T(8,128)(2,1)S(1)} %get-tuple-element.413), channel_id=1, source_target_pairs={{0,4},{2,6},{4,0},{6,2},{8,12},{10,14},{12,8},{14,10},{16,20},{18,... | collective-permute-start | bytes 4423688 | tf_op jit(solution)/shard_map/ppermute | solution.py:247
  282.1 35.9 %collective-permute-start.33 = (bf16[288,2560]{1,0:T(8,128)(2,1)}, bf16[288,2560]{1,0:T(8,128)(2,1)}, u32[]{:S(2)}, u32[]{:S(2)}) collective-permute-start(bf16[288,2560]{1,0:T(8,128)(2,1)} %get-tuple-element.411), channel_id=1, source_target_pairs={{0,4},{2,6},{4,0},{6,2},{8,12},{10,14},{12,8},{14,10},{16,20},{18,... | collective-permute-start | bytes 4423688 | tf_op jit(solution)/shard_map/ppermute | solution.py:247
  320.0 31.9 %collective-permute-start.37 = (bf16[288,2304]{1,0:T(8,128)(2,1)}, bf16[288,2304]{1,0:T(8,128)(2,1)}, u32[]{:S(2)}, u32[]{:S(2)}) collective-permute-start(bf16[288,2304]{1,0:T(8,128)(2,1)} %get-tuple-element.418), channel_id=1, source_target_pairs={{0,4},{2,6},{4,0},{6,2},{8,12},{10,14},{12,8},{14,10},{16,20},{18,... | collective-permute-start | bytes 3981320 | tf_op jit(solution)/shard_map/ppermute | solution.py:247
  357.2 32.2 %collective-permute-start.41 = (bf16[288,2304]{1,0:T(8,128)(2,1)}, bf16[288,2304]{1,0:T(8,128)(2,1)}, u32[]{:S(2)}, u32[]{:S(2)}) collective-permute-start(bf16[288,2304]{1,0:T(8,128)(2,1)} %get-tuple-element.415), channel_id=1, source_target_pairs={{0,4},{2,6},{4,0},{6,2},{8,12},{10,14},{12,8},{14,10},{16,20},{18,... | collective-permute-start | bytes 3981320 | tf_op jit(solution)/shard_map/ppermute | solution.py:247
  430.8 30.7 %collective-permute-start.47 = (bf16[576,2304]{1,0:T(8,128)(2,1)S(1)}, bf16[576,2304]{1,0:T(8,128)(2,1)S(1)}, u32[]{:S(2)}, u32[]{:S(2)}) collective-permute-start(bf16[576,2304]{1,0:T(8,128)(2,1)S(1)} %convolution_convert_fusion.3), channel_id=1, source_target_pairs={{0,2},{2,0},{4,6},{6,4},{8,10},{10,8},{12,14},{14,12},{16,18},{18,... | collective-permute-start | bytes 7962632 | tf_op jit(solution)/shard_map/ppermute | solution.py:247
  443.0 41.7 %collective-permute-start.49 = (bf16[576,2304]{1,0:T(8,128)(2,1)}, bf16[576,2304]{1,0:T(8,128)(2,1)}, u32[]{:S(2)}, u32[]{:S(2)}) collective-permute-start(bf16[576,2304]{1,0:T(8,128)(2,1)} %convolution_convert_fusion.2), channel_id=1, source_target_pairs={{0,2},{2,0},{4,6},{6,4},{8,10},{10,8},{12,14},{14,12},{16,18},{18,... | collective-permute-start | bytes 7962632 | tf_op jit(solution)/shard_map/ppermute | solution.py:247
  473.7 33.2 %collective-permute-start.50 = (bf16[288,2304]{1,0:T(8,128)(2,1)}, bf16[288,2304]{1,0:T(8,128)(2,1)}, u32[]{:S(2)}, u32[]{:S(2)}) collective-permute-start(bf16[288,2304]{1,0:T(8,128)(2,1)} %slice.703), channel_id=1, source_target_pairs={{0,4},{2,6},{4,0},{6,2},{8,12},{10,14},{12,8},{14,10},{16,20},{18,... | collective-permute-start | bytes 3981320 | tf_op jit(solution)/shard_map/ppermute | solution.py:247
  511.6 30.3 %collective-permute-start.54 = (bf16[288,2304]{1,0:T(8,128)(2,1)S(1)}, bf16[288,2304]{1,0:T(8,128)(2,1)S(1)}, u32[]{:S(2)}, u32[]{:S(2)}) collective-permute-start(bf16[288,2304]{1,0:T(8,128)(2,1)S(1)} %slice.708), channel_id=1, source_target_pairs={{0,4},{2,6},{4,0},{6,2},{8,12},{10,14},{12,8},{14,10},{16,20},{18,... | collective-permute-start | bytes 3981320 | tf_op jit(solution)/shard_map/ppermute | solution.py:247
  547.7 32.4 %collective-permute-start.58 = (bf16[288,2560]{1,0:T(8,128)(2,1)}, bf16[288,2560]{1,0:T(8,128)(2,1)}, u32[]{:S(2)}, u32[]{:S(2)}) collective-permute-start(bf16[288,2560]{1,0:T(8,128)(2,1)} %slice.719), channel_id=1, source_target_pairs={{0,4},{2,6},{4,0},{6,2},{8,12},{10,14},{12,8},{14,10},{16,20},{18,... | collective-permute-start | bytes 4423688 | tf_op jit(solution)/shard_map/ppermute | solution.py:247
  558.4 40.1 %collective-permute-start.60 = (bf16[576,640]{1,0:T(8,128)(2,1)}, bf16[576,640]{1,0:T(8,128)(2,1)}, u32[]{:S(2)}, u32[]{:S(2)}) collective-permute-start(bf16[576,640]{1,0:T(8,128)(2,1)} %convolution_convert_fusion.21), channel_id=1, source_target_pairs={{0,2},{2,0},{4,6},{6,4},{8,10},{10,8},{12,14},{14,12},{16,18},{18,... | collective-permute-start | bytes 2211848 | tf_op jit(solution)/shard_map/ppermute | solution.py:247
  575.6 50.9 %collective-permute-start.64 = (bf16[576,1920]{1,0:T(8,128)(2,1)}, bf16[576,1920]{1,0:T(8,128)(2,1)}, u32[]{:S(2)}, u32[]{:S(2)}) collective-permute-start(bf16[576,1920]{1,0:T(8,128)(2,1)} %convolution_convert_fusion.5), channel_id=1, source_target_pairs={{0,2},{2,0},{4,6},{6,4},{8,10},{10,8},{12,14},{14,12},{16,18},{18,... | collective-permute-start | bytes 6635528 | tf_op jit(solution)/shard_map/ppermute | solution.py:247
  644.4 45.8 %collective-permute-start.72 = (bf16[576,2304]{1,0:T(8,128)(2,1)}, bf16[576,2304]{1,0:T(8,128)(2,1)}, u32[]{:S(2)}, u32[]{:S(2)}) collective-permute-start(bf16[576,2304]{1,0:T(8,128)(2,1)} %convolution_convert_fusion), channel_id=1, source_target_pairs={{0,2},{2,0},{4,6},{6,4},{8,10},{10,8},{12,14},{14,12},{16,18},{18,... | collective-permute-start | bytes 7962632 | tf_op jit(solution)/shard_map/ppermute | solution.py:247
  677.1 43.5 %collective-permute-start.75 = (bf16[288,2304]{1,0:T(8,128)(2,1)}, bf16[288,2304]{1,0:T(8,128)(2,1)}, u32[]{:S(2)}, u32[]{:S(2)}) collective-permute-start(bf16[288,2304]{1,0:T(8,128)(2,1)} %slice.742), channel_id=1, source_target_pairs={{0,4},{2,6},{4,0},{6,2},{8,12},{10,14},{12,8},{14,10},{16,20},{18,... | collective-permute-start | bytes 3981320 | tf_op jit(solution)/shard_map/ppermute | solution.py:247
  677.4 43.2 %collective-permute-start.74 = (bf16[144,1920]{1,0:T(8,128)(2,1)}, bf16[144,1920]{1,0:T(8,128)(2,1)}, u32[]{:S(2)}, u32[]{:S(2)}) collective-permute-start(bf16[144,1920]{1,0:T(8,128)(2,1)} %slice.741), channel_id=1, source_target_pairs={{0,8},{2,10},{4,12},{6,14},{8,0},{10,2},{12,4},{14,6},{16,24},{18,... | collective-permute-start | bytes 1658888 | tf_op jit(solution)/shard_map/ppermute | solution.py:247
  677.8 42.6 %collective-permute-start.73 = (bf16[72,640]{1,0:T(8,128)(2,1)S(1)}, bf16[72,640]{1,0:T(8,128)(2,1)S(1)}, u32[]{:S(2)}, u32[]{:S(2)}) collective-permute-start(bf16[72,640]{1,0:T(8,128)(2,1)S(1)} %get-tuple-element.491), channel_id=1, source_target_pairs={{0,16},{2,18},{4,20},{6,22},{8,24},{10,26},{12,28},{14,30},{16,0},... | collective-permute-start | bytes 276488 | tf_op jit(solution)/shard_map/ppermute | solution.py:247
  706.9 34.8 %collective-permute-start.77 = (bf16[576,2560]{1,0:T(8,128)(2,1)S(1)}, bf16[576,2560]{1,0:T(8,128)(2,1)S(1)}, u32[]{:S(2)}, u32[]{:S(2)}) collective-permute-start(bf16[576,2560]{1,0:T(8,128)(2,1)S(1)} %pad_maximum_fusion.4), channel_id=1, source_target_pairs={{0,2},{2,0},{4,6},{6,4},{8,10},{10,8},{12,14},{14,12},{16,18},{18,... | collective-permute-start | bytes 8847368 | tf_op jit(solution)/shard_map/ppermute | solution.py:247
  763.4 31.9 %collective-permute-start.84 = (bf16[288,2560]{1,0:T(8,128)(2,1)}, bf16[288,2560]{1,0:T(8,128)(2,1)}, u32[]{:S(2)}, u32[]{:S(2)}) collective-permute-start(bf16[288,2560]{1,0:T(8,128)(2,1)} %slice.758), channel_id=1, source_target_pairs={{0,4},{2,6},{4,0},{6,2},{8,12},{10,14},{12,8},{14,10},{16,20},{18,... | collective-permute-start | bytes 4423688 | tf_op jit(solution)/shard_map/ppermute | solution.py:247
  764.7 30.0 %collective-permute-start.83 = (bf16[144,2304]{1,0:T(8,128)(2,1)}, bf16[144,2304]{1,0:T(8,128)(2,1)}, u32[]{:S(2)}, u32[]{:S(2)}) collective-permute-start(bf16[144,2304]{1,0:T(8,128)(2,1)} %slice.757), channel_id=1, source_target_pairs={{0,8},{2,10},{4,12},{6,14},{8,0},{10,2},{12,4},{14,6},{16,24},{18,... | collective-permute-start | bytes 1990664 | tf_op jit(solution)/shard_map/ppermute | solution.py:247
  (274 other events, 3941.9 us)

commit v4 on v3

--- a/solution.py
+++ b/solution.py
@@ -321,8 +321,6 @@
             leaving += self.resume(name, steps, [flat.pop(0) for _ in blocks])
         for name, begin, fields in begun:
             leaving += self.resume(name, begin(*[flat.pop(0) for _ in fields]), None)
-        if field is not None:
-            came = after(came, *[hop[0] for *_, hops in leaving for hop in hops])
         self.depart(leaving)
         if field is None:
             return None
@@ -468,7 +466,7 @@
         for name, part in zip(names, parts):
             place_of[layer, name] = (index, start, start + part.shape[1])
             start += part.shape[1]
-    starts_at = {6: 1, 8: 1, 9: 1, 10: 1, 12: 1}
+    starts_at = {6: 1, 7: 1, 9: 1, 10: 1, 12: 1}
 
     def weight(layer, name):
         index, start, stop = place_of[layer, name]

time: 890 us -> 854 us (0.960)
  other arithmetic: 61.1 us -> 83.8 us
  matrix products: 221 us -> 200 us
  local copies, waits for them, and re-layouts: 93.8 us -> 73.6 us
  waiting for transfers between devices: 336 us -> 324 us
    ppermute x27, waiting for transfers between devices: 179 us -> 144 us  [shift(): lax.ppermute(field, 'tensor', [(i, (i + step) % size) for i in range(size)])]
    concatenate x9 -> x24, other arithmetic: 14.4 us -> 38.3 us  [gathering(): rows = jnp.concatenate([rows] + (yield [(rows, bit)]), axis=0)]
    ppermute x72, waiting for transfers between devices: 157 us -> 180 us  [send(): lax.ppermute(field, 'dp', [(place, place ^ 1 << bit) for place in range(s...]
    dot_general x85, matrix products: 209 us -> 188 us  [dot(): lax.dot_general(left, right, (contract, ((), ())), preferred_element_type...]
    unnamed x432 -> x459, local copies, waits for them, and re-layouts: 56.4 us -> 39.1 us
  transfers between devices with their start and end apart: 99 -> 99, of which waited for: 56 -> 50; matrix products, arithmetic and copies ran while one was open for 37% -> 39% of each run, Pallas kernels for 8% -> 8%
where the time goes in v4:
time: 854 us; the launch traced here: 847 us
  waiting for transfers between devices  324 us (38%)
  matrix products  200 us (23%)
  starting transfers between devices  93.6 us (11%)
  other arithmetic  83.8 us (10%)
  local copies, waits for them, and re-layouts  73.6 us (9%)
  Pallas kernels  67.1 us (8%)
    dot_general x85, matrix products, dot(): lax.dot_general(left, right, (contract, ((), ())), preferred_element_type...  188 us
    ppermute x72, waiting for transfers between devices, send(): lax.ppermute(field, 'dp', [(place, place ^ 1 << bit) for place in range(s...  180 us
    ppermute x27, waiting for transfers between devices, shift(): lax.ppermute(field, 'tensor', [(i, (i + step) % size) for i in range(size)])  144 us
    ppermute x72, starting transfers between devices, send(): lax.ppermute(field, 'dp', [(place, place ^ 1 << bit) for place in range(s...  67.8 us
    pallas_call x7, Pallas kernels, attend_back(): pl.pallas_call(lambda *refs: attend_back_kernel(heads, period, limited, k...  42.3 us
    unnamed x459, local copies, waits for them, and re-layouts  39.1 us
    concatenate x24, other arithmetic, gathering(): rows = jnp.concatenate([rows] + (yield [(rows, bit)]), axis=0)  38.3 us
    ppermute x27, starting transfers between devices, shift(): lax.ppermute(field, 'tensor', [(i, (i + step) % size) for i in range(size)])  25.8 us
  transfers between devices with their start and end apart: 99, of which 50 were waited for; matrix products, arithmetic and copies ran while one was open for 39% of the time, Pallas kernels for 8%

profile of v4, /device:TPU:0, one launch (start us, length us, event | category | flops | bytes accessed | tf_op | source)
XLA Modules:
  0.0 846.8 jit_solution(3368657686530091202)
XLA Ops:
  25.8 16.1 %collective-permute-done.1 = bf16[144,2560]{1,0:T(8,128)(2,1)S(1)} collective-permute-done((bf16[144,2560]{1,0:T(8,128)(2,1)S(1)}, bf16[144,2560]{1,0:T(8,128)(2,1)S(1)}, u32[]{:S(2)}, u32[]{:S(2)}) %collective-permute-start.1) | collective-permute-done | bytes 737312 | tf_op jit(solution)/shard_map/ppermute | solution.py:247
  49.2 11.9 %collective-permute-done.3 = bf16[72,2560]{1,0:T(8,128)(2,1)S(1)} collective-permute-done((bf16[72,2560]{1,0:T(8,128)(2,1)S(1)}, bf16[72,2560]{1,0:T(8,128)(2,1)S(1)}, u32[]{:S(2)}, u32[]{:S(2)}) %collective-permute-start.3) | collective-permute-done | bytes 368672 | tf_op jit(solution)/shard_map/ppermute | solution.py:247
  66.0 14.0 %collective-permute-done.4 = bf16[144,2560]{1,0:T(8,128)(2,1)} collective-permute-done((bf16[144,2560]{1,0:T(8,128)(2,1)}, bf16[144,2560]{1,0:T(8,128)(2,1)}, u32[]{:S(2)}, u32[]{:S(2)}) %collective-permute-start.4) | collective-permute-done | bytes 737312 | tf_op jit(solution)/shard_map/ppermute | solution.py:247
  151.6 8.3 collective-permute-done.13
  199.8 9.4 %collective-permute-done.22 = bf16[288,2304]{1,0:T(8,128)(2,1)} collective-permute-done((bf16[288,2304]{1,0:T(8,128)(2,1)}, bf16[288,2304]{1,0:T(8,128)(2,1)}, u32[]{:S(2)}, u32[]{:S(2)}) %collective-permute-start.22) | collective-permute-done | bytes 1327136 | tf_op jit(solution)/shard_map/ppermute | solution.py:247
  226.9 6.9 collective-permute-done.24
  240.8 7.9 collective-permute-done.25
  252.2 9.3 %collective-permute-done.28 = bf16[72,2304]{1,0:T(8,128)(2,1)S(1)} collective-permute-done((bf16[72,2304]{1,0:T(8,128)(2,1)S(1)}, bf16[72,2304]{1,0:T(8,128)(2,1)S(1)}, u32[]{:S(2)}, u32[]{:S(2)}) %collective-permute-start.28) | collective-permute-done | bytes 331808 | tf_op jit(solution)/shard_map/ppermute | solution.py:247
  273.2 12.6 %collective-permute-done.30 = bf16[256,1152]{1,0:T(8,128)(2,1)S(1)} collective-permute-done((bf16[256,1152]{1,0:T(8,128)(2,1)S(1)}, bf16[256,1152]{1,0:T(8,128)(2,1)S(1)}, u32[]{:S(2)}, u32[]{:S(2)}) %collective-permute-start.30) | collective-permute-done | bytes 589856 | tf_op jit(solution)/shard_map/ppermute | solution.py:251
  301.3 12.6 %collective-permute-done.32 = bf16[256,1152]{1,0:T(8,128)(2,1)S(1)} collective-permute-done((bf16[256,1152]{1,0:T(8,128)(2,1)S(1)}, bf16[256,1152]{1,0:T(8,128)(2,1)S(1)}, u32[]{:S(2)}, u32[]{:S(2)}) %collective-permute-start.32) | collective-permute-done | bytes 589856 | tf_op jit(solution)/shard_map/ppermute | solution.py:251
  325.8 10.9 %collective-permute-done.36 = bf16[256,1152]{1,0:T(8,128)(2,1)S(1)} collective-permute-done((bf16[256,1152]{1,0:T(8,128)(2,1)S(1)}, bf16[256,1152]{1,0:T(8,128)(2,1)S(1)}, u32[]{:S(2)}, u32[]{:S(2)}) %collective-permute-start.36) | collective-permute-done | bytes 589856 | tf_op jit(solution)/shard_map/ppermute | solution.py:251
  364.7 6.1 collective-permute-done.39
  378.5 11.0 %collective-permute-done.41 = bf16[288,2304]{1,0:T(8,128)(2,1)} collective-permute-done((bf16[288,2304]{1,0:T(8,128)(2,1)}, bf16[288,2304]{1,0:T(8,128)(2,1)}, u32[]{:S(2)}, u32[]{:S(2)}) %collective-permute-start.41) | collective-permute-done | bytes 1327136 | tf_op jit(solution)/shard_map/ppermute | solution.py:247
  420.9 8.6 %collective-permute-done.46 = bf16[256,1152]{1,0:T(8,128)(2,1)S(1)} collective-permute-done((bf16[256,1152]{1,0:T(8,128)(2,1)S(1)}, bf16[256,1152]{1,0:T(8,128)(2,1)S(1)}, u32[]{:S(2)}, u32[]{:S(2)}) %collective-permute-start.46) | collective-permute-done | bytes 589856 | tf_op jit(solution)/shard_map/ppermute | solution.py:251
  431.6 9.6 %collective-permute-done.44 = bf16[256,1152]{1,0:T(8,128)(2,1)S(1)} collective-permute-done((bf16[256,1152]{1,0:T(8,128)(2,1)S(1)}, bf16[256,1152]{1,0:T(8,128)(2,1)S(1)}, u32[]{:S(2)}, u32[]{:S(2)}) %collective-permute-start.44) | collective-permute-done | bytes 589856 | tf_op jit(solution)/shard_map/ppermute | solution.py:251
  490.0 10.1 %collective-permute-done.51 = bf16[256,1152]{1,0:T(8,128)(2,1)S(1)} collective-permute-done((bf16[256,1152]{1,0:T(8,128)(2,1)S(1)}, bf16[256,1152]{1,0:T(8,128)(2,1)S(1)}, u32[]{:S(2)}, u32[]{:S(2)}) %collective-permute-start.51) | collective-permute-done | bytes 589856 | tf_op jit(solution)/shard_map/ppermute | solution.py:251
  504.5 10.8 %collective-permute-done.54 = bf16[288,2304]{1,0:T(8,128)(2,1)S(1)} collective-permute-done((bf16[288,2304]{1,0:T(8,128)(2,1)S(1)}, bf16[288,2304]{1,0:T(8,128)(2,1)S(1)}, u32[]{:S(2)}, u32[]{:S(2)}) %collective-permute-start.54) | collective-permute-done | bytes 1327136 | tf_op jit(solution)/shard_map/ppermute | solution.py:247
  532.6 9.6 %attend_back.9 = bf16[2,256,1920]{2,1,0:T(8,128)(2,1)} custom-call(bf16[2,256,1920]{2,1,0:T(8,128)(2,1)} %bitcast.323, bf16[2,256,1920]{2,1,0:T(8,128)(2,1)} %bitcast.324, bf16[2,256,1920]{2,1,0:T(8,128)(2,1)} %bitcast.325, bf16[2,256,640]{2,1,0:T(8,128)(2,1)} %bitcast.336, f32[2,256,128]{2,1,0:T(8,128)} %get-tuple-element.220.refs_4_), custom_call_target="tpu_custom_call" | custom-call | flops 2684354560 | bytes 3932160 | tf_op jit(solution)/shard_map/attend_back/pallas_call | solution.py:221
  621.7 16.6 %collective-permute-done.70 = bf16[288,1920]{1,0:T(8,128)(2,1)S(1)} collective-permute-done((bf16[288,1920]{1,0:T(8,128)(2,1)S(1)}, bf16[288,1920]{1,0:T(8,128)(2,1)S(1)}, u32[]{:S(2)}, u32[]{:S(2)}) %collective-permute-start.70) | collective-permute-done | bytes 1105952 | tf_op jit(solution)/shard_map/ppermute | solution.py:247
  700.0 9.1 %collective-permute-done.76 = bf16[256,1152]{1,0:T(8,128)(2,1)S(1)} collective-permute-done((bf16[256,1152]{1,0:T(8,128)(2,1)S(1)}, bf16[256,1152]{1,0:T(8,128)(2,1)S(1)}, u32[]{:S(2)}, u32[]{:S(2)}) %collective-permute-start.76) | collective-permute-done | bytes 589856 | tf_op jit(solution)/shard_map/ppermute | solution.py:251
  766.8 8.2 collective-permute-done.85
  801.6 5.9 collective-permute-done.97
  819.5 10.3 %collective-permute-done.95 = bf16[72,640]{1,0:T(8,128)(2,1)S(1)} collective-permute-done((bf16[72,640]{1,0:T(8,128)(2,1)S(1)}, bf16[72,640]{1,0:T(8,128)(2,1)S(1)}, u32[]{:S(2)}, u32[]{:S(2)}) %collective-permute-start.95) | collective-permute-done | bytes 92192 | tf_op jit(solution)/shard_map/ppermute | solution.py:247
  834.2 11.0 %collective-permute-done.92 = bf16[72,1920]{1,0:T(8,128)(2,1)S(1)} collective-permute-done((bf16[72,1920]{1,0:T(8,128)(2,1)S(1)}, bf16[72,1920]{1,0:T(8,128)(2,1)S(1)}, u32[]{:S(2)}, u32[]{:S(2)}) %collective-permute-start.92) | collective-permute-done | bytes 276512 | tf_op jit(solution)/shard_map/ppermute | solution.py:247
  (929 shorter events, 594.9 us)
Async XLA Ops:
  14.0 83.1 %collective-permute-start.6 = (bf16[256,1152]{1,0:T(8,128)(2,1)}, bf16[256,1152]{1,0:T(8,128)(2,1)}, u32[]{:S(2)}, u32[]{:S(2)}) collective-permute-start(bf16[256,1152]{1,0:T(8,128)(2,1)} %add_convert_fusion.26), channel_id=1, source_target_pairs={{0,1},{1,0},{2,3},{3,2},{4,5},{5,4},{6,7},{7,6},{8,9},{9,8},{10,11... | collective-permute-start | bytes 1769480 | tf_op jit(solution)/shard_map/ppermute | solution.py:251
  16.2 120.6 %collective-permute-start.14 = (bf16[128,576]{0,1:T(8,128)(2,1)}, bf16[128,576]{0,1:T(8,128)(2,1)}, u32[]{:S(2)}, u32[]{:S(2)}) collective-permute-start(bf16[128,576]{0,1:T(8,128)(2,1)} %pad.65), channel_id=1, source_target_pairs={{0,1},{1,0},{2,3},{3,2},{4,5},{5,4},{6,7},{7,6},{8,9},{9,8},{10,11... | collective-permute-start | bytes 442376 | tf_op jit(solution)/shard_map/ppermute | solution.py:251
  46.2 33.7 %collective-permute-start.2 = (bf16[288,2560]{1,0:T(8,128)(2,1)}, bf16[288,2560]{1,0:T(8,128)(2,1)}, u32[]{:S(2)}, u32[]{:S(2)}) collective-permute-start(bf16[288,2560]{1,0:T(8,128)(2,1)} %pad_maximum_fusion.25), channel_id=1, source_target_pairs={{0,4},{2,6},{4,0},{6,2},{8,12},{10,14},{12,8},{14,10},{16,20},{18,... | collective-permute-start | bytes 4423688 | tf_op jit(solution)/shard_map/ppermute | solution.py:247
  93.7 34.7 %collective-permute-start.9 = (bf16[288,2560]{1,0:T(8,128)(2,1)}, bf16[288,2560]{1,0:T(8,128)(2,1)}, u32[]{:S(2)}, u32[]{:S(2)}) collective-permute-start(bf16[288,2560]{1,0:T(8,128)(2,1)} %pad_maximum_fusion.26), channel_id=1, source_target_pairs={{0,4},{2,6},{4,0},{6,2},{8,12},{10,14},{12,8},{14,10},{16,20},{18,... | collective-permute-start | bytes 4423688 | tf_op jit(solution)/shard_map/ppermute | solution.py:247
  149.5 41.5 %collective-permute-start.18 = (bf16[288,2304]{1,0:T(8,128)(2,1)}, bf16[288,2304]{1,0:T(8,128)(2,1)}, u32[]{:S(2)}, u32[]{:S(2)}) collective-permute-start(bf16[288,2304]{1,0:T(8,128)(2,1)} %pad_maximum_fusion.29), channel_id=1, source_target_pairs={{0,4},{2,6},{4,0},{6,2},{8,12},{10,14},{12,8},{14,10},{16,20},{18,... | collective-permute-start | bytes 3981320 | tf_op jit(solution)/shard_map/ppermute | solution.py:247
  172.7 36.6 %collective-permute-start.22 = (bf16[288,2304]{1,0:T(8,128)(2,1)}, bf16[288,2304]{1,0:T(8,128)(2,1)}, u32[]{:S(2)}, u32[]{:S(2)}) collective-permute-start(bf16[288,2304]{1,0:T(8,128)(2,1)} %pad_maximum_fusion.30), channel_id=1, source_target_pairs={{0,4},{2,6},{4,0},{6,2},{8,12},{10,14},{12,8},{14,10},{16,20},{18,... | collective-permute-start | bytes 3981320 | tf_op jit(solution)/shard_map/ppermute | solution.py:247
  216.1 36.1 %collective-permute-start.26 = (bf16[288,2560]{1,0:T(8,128)(2,1)S(1)}, bf16[288,2560]{1,0:T(8,128)(2,1)S(1)}, u32[]{:S(2)}, u32[]{:S(2)}) collective-permute-start(bf16[288,2560]{1,0:T(8,128)(2,1)S(1)} %pad_maximum_fusion.27), channel_id=1, source_target_pairs={{0,4},{2,6},{4,0},{6,2},{8,12},{10,14},{12,8},{14,10},{16,20},{18,... | collective-permute-start | bytes 4423688 | tf_op jit(solution)/shard_map/ppermute | solution.py:247
  272.2 44.9 %collective-permute-start.33 = (bf16[288,2560]{1,0:T(8,128)(2,1)}, bf16[288,2560]{1,0:T(8,128)(2,1)}, u32[]{:S(2)}, u32[]{:S(2)}) collective-permute-start(bf16[288,2560]{1,0:T(8,128)(2,1)} %pad_maximum_fusion.28), channel_id=1, source_target_pairs={{0,4},{2,6},{4,0},{6,2},{8,12},{10,14},{12,8},{14,10},{16,20},{18,... | collective-permute-start | bytes 4423688 | tf_op jit(solution)/shard_map/ppermute | solution.py:247
  321.0 31.1 %collective-permute-start.37 = (bf16[288,2304]{1,0:T(8,128)(2,1)}, bf16[288,2304]{1,0:T(8,128)(2,1)}, u32[]{:S(2)}, u32[]{:S(2)}) collective-permute-start(bf16[288,2304]{1,0:T(8,128)(2,1)} %pad_maximum_fusion.31), channel_id=1, source_target_pairs={{0,4},{2,6},{4,0},{6,2},{8,12},{10,14},{12,8},{14,10},{16,20},{18,... | collective-permute-start | bytes 3981320 | tf_op jit(solution)/shard_map/ppermute | solution.py:247
  357.9 31.6 %collective-permute-start.41 = (bf16[288,2304]{1,0:T(8,128)(2,1)}, bf16[288,2304]{1,0:T(8,128)(2,1)}, u32[]{:S(2)}, u32[]{:S(2)}) collective-permute-start(bf16[288,2304]{1,0:T(8,128)(2,1)} %pad_maximum_fusion.32), channel_id=1, source_target_pairs={{0,4},{2,6},{4,0},{6,2},{8,12},{10,14},{12,8},{14,10},{16,20},{18,... | collective-permute-start | bytes 3981320 | tf_op jit(solution)/shard_map/ppermute | solution.py:247
  417.9 39.3 %collective-permute-start.49 = (bf16[576,2304]{1,0:T(8,128)(2,1)}, bf16[576,2304]{1,0:T(8,128)(2,1)}, u32[]{:S(2)}, u32[]{:S(2)}) collective-permute-start(bf16[576,2304]{1,0:T(8,128)(2,1)} %convolution_convert_fusion.2), channel_id=1, source_target_pairs={{0,2},{2,0},{4,6},{6,4},{8,10},{10,8},{12,14},{14,12},{16,18},{18,... | collective-permute-start | bytes 7962632 | tf_op jit(solution)/shard_map/ppermute | solution.py:247
  448.3 32.8 %collective-permute-start.50 = (bf16[288,2304]{1,0:T(8,128)(2,1)}, bf16[288,2304]{1,0:T(8,128)(2,1)}, u32[]{:S(2)}, u32[]{:S(2)}) collective-permute-start(bf16[288,2304]{1,0:T(8,128)(2,1)} %slice.705), channel_id=1, source_target_pairs={{0,4},{2,6},{4,0},{6,2},{8,12},{10,14},{12,8},{14,10},{16,20},{18,... | collective-permute-start | bytes 3981320 | tf_op jit(solution)/shard_map/ppermute | solution.py:247
  518.1 33.5 %collective-permute-start.58 = (bf16[288,2560]{1,0:T(8,128)(2,1)}, bf16[288,2560]{1,0:T(8,128)(2,1)}, u32[]{:S(2)}, u32[]{:S(2)}) collective-permute-start(bf16[288,2560]{1,0:T(8,128)(2,1)} %slice.721), channel_id=1, source_target_pairs={{0,4},{2,6},{4,0},{6,2},{8,12},{10,14},{12,8},{14,10},{16,20},{18,... | collective-permute-start | bytes 4423688 | tf_op jit(solution)/shard_map/ppermute | solution.py:247
  520.3 31.4 %collective-permute-start.57 = (bf16[144,2304]{1,0:T(8,128)(2,1)}, bf16[144,2304]{1,0:T(8,128)(2,1)}, u32[]{:S(2)}, u32[]{:S(2)}) collective-permute-start(bf16[144,2304]{1,0:T(8,128)(2,1)} %slice.719), channel_id=1, source_target_pairs={{0,8},{2,10},{4,12},{6,14},{8,0},{10,2},{12,4},{14,6},{16,24},{18,... | collective-permute-start | bytes 1990664 | tf_op jit(solution)/shard_map/ppermute | solution.py:247
  531.0 31.0 %collective-permute-start.60 = (bf16[576,640]{1,0:T(8,128)(2,1)}, bf16[576,640]{1,0:T(8,128)(2,1)}, u32[]{:S(2)}, u32[]{:S(2)}) collective-permute-start(bf16[576,640]{1,0:T(8,128)(2,1)} %convolution_convert_fusion.21), channel_id=1, source_target_pairs={{0,2},{2,0},{4,6},{6,4},{8,10},{10,8},{12,14},{14,12},{16,18},{18,... | collective-permute-start | bytes 2211848 | tf_op jit(solution)/shard_map/ppermute | solution.py:247
  547.0 43.5 %collective-permute-start.64 = (bf16[576,1920]{1,0:T(8,128)(2,1)}, bf16[576,1920]{1,0:T(8,128)(2,1)}, u32[]{:S(2)}, u32[]{:S(2)}) collective-permute-start(bf16[576,1920]{1,0:T(8,128)(2,1)} %convolution_convert_fusion.5), channel_id=1, source_target_pairs={{0,2},{2,0},{4,6},{6,4},{8,10},{10,8},{12,14},{14,12},{16,18},{18,... | collective-permute-start | bytes 6635528 | tf_op jit(solution)/shard_map/ppermute | solution.py:247
  608.3 48.1 %collective-permute-start.72 = (bf16[576,2304]{1,0:T(8,128)(2,1)}, bf16[576,2304]{1,0:T(8,128)(2,1)}, u32[]{:S(2)}, u32[]{:S(2)}) collective-permute-start(bf16[576,2304]{1,0:T(8,128)(2,1)} %convolution_convert_fusion), channel_id=1, source_target_pairs={{0,2},{2,0},{4,6},{6,4},{8,10},{10,8},{12,14},{14,12},{16,18},{18,... | collective-permute-start | bytes 7962632 | tf_op jit(solution)/shard_map/ppermute | solution.py:247
  642.4 45.5 %collective-permute-start.75 = (bf16[288,2304]{1,0:T(8,128)(2,1)}, bf16[288,2304]{1,0:T(8,128)(2,1)}, u32[]{:S(2)}, u32[]{:S(2)}) collective-permute-start(bf16[288,2304]{1,0:T(8,128)(2,1)} %slice.744), channel_id=1, source_target_pairs={{0,4},{2,6},{4,0},{6,2},{8,12},{10,14},{12,8},{14,10},{16,20},{18,... | collective-permute-start | bytes 3981320 | tf_op jit(solution)/shard_map/ppermute | solution.py:247
  644.5 43.4 %collective-permute-start.74 = (bf16[144,1920]{1,0:T(8,128)(2,1)}, bf16[144,1920]{1,0:T(8,128)(2,1)}, u32[]{:S(2)}, u32[]{:S(2)}) collective-permute-start(bf16[144,1920]{1,0:T(8,128)(2,1)} %slice.743), channel_id=1, source_target_pairs={{0,8},{2,10},{4,12},{6,14},{8,0},{10,2},{12,4},{14,6},{16,24},{18,... | collective-permute-start | bytes 1658888 | tf_op jit(solution)/shard_map/ppermute | solution.py:247
  644.6 43.3 %collective-permute-start.73 = (bf16[72,640]{1,0:T(8,128)(2,1)S(1)}, bf16[72,640]{1,0:T(8,128)(2,1)S(1)}, u32[]{:S(2)}, u32[]{:S(2)}) collective-permute-start(bf16[72,640]{1,0:T(8,128)(2,1)S(1)} %get-tuple-element.388), channel_id=1, source_target_pairs={{0,16},{2,18},{4,20},{6,22},{8,24},{10,26},{12,28},{14,30},{16,0},... | collective-permute-start | bytes 276488 | tf_op jit(solution)/shard_map/ppermute | solution.py:247
  673.0 36.1 %collective-permute-start.77 = (bf16[576,2560]{1,0:T(8,128)(2,1)S(1)}, bf16[576,2560]{1,0:T(8,128)(2,1)S(1)}, u32[]{:S(2)}, u32[]{:S(2)}) collective-permute-start(bf16[576,2560]{1,0:T(8,128)(2,1)S(1)} %pad_maximum_fusion.5), channel_id=1, source_target_pairs={{0,2},{2,0},{4,6},{6,4},{8,10},{10,8},{12,14},{14,12},{16,18},{18,... | collective-permute-start | bytes 8847368 | tf_op jit(solution)/shard_map/ppermute | solution.py:247
  723.3 34.6 %collective-permute-start.84 = (bf16[288,2560]{1,0:T(8,128)(2,1)}, bf16[288,2560]{1,0:T(8,128)(2,1)}, u32[]{:S(2)}, u32[]{:S(2)}) collective-permute-start(bf16[288,2560]{1,0:T(8,128)(2,1)} %slice.758), channel_id=1, source_target_pairs={{0,4},{2,6},{4,0},{6,2},{8,12},{10,14},{12,8},{14,10},{16,20},{18,... | collective-permute-start | bytes 4423688 | tf_op jit(solution)/shard_map/ppermute | solution.py:247
  725.3 32.6 %collective-permute-start.83 = (bf16[144,2304]{1,0:T(8,128)(2,1)}, bf16[144,2304]{1,0:T(8,128)(2,1)}, u32[]{:S(2)}, u32[]{:S(2)}) collective-permute-start(bf16[144,2304]{1,0:T(8,128)(2,1)} %slice.757), channel_id=1, source_target_pairs={{0,8},{2,10},{4,12},{6,14},{8,0},{10,2},{12,4},{14,6},{16,24},{18,... | collective-permute-start | bytes 1990664 | tf_op jit(solution)/shard_map/ppermute | solution.py:247
  726.3 31.7 %collective-permute-start.82 = (bf16[72,2304]{1,0:T(8,128)(2,1)}, bf16[72,2304]{1,0:T(8,128)(2,1)}, u32[]{:S(2)}, u32[]{:S(2)}) collective-permute-start(bf16[72,2304]{1,0:T(8,128)(2,1)} %slice.755), channel_id=1, source_target_pairs={{0,16},{2,18},{4,20},{6,22},{8,24},{10,26},{12,28},{14,30},{16,0},... | collective-permute-start | bytes 995336 | tf_op jit(solution)/shard_map/ppermute | solution.py:247
  (287 other events, 4120.1 us)

commit v5 on v4

--- a/solution.py
+++ b/solution.py
@@ -466,7 +466,7 @@
         for name, part in zip(names, parts):
             place_of[layer, name] = (index, start, start + part.shape[1])
             start += part.shape[1]
-    starts_at = {6: 1, 7: 1, 9: 1, 10: 1, 12: 1}
+    starts_at = {6: 1, 7: 1, 9: 1, 11: 1, 12: 1}
 
     def weight(layer, name):
         index, start, stop = place_of[layer, name]

time: 854 us -> 863 us (1.011)
  matrix products: 200 us -> 213 us
    dot_general x85, matrix products: 188 us -> 202 us  [dot(): lax.dot_general(left, right, (contract, ((), ())), preferred_element_type...]
  transfers between devices with their start and end apart: 99 -> 99, of which waited for: 50 -> 47; matrix products, arithmetic and copies ran while one was open for 39% -> 39% of each run, Pallas kernels for 8% -> 8%
where the time goes in v5:
time: 863 us; the launch traced here: 855 us
  waiting for transfers between devices  325 us (38%)
  matrix products  213 us (25%)
  starting transfers between devices  92.1 us (11%)
  other arithmetic  80.5 us (9%)
  local copies, waits for them, and re-layouts  71.7 us (8%)
  Pallas kernels  67.1 us (8%)
    dot_general x85, matrix products, dot(): lax.dot_general(left, right, (contract, ((), ())), preferred_element_type...  202 us
    ppermute x72, waiting for transfers between devices, send(): lax.ppermute(field, 'dp', [(place, place ^ 1 << bit) for place in range(s...  187 us
    ppermute x27, waiting for transfers between devices, shift(): lax.ppermute(field, 'tensor', [(i, (i + step) % size) for i in range(size)])  138 us
    ppermute x72, starting transfers between devices, send(): lax.ppermute(field, 'dp', [(place, place ^ 1 << bit) for place in range(s...  65 us
    pallas_call x7, Pallas kernels, attend_back(): pl.pallas_call(lambda *refs: attend_back_kernel(heads, period, limited, k...  42.3 us
    unnamed x459, local copies, waits for them, and re-layouts  38.7 us
    concatenate x24, other arithmetic, gathering(): rows = jnp.concatenate([rows] + (yield [(rows, bit)]), axis=0)  35 us
    ppermute x27, starting transfers between devices, shift(): lax.ppermute(field, 'tensor', [(i, (i + step) % size) for i in range(size)])  27.1 us
  transfers between devices with their start and end apart: 99, of which 47 were waited for; matrix products, arithmetic and copies ran while one was open for 39% of the time, Pallas kernels for 8%

profile of v5, /device:TPU:0, one launch (start us, length us, event | category | flops | bytes accessed | tf_op | source)
XLA Modules:
  0.0 855.4 jit_solution(17085594300185100991)
XLA Ops:
  25.8 16.1 %collective-permute-done.1 = bf16[144,2560]{1,0:T(8,128)(2,1)S(1)} collective-permute-done((bf16[144,2560]{1,0:T(8,128)(2,1)S(1)}, bf16[144,2560]{1,0:T(8,128)(2,1)S(1)}, u32[]{:S(2)}, u32[]{:S(2)}) %collective-permute-start.1) | collective-permute-done | bytes 737312 | tf_op jit(solution)/shard_map/ppermute | solution.py:247
  49.3 11.9 %collective-permute-done.3 = bf16[72,2560]{1,0:T(8,128)(2,1)S(1)} collective-permute-done((bf16[72,2560]{1,0:T(8,128)(2,1)S(1)}, bf16[72,2560]{1,0:T(8,128)(2,1)S(1)}, u32[]{:S(2)}, u32[]{:S(2)}) %collective-permute-start.3) | collective-permute-done | bytes 368672 | tf_op jit(solution)/shard_map/ppermute | solution.py:247
  66.0 14.0 %collective-permute-done.4 = bf16[144,2560]{1,0:T(8,128)(2,1)} collective-permute-done((bf16[144,2560]{1,0:T(8,128)(2,1)}, bf16[144,2560]{1,0:T(8,128)(2,1)}, u32[]{:S(2)}, u32[]{:S(2)}) %collective-permute-start.4) | collective-permute-done | bytes 737312 | tf_op jit(solution)/shard_map/ppermute | solution.py:247
  151.7 6.3 collective-permute-done.13
  197.3 12.2 %collective-permute-done.22 = bf16[288,2304]{1,0:T(8,128)(2,1)} collective-permute-done((bf16[288,2304]{1,0:T(8,128)(2,1)}, bf16[288,2304]{1,0:T(8,128)(2,1)}, u32[]{:S(2)}, u32[]{:S(2)}) %collective-permute-start.22) | collective-permute-done | bytes 1327136 | tf_op jit(solution)/shard_map/ppermute | solution.py:247
  225.8 8.2 collective-permute-done.24
  239.0 9.9 %collective-permute-done.25 = bf16[256,1152]{1,0:T(8,128)(2,1)S(1)} collective-permute-done((bf16[256,1152]{1,0:T(8,128)(2,1)S(1)}, bf16[256,1152]{1,0:T(8,128)(2,1)S(1)}, u32[]{:S(2)}, u32[]{:S(2)}) %collective-permute-start.25) | collective-permute-done | bytes 589856 | tf_op jit(solution)/shard_map/ppermute | solution.py:251
  264.7 12.9 %collective-permute-done.29 = bf16[256,1152]{1,0:T(8,128)(2,1)S(1)} collective-permute-done((bf16[256,1152]{1,0:T(8,128)(2,1)S(1)}, bf16[256,1152]{1,0:T(8,128)(2,1)S(1)}, u32[]{:S(2)}, u32[]{:S(2)}) %collective-permute-start.29) | collective-permute-done | bytes 589856 | tf_op jit(solution)/shard_map/ppermute | solution.py:251
  293.8 12.3 %collective-permute-done.31 = bf16[256,1152]{1,0:T(8,128)(2,1)S(1)} collective-permute-done((bf16[256,1152]{1,0:T(8,128)(2,1)S(1)}, bf16[256,1152]{1,0:T(8,128)(2,1)S(1)}, u32[]{:S(2)}, u32[]{:S(2)}) %collective-permute-start.31) | collective-permute-done | bytes 589856 | tf_op jit(solution)/shard_map/ppermute | solution.py:251
  326.2 21.8 %collective-permute-done.36 = bf16[256,1152]{1,0:T(8,128)(2,1)S(1)} collective-permute-done((bf16[256,1152]{1,0:T(8,128)(2,1)S(1)}, bf16[256,1152]{1,0:T(8,128)(2,1)S(1)}, u32[]{:S(2)}, u32[]{:S(2)}) %collective-permute-start.36) | collective-permute-done | bytes 589856 | tf_op jit(solution)/shard_map/ppermute | solution.py:251
  381.6 11.0 %collective-permute-done.41 = bf16[256,1152]{1,0:T(8,128)(2,1)S(1)} collective-permute-done((bf16[256,1152]{1,0:T(8,128)(2,1)S(1)}, bf16[256,1152]{1,0:T(8,128)(2,1)S(1)}, u32[]{:S(2)}, u32[]{:S(2)}) %collective-permute-start.41) | collective-permute-done | bytes 589856 | tf_op jit(solution)/shard_map/ppermute | solution.py:251
  424.8 8.5 collective-permute-done.46
  435.4 10.0 %collective-permute-done.44 = bf16[256,1152]{1,0:T(8,128)(2,1)S(1)} collective-permute-done((bf16[256,1152]{1,0:T(8,128)(2,1)S(1)}, bf16[256,1152]{1,0:T(8,128)(2,1)S(1)}, u32[]{:S(2)}, u32[]{:S(2)}) %collective-permute-start.44) | collective-permute-done | bytes 589856 | tf_op jit(solution)/shard_map/ppermute | solution.py:251
  502.2 8.0 collective-permute-done.53
  510.2 10.8 %collective-permute-done.54 = bf16[288,2304]{1,0:T(8,128)(2,1)S(1)} collective-permute-done((bf16[288,2304]{1,0:T(8,128)(2,1)S(1)}, bf16[288,2304]{1,0:T(8,128)(2,1)S(1)}, u32[]{:S(2)}, u32[]{:S(2)}) %collective-permute-start.54) | collective-permute-done | bytes 1327136 | tf_op jit(solution)/shard_map/ppermute | solution.py:247
  538.0 9.6 %attend_back.9 = bf16[2,256,1920]{2,1,0:T(8,128)(2,1)} custom-call(bf16[2,256,1920]{2,1,0:T(8,128)(2,1)} %bitcast.323, bf16[2,256,1920]{2,1,0:T(8,128)(2,1)} %bitcast.324, bf16[2,256,1920]{2,1,0:T(8,128)(2,1)} %bitcast.325, bf16[2,256,640]{2,1,0:T(8,128)(2,1)} %bitcast.334, f32[2,256,128]{2,1,0:T(8,128)} %get-tuple-element.220.refs_4_), custom_call_target="tpu_custom_call" | custom-call | flops 2684354560 | bytes 3932160 | tf_op jit(solution)/shard_map/attend_back/pallas_call | solution.py:221
  580.8 8.2 collective-permute-done.62
  630.4 12.7 %collective-permute-done.70 = bf16[288,1920]{1,0:T(8,128)(2,1)S(1)} collective-permute-done((bf16[288,1920]{1,0:T(8,128)(2,1)S(1)}, bf16[288,1920]{1,0:T(8,128)(2,1)S(1)}, u32[]{:S(2)}, u32[]{:S(2)}) %collective-permute-start.70) | collective-permute-done | bytes 1105952 | tf_op jit(solution)/shard_map/ppermute | solution.py:247
  683.0 6.3 collective-permute-done.88
  710.6 10.8 %collective-permute-done.79 = bf16[144,2304]{1,0:T(8,128)(2,1)S(1)} collective-permute-done((bf16[144,2304]{1,0:T(8,128)(2,1)S(1)}, bf16[144,2304]{1,0:T(8,128)(2,1)S(1)}, u32[]{:S(2)}, u32[]{:S(2)}) %collective-permute-start.79) | collective-permute-done | bytes 663584 | tf_op jit(solution)/shard_map/ppermute | solution.py:247
  721.4 7.2 collective-permute-done.80
  808.7 7.5 collective-permute-done.97
  829.6 8.6 %collective-permute-done.95 = bf16[72,640]{1,0:T(8,128)(2,1)S(1)} collective-permute-done((bf16[72,640]{1,0:T(8,128)(2,1)S(1)}, bf16[72,640]{1,0:T(8,128)(2,1)S(1)}, u32[]{:S(2)}, u32[]{:S(2)}) %collective-permute-start.95) | collective-permute-done | bytes 92192 | tf_op jit(solution)/shard_map/ppermute | solution.py:247
  842.6 11.3 %collective-permute-done.92 = bf16[72,1920]{1,0:T(8,128)(2,1)S(1)} collective-permute-done((bf16[72,1920]{1,0:T(8,128)(2,1)S(1)}, bf16[72,1920]{1,0:T(8,128)(2,1)S(1)}, u32[]{:S(2)}, u32[]{:S(2)}) %collective-permute-start.92) | collective-permute-done | bytes 276512 | tf_op jit(solution)/shard_map/ppermute | solution.py:247
  (928 shorter events, 594.2 us)
Async XLA Ops:
  14.1 83.2 %collective-permute-start.6 = (bf16[256,1152]{1,0:T(8,128)(2,1)}, bf16[256,1152]{1,0:T(8,128)(2,1)}, u32[]{:S(2)}, u32[]{:S(2)}) collective-permute-start(bf16[256,1152]{1,0:T(8,128)(2,1)} %add_convert_fusion.26), channel_id=1, source_target_pairs={{0,1},{1,0},{2,3},{3,2},{4,5},{5,4},{6,7},{7,6},{8,9},{9,8},{10,11... | collective-permute-start | bytes 1769480 | tf_op jit(solution)/shard_map/ppermute | solution.py:251
  16.3 120.7 %collective-permute-start.14 = (bf16[128,576]{0,1:T(8,128)(2,1)}, bf16[128,576]{0,1:T(8,128)(2,1)}, u32[]{:S(2)}, u32[]{:S(2)}) collective-permute-start(bf16[128,576]{0,1:T(8,128)(2,1)} %pad.65), channel_id=1, source_target_pairs={{0,1},{1,0},{2,3},{3,2},{4,5},{5,4},{6,7},{7,6},{8,9},{9,8},{10,11... | collective-permute-start | bytes 442376 | tf_op jit(solution)/shard_map/ppermute | solution.py:251
  46.3 33.7 %collective-permute-start.2 = (bf16[288,2560]{1,0:T(8,128)(2,1)}, bf16[288,2560]{1,0:T(8,128)(2,1)}, u32[]{:S(2)}, u32[]{:S(2)}) collective-permute-start(bf16[288,2560]{1,0:T(8,128)(2,1)} %pad_maximum_fusion.25), channel_id=1, source_target_pairs={{0,4},{2,6},{4,0},{6,2},{8,12},{10,14},{12,8},{14,10},{16,20},{18,... | collective-permute-start | bytes 4423688 | tf_op jit(solution)/shard_map/ppermute | solution.py:247
  93.9 34.7 %collective-permute-start.9 = (bf16[288,2560]{1,0:T(8,128)(2,1)}, bf16[288,2560]{1,0:T(8,128)(2,1)}, u32[]{:S(2)}, u32[]{:S(2)}) collective-permute-start(bf16[288,2560]{1,0:T(8,128)(2,1)} %pad_maximum_fusion.26), channel_id=1, source_target_pairs={{0,4},{2,6},{4,0},{6,2},{8,12},{10,14},{12,8},{14,10},{16,20},{18,... | collective-permute-start | bytes 4423688 | tf_op jit(solution)/shard_map/ppermute | solution.py:247
  149.7 38.5 %collective-permute-start.18 = (bf16[288,2304]{1,0:T(8,128)(2,1)}, bf16[288,2304]{1,0:T(8,128)(2,1)}, u32[]{:S(2)}, u32[]{:S(2)}) collective-permute-start(bf16[288,2304]{1,0:T(8,128)(2,1)} %pad_maximum_fusion.29), channel_id=1, source_target_pairs={{0,4},{2,6},{4,0},{6,2},{8,12},{10,14},{12,8},{14,10},{16,20},{18,... | collective-permute-start | bytes 3981320 | tf_op jit(solution)/shard_map/ppermute | solution.py:247
  215.9 36.4 %collective-permute-start.26 = (bf16[288,2560]{1,0:T(8,128)(2,1)S(1)}, bf16[288,2560]{1,0:T(8,128)(2,1)S(1)}, u32[]{:S(2)}, u32[]{:S(2)}) collective-permute-start(bf16[288,2560]{1,0:T(8,128)(2,1)S(1)} %pad_maximum_fusion.27), channel_id=1, source_target_pairs={{0,4},{2,6},{4,0},{6,2},{8,12},{10,14},{12,8},{14,10},{16,20},{18,... | collective-permute-start | bytes 4423688 | tf_op jit(solution)/shard_map/ppermute | solution.py:247
  264.1 45.2 %collective-permute-start.32 = (bf16[288,2560]{1,0:T(8,128)(2,1)}, bf16[288,2560]{1,0:T(8,128)(2,1)}, u32[]{:S(2)}, u32[]{:S(2)}) collective-permute-start(bf16[288,2560]{1,0:T(8,128)(2,1)} %pad_maximum_fusion.28), channel_id=1, source_target_pairs={{0,4},{2,6},{4,0},{6,2},{8,12},{10,14},{12,8},{14,10},{16,20},{18,... | collective-permute-start | bytes 4423688 | tf_op jit(solution)/shard_map/ppermute | solution.py:247
  316.8 31.1 %collective-permute-start.35 = (bf16[576,2560]{1,0:T(8,128)(2,1)S(1)}, bf16[576,2560]{1,0:T(8,128)(2,1)S(1)}, u32[]{:S(2)}, u32[]{:S(2)}) collective-permute-start(bf16[576,2560]{1,0:T(8,128)(2,1)S(1)} %pad_maximum_fusion.3), channel_id=1, source_target_pairs={{0,2},{2,0},{4,6},{6,4},{8,10},{10,8},{12,14},{14,12},{16,18},{18,... | collective-permute-start | bytes 8847368 | tf_op jit(solution)/shard_map/ppermute | solution.py:247
  319.4 86.2 %collective-permute-start.45 = (bf16[256,1152]{1,0:T(8,128)(2,1)}, bf16[256,1152]{1,0:T(8,128)(2,1)}, u32[]{:S(2)}, u32[]{:S(2)}) collective-permute-start(bf16[256,1152]{1,0:T(8,128)(2,1)} %get-tuple-element.414), channel_id=1, source_target_pairs={{0,1},{1,0},{2,3},{3,2},{4,5},{5,4},{6,7},{7,6},{8,9},{9,8},{10,11... | collective-permute-start | bytes 1769480 | tf_op jit(solution)/shard_map/ppermute | solution.py:251
  322.5 36.4 %collective-permute-start.37 = (bf16[144,2304]{1,0:T(8,128)(2,1)}, bf16[144,2304]{1,0:T(8,128)(2,1)S(1)}, u32[]{:S(2)}, u32[]{:S(2)}) collective-permute-start(bf16[144,2304]{1,0:T(8,128)(2,1)} %pad_maximum_fusion.48), channel_id=1, source_target_pairs={{0,8},{2,10},{4,12},{6,14},{8,0},{10,2},{12,4},{14,6},{16,24},{18,... | collective-permute-start | bytes 1990664 | tf_op jit(solution)/shard_map/ppermute | solution.py:247
  324.2 54.1 %collective-permute-start.39 = (bf16[288,2304]{1,0:T(8,128)(2,1)}, bf16[288,2304]{1,0:T(8,128)(2,1)}, u32[]{:S(2)}, u32[]{:S(2)}) collective-permute-start(bf16[288,2304]{1,0:T(8,128)(2,1)} %pad_maximum_fusion.31), channel_id=1, source_target_pairs={{0,4},{2,6},{4,0},{6,2},{8,12},{10,14},{12,8},{14,10},{16,20},{18,... | collective-permute-start | bytes 3981320 | tf_op jit(solution)/shard_map/ppermute | solution.py:247
  422.4 40.3 %collective-permute-start.49 = (bf16[576,2304]{1,0:T(8,128)(2,1)}, bf16[576,2304]{1,0:T(8,128)(2,1)}, u32[]{:S(2)}, u32[]{:S(2)}) collective-permute-start(bf16[576,2304]{1,0:T(8,128)(2,1)} %convolution_convert_fusion.2), channel_id=1, source_target_pairs={{0,2},{2,0},{4,6},{6,4},{8,10},{10,8},{12,14},{14,12},{16,18},{18,... | collective-permute-start | bytes 7962632 | tf_op jit(solution)/shard_map/ppermute | solution.py:247
  454.2 31.5 %collective-permute-start.50 = (bf16[288,2304]{1,0:T(8,128)(2,1)}, bf16[288,2304]{1,0:T(8,128)(2,1)}, u32[]{:S(2)}, u32[]{:S(2)}) collective-permute-start(bf16[288,2304]{1,0:T(8,128)(2,1)} %slice.705), channel_id=1, source_target_pairs={{0,4},{2,6},{4,0},{6,2},{8,12},{10,14},{12,8},{14,10},{16,20},{18,... | collective-permute-start | bytes 3981320 | tf_op jit(solution)/shard_map/ppermute | solution.py:247
  522.6 34.3 %collective-permute-start.56 = (bf16[72,2304]{1,0:T(8,128)(2,1)}, bf16[72,2304]{1,0:T(8,128)(2,1)}, u32[]{:S(2)}, u32[]{:S(2)}) collective-permute-start(bf16[72,2304]{1,0:T(8,128)(2,1)} %slice.717), channel_id=1, source_target_pairs={{0,16},{2,18},{4,20},{6,22},{8,24},{10,26},{12,28},{14,30},{16,0},... | collective-permute-start | bytes 995336 | tf_op jit(solution)/shard_map/ppermute | solution.py:247
  525.2 31.8 %collective-permute-start.57 = (bf16[144,2304]{1,0:T(8,128)(2,1)}, bf16[144,2304]{1,0:T(8,128)(2,1)}, u32[]{:S(2)}, u32[]{:S(2)}) collective-permute-start(bf16[144,2304]{1,0:T(8,128)(2,1)} %slice.719), channel_id=1, source_target_pairs={{0,8},{2,10},{4,12},{6,14},{8,0},{10,2},{12,4},{14,6},{16,24},{18,... | collective-permute-start | bytes 1990664 | tf_op jit(solution)/shard_map/ppermute | solution.py:247
  528.0 32.0 %collective-permute-start.58 = (bf16[288,2560]{1,0:T(8,128)(2,1)}, bf16[288,2560]{1,0:T(8,128)(2,1)}, u32[]{:S(2)}, u32[]{:S(2)}) collective-permute-start(bf16[288,2560]{1,0:T(8,128)(2,1)} %slice.721), channel_id=1, source_target_pairs={{0,4},{2,6},{4,0},{6,2},{8,12},{10,14},{12,8},{14,10},{16,20},{18,... | collective-permute-start | bytes 4423688 | tf_op jit(solution)/shard_map/ppermute | solution.py:247
  536.4 34.9 %collective-permute-start.60 = (bf16[576,640]{1,0:T(8,128)(2,1)}, bf16[576,640]{1,0:T(8,128)(2,1)}, u32[]{:S(2)}, u32[]{:S(2)}) collective-permute-start(bf16[576,640]{1,0:T(8,128)(2,1)} %convolution_convert_fusion.21), channel_id=1, source_target_pairs={{0,2},{2,0},{4,6},{6,4},{8,10},{10,8},{12,14},{14,12},{16,18},{18,... | collective-permute-start | bytes 2211848 | tf_op jit(solution)/shard_map/ppermute | solution.py:247
  552.5 49.6 %collective-permute-start.64 = (bf16[576,1920]{1,0:T(8,128)(2,1)}, bf16[576,1920]{1,0:T(8,128)(2,1)}, u32[]{:S(2)}, u32[]{:S(2)}) collective-permute-start(bf16[576,1920]{1,0:T(8,128)(2,1)} %convolution_convert_fusion.5), channel_id=1, source_target_pairs={{0,2},{2,0},{4,6},{6,4},{8,10},{10,8},{12,14},{14,12},{16,18},{18,... | collective-permute-start | bytes 6635528 | tf_op jit(solution)/shard_map/ppermute | solution.py:247
  620.4 39.7 %collective-permute-start.72 = (bf16[576,2304]{1,0:T(8,128)(2,1)}, bf16[576,2304]{1,0:T(8,128)(2,1)}, u32[]{:S(2)}, u32[]{:S(2)}) collective-permute-start(bf16[576,2304]{1,0:T(8,128)(2,1)} %convolution_convert_fusion), channel_id=1, source_target_pairs={{0,2},{2,0},{4,6},{6,4},{8,10},{10,8},{12,14},{14,12},{16,18},{18,... | collective-permute-start | bytes 7962632 | tf_op jit(solution)/shard_map/ppermute | solution.py:247
  643.6 47.7 %collective-permute-start.73 = (bf16[72,640]{1,0:T(8,128)(2,1)S(1)}, bf16[72,640]{1,0:T(8,128)(2,1)S(1)}, u32[]{:S(2)}, u32[]{:S(2)}) collective-permute-start(bf16[72,640]{1,0:T(8,128)(2,1)S(1)} %get-tuple-element.388), channel_id=1, source_target_pairs={{0,16},{2,18},{4,20},{6,22},{8,24},{10,26},{12,28},{14,30},{16,0},... | collective-permute-start | bytes 276488 | tf_op jit(solution)/shard_map/ppermute | solution.py:247
  647.6 43.7 %collective-permute-start.74 = (bf16[144,1920]{1,0:T(8,128)(2,1)}, bf16[144,1920]{1,0:T(8,128)(2,1)}, u32[]{:S(2)}, u32[]{:S(2)}) collective-permute-start(bf16[144,1920]{1,0:T(8,128)(2,1)} %slice.743), channel_id=1, source_target_pairs={{0,8},{2,10},{4,12},{6,14},{8,0},{10,2},{12,4},{14,6},{16,24},{18,... | collective-permute-start | bytes 1658888 | tf_op jit(solution)/shard_map/ppermute | solution.py:247
  651.0 40.4 %collective-permute-start.75 = (bf16[288,2304]{1,0:T(8,128)(2,1)}, bf16[288,2304]{1,0:T(8,128)(2,1)}, u32[]{:S(2)}, u32[]{:S(2)}) collective-permute-start(bf16[288,2304]{1,0:T(8,128)(2,1)} %slice.744), channel_id=1, source_target_pairs={{0,4},{2,6},{4,0},{6,2},{8,12},{10,14},{12,8},{14,10},{16,20},{18,... | collective-permute-start | bytes 3981320 | tf_op jit(solution)/shard_map/ppermute | solution.py:247
  729.9 35.4 %collective-permute-start.82 = (bf16[72,2304]{1,0:T(8,128)(2,1)}, bf16[72,2304]{1,0:T(8,128)(2,1)}, u32[]{:S(2)}, u32[]{:S(2)}) collective-permute-start(bf16[72,2304]{1,0:T(8,128)(2,1)} %slice.755), channel_id=1, source_target_pairs={{0,16},{2,18},{4,20},{6,22},{8,24},{10,26},{12,28},{14,30},{16,0},... | collective-permute-start | bytes 995336 | tf_op jit(solution)/shard_map/ppermute | solution.py:247
  733.7 31.6 %collective-permute-start.84 = (bf16[288,2560]{1,0:T(8,128)(2,1)}, bf16[288,2560]{1,0:T(8,128)(2,1)}, u32[]{:S(2)}, u32[]{:S(2)}) collective-permute-start(bf16[288,2560]{1,0:T(8,128)(2,1)} %slice.758), channel_id=1, source_target_pairs={{0,4},{2,6},{4,0},{6,2},{8,12},{10,14},{12,8},{14,10},{16,20},{18,... | collective-permute-start | bytes 4423688 | tf_op jit(solution)/shard_map/ppermute | solution.py:247
  (287 other events, 4189.8 us)
